TPU v7x, 32 devices: a whole 2x2x4 slice. The times are simulated.
32 devices in a mesh: row: 4 (over z), col: 4 (over y, core), rep: 2 (over x).
Axes of the slice: x: 2, y: 2, z: 4, core: 2. Of those that a mesh axis runs over, the one named last changes fastest.
Arguments:
- queries: bfloat16 [16384, 768], P(('rep', 'row', 'col')), parts along dimension 0, may hold values from -16 to 16
- passages: bfloat16 [12288, 768], P(('rep', 'row', 'col')), parts along dimension 0, may hold values from -16 to 16
- positive: int32 [16384], P(('rep', 'row', 'col')), parts along dimension 0, may hold values from 0 to 383
- block_mask: int32 [16384, 9], P(('rep', 'row', 'col')), parts along dimension 0, may hold values from 0 to 1
- roster: int32 [16384, 3], P(('rep', 'row', 'col')), parts along dimension 0, may hold values from 0 to 2
Outputs:
- loss: float32 [2], P('rep'), parts along dimension 0
- grad_queries: float32 [16384, 768], P(('rep', 'row', 'col')), parts along dimension 0
- grad_passages: float32 [12288, 768], P(('rep', 'row', 'col')), parts along dimension 0
There are 2 independent parts, one for each index of `rep`. A program takes and returns all parts, laid end to end along the dimension named above; each array names one. Nothing has to cross between parts.
All inputs are finite; a program needn't handle non-finite values.
Results may differ from a plain program's by a relative error of at most 0.002.
Values may be sent and summed in bfloat16 or wider, within the bound.
No kernel may reach another device: no remote copies, remote signals or barrier semaphores. Data moves between devices by JAX's collectives and lax.ppermute only.
A program may use at most 128 MiB of HBM per device.

v0:
```python
import jax
import jax.numpy as jnp
from jax import lax
from jax.sharding import PartitionSpec as P

BLK = 128


LOWEST = -1e30


def from_behind(block, axis, distance):
    devices = range(lax.axis_size(axis))
    route = [((i - distance) % len(devices), i) for i in devices]
    return lax.ppermute(block, axis, route)


def block_scores(query_rows, block_rows):
    scale = query_rows.shape[1] ** (-0.5)
    return (
        lax.dot_general(
            query_rows, block_rows, (((1,), (1,)), ((), ())), preferred_element_type=jnp.float32
        )
        * scale
    )


def forward_block(running, query_rows, block_rows, visible, target):
    highest, summed, positive_score = running
    scores = block_scores(query_rows, block_rows)
    masked = jnp.where(visible[:, None], scores, LOWEST)
    raised = jnp.maximum(highest, jnp.max(masked, axis=1))
    summed = summed * jnp.exp(highest - raised) + jnp.sum(
        jnp.where(visible[:, None], jnp.exp(scores - raised[:, None]), 0.0), axis=1
    )
    if target is not None:
        positive_score = positive_score + jnp.sum(jnp.where(target, scores, 0.0), axis=1)
    return (raised, summed, positive_score)


def backward_block(query_rows, block_rows, visible, target, log_total):
    scale = query_rows.shape[1] ** (-0.5)
    scores = block_scores(query_rows, block_rows)
    weights = jnp.where(visible[:, None], jnp.exp(scores - log_total[:, None]), 0.0)
    if target is not None:
        weights = weights - target.astype(jnp.float32)
    weights = weights.astype(jnp.bfloat16)
    toward = jnp.dot(weights, block_rows, preferred_element_type=jnp.float32)
    gradient = (
        lax.dot_general(
            weights, query_rows, (((0,), (0,)), ((), ())), preferred_element_type=jnp.float32
        )
        * scale
    )
    return (toward, gradient)


def sparse_forward(running, query_rows, block_rows, visible):
    return forward_block(running, query_rows, block_rows, visible, None)


def sparse_backward(query_rows, block_rows, visible, log_total):
    return backward_block(query_rows, block_rows, visible, None, log_total)


def cell_backward(query_rows, cell_rows, visible_list, target_list, log_total):
    toward_sum = jnp.zeros((query_rows.shape[0], cell_rows.shape[1]), jnp.float32)
    pieces = []
    for block_at, visible in enumerate(visible_list):
        block_rows = cell_rows[block_at * BLK : (block_at + 1) * BLK]
        if target_list is None:
            toward, gradient = sparse_backward(query_rows, block_rows, visible, log_total)
        else:
            toward, gradient = backward_block(
                query_rows, block_rows, visible, target_list[block_at], log_total
            )
        toward_sum = toward_sum + toward
        pieces.append(gradient)
    return (toward_sum, jnp.concatenate(pieces, axis=0))


def roll_cells(cell_rows, offset):
    return from_behind(cell_rows, "col", offset)


def roll_terms(gradient, offset):
    return from_behind(gradient, "col", offset)


def local(queries, passages, positive, block_mask, roster):
    n_row = lax.axis_size("row")
    n_col = lax.axis_size("col")
    reach = min(2, (n_row - 1) // 2)
    offsets = list(range(-reach, 0)) + list(range(1, reach + 1))
    blocks = passages.shape[0] // BLK
    scale = queries.shape[1] ** (-0.5)
    ahead = n_col // 2
    near_rows = [from_behind(passages, "row", -offset) for offset in offsets]
    random_rows = {}
    current = passages
    for stride in range(1, ahead + 1):
        current = roll_cells(current, 1)
        random_rows[stride] = current
    current = passages
    behind = 1
    current = roll_cells(current, -1)
    random_rows[n_col - behind] = current
    column_ids = jnp.arange(BLK, dtype=jnp.int32)
    target_block = positive // BLK
    own_visible = [
        (block_mask[:, block_at] == 1) | (target_block == block_at) for block_at in range(blocks)
    ]
    own_target = [
        (block_at * BLK + column_ids)[None, :] == positive[:, None] for block_at in range(blocks)
    ]
    near_visible = [
        [block_mask[:, (group_at + 1) * blocks + block_at] == 1 for block_at in range(blocks)]
        for group_at in range(len(offsets))
    ]
    random_visible = {}
    for stride in range(1, n_col):
        random_visible[stride] = [roster[:, stride - 1] == block_at for block_at in range(blocks)]
    count = queries.shape[0]
    running = (
        jnp.full((count,), LOWEST, jnp.float32),
        jnp.zeros((count,), jnp.float32),
        jnp.zeros((count,), jnp.float32),
    )
    for block_at in range(blocks):
        running = forward_block(
            running,
            queries,
            passages[block_at * BLK : (block_at + 1) * BLK],
            own_visible[block_at],
            own_target[block_at],
        )
    for group_at in range(len(offsets)):
        for block_at in range(blocks):
            running = sparse_forward(
                running,
                queries,
                near_rows[group_at][block_at * BLK : (block_at + 1) * BLK],
                near_visible[group_at][block_at],
            )
    for stride in range(1, n_col):
        for block_at in range(blocks):
            running = sparse_forward(
                running,
                queries,
                random_rows[stride][block_at * BLK : (block_at + 1) * BLK],
                random_visible[stride][block_at],
            )
    highest, summed, positive_score = running
    log_total = highest + jnp.log(summed)
    loss_total = lax.psum(jnp.sum(log_total - positive_score), ("row", "col"))
    loss = (loss_total / (count * n_row * n_col)).reshape(1)
    toward_total, own_gradient = cell_backward(
        queries, passages, own_visible, own_target, log_total
    )
    near_gradients = []
    for group_at in range(len(offsets)):
        toward, gradient = cell_backward(
            queries, near_rows[group_at], near_visible[group_at], None, log_total
        )
        toward_total = toward_total + toward
        near_gradients.append(gradient)
    random_gradients = {}
    for stride in range(1, n_col):
        toward, gradient = cell_backward(
            queries, random_rows[stride], random_visible[stride], None, log_total
        )
        toward_total = toward_total + toward
        random_gradients[stride] = gradient
    returned = jnp.zeros_like(own_gradient)
    for offset, gradient in zip(offsets, near_gradients):
        returned = returned + from_behind(gradient, "row", offset)
    carried = jnp.zeros_like(own_gradient)
    for stride in range(ahead, 0, -1):
        carried = roll_terms(random_gradients[stride] + carried, -1)
    behind = 1
    second = roll_terms(random_gradients[n_col - behind], 1)
    arrived = carried + second
    grad_queries = toward_total * scale
    grad_passages = own_gradient + returned + arrived
    return (loss, grad_queries, grad_passages)


def solution(mesh):
    return jax.shard_map(
        local,
        mesh=mesh,
        in_specs=(
            P(("rep", "row", "col"), None),
            P(("rep", "row", "col"), None),
            P(("rep", "row", "col")),
            P(("rep", "row", "col"), None),
            P(("rep", "row", "col"), None),
        ),
        out_specs=(P("rep"), P(("rep", "row", "col"), None), P(("rep", "row", "col"), None)),
        check_vma=False,
    )
```

profile of v0, /device:TPU:0, one launch (start us, length us, event | category | flops | bytes accessed | tf_op | source)
XLA Modules:
  0.0 148.9 jit_solution(16061129660458759586)
XLA Ops:
  0.7 5.1 %collective-permute-start.1 = (bf16[384,768]{1,0:T(8,128)(2,1)}, bf16[384,768]{1,0:T(8,128)(2,1)S(1)}, u32[]{:S(2)}, u32[]{:S(2)}) collective-permute-start(bf16[384,768]{1,0:T(8,128)(2,1)} %param.6), channel_id=1, source_target_pairs={{8,0},{16,8},{24,16},{0,24},{9,1},{17,9},{25,17},{1,25},{10,2},{18... | collective-permute-start | bytes 1769480 | tf_op jit(solution)/shard_map/ppermute | solution.py:15
  5.8 0.7 collective-permute-start.4
  6.5 1.1 compare_reduce_fusion.9
  7.6 0.9 compare_reduce_fusion
  8.4 0.7 compare_or_fusion
  9.2 1.3 select_reduce_fusion.36
  10.5 1.3 select_reduce_fusion.35
  11.8 0.4 select_reduce_fusion.34
  12.3 7.6 %collective-permute-done.1 = bf16[384,768]{1,0:T(8,128)(2,1)S(1)} collective-permute-done((bf16[384,768]{1,0:T(8,128)(2,1)}, bf16[384,768]{1,0:T(8,128)(2,1)S(1)}, u32[]{:S(2)}, u32[]{:S(2)}) %collective-permute-start.1) | collective-permute-done | bytes 589856 | tf_op jit(solution)/shard_map/ppermute | solution.py:15
  19.8 0.4 select_reduce_fusion.28
  20.2 0.4 select_reduce_fusion.29
  20.6 0.4 select_reduce_fusion.30
  21.1 11.1 %collective-permute-done = bf16[384,768]{1,0:T(8,128)(2,1)S(1)} collective-permute-done((bf16[384,768]{1,0:T(8,128)(2,1)}, bf16[384,768]{1,0:T(8,128)(2,1)S(1)}, u32[]{:S(2)}, u32[]{:S(2)}) %collective-permute-start) | collective-permute-done | bytes 589856 | tf_op jit(solution)/shard_map/ppermute | solution.py:15
  32.1 0.4 select_reduce_fusion.31
  32.5 0.4 select_reduce_fusion.32
  33.0 0.4 select_reduce_fusion.33
  33.4 0.4 select_reduce_fusion.19
  33.8 0.4 select_reduce_fusion.20
  34.2 0.4 select_reduce_fusion.21
  34.7 0.4 select_reduce_fusion.25
  35.1 0.4 select_reduce_fusion.26
  35.5 0.4 select_reduce_fusion.27
  35.9 8.1 %collective-permute-done.3 = bf16[384,768]{1,0:T(8,128)(2,1)S(1)} collective-permute-done((bf16[384,768]{1,0:T(8,128)(2,1)S(1)}, bf16[384,768]{1,0:T(8,128)(2,1)S(1)}, u32[]{:S(2)}, u32[]{:S(2)}) %collective-permute-start.3) | collective-permute-done | bytes 589856 | tf_op jit(solution)/shard_map/ppermute | solution.py:15
  44.0 0.4 select_reduce_fusion.22
  44.4 0.4 select_reduce_fusion.23
  44.8 0.4 select_reduce_fusion.24
  46.1 0.3 fusion.1
  46.4 0.7 subtract_reduce_fusion
  47.1 0.3 convolution_multiply_fusion.15
  47.4 0.3 convolution_multiply_fusion
  47.7 0.3 convolution_multiply_fusion.1
  48.0 0.3 convolution_multiply_fusion.2
  48.6 0.3 convolution_multiply_fusion.4
  48.9 0.3 convolution_multiply_fusion.5
  49.2 0.3 convolution_multiply_fusion.6
  51.5 0.3 convolution_multiply_fusion.16
  51.8 1.1 pad_maximum_fusion
  52.9 1.7 %collective-permute-start.5 = (f32[384,768]{1,0:T(8,128)}, f32[384,768]{1,0:T(8,128)}, u32[]{:S(2)}, u32[]{:S(2)}) collective-permute-start(f32[384,768]{1,0:T(8,128)} %pad_maximum_fusion), channel_id=1, source_target_pairs={{8,0},{16,8},{24,16},{0,24},{9,1},{17,9},{25,17},{1,25},{10,2},{18... | collective-permute-start | bytes 3538952 | tf_op jit(solution)/shard_map/ppermute | solution.py:15
  54.7 1.1 pad_maximum_fusion.1
  56.2 1.2 pad_maximum_fusion.3
  57.4 0.5 collective-permute-start.9
  57.9 1.6 %fusion.51 = f32[512,768]{1,0:T(8,128)} fusion(bf16[384,768]{1,0:T(8,128)(2,1)S(1)} %collective-permute-done, f32[512,128]{0,1:T(8,128)S(1)} %get-tuple-element.84, f32[512]{0:T(512)S(1)} %get-tuple-element.32, pred[512]{0:T(512)(128)(4,1)S(1)} %get-tuple-element.13), kind=kOutput, calls=%fused_computation.150 | convolution fusion | flops 100859904 | bytes 2034176 | tf_op jit(solution)/shard_map/dot_general | solution.py:48
  59.5 1.6 %fusion.48 = f32[512,768]{1,0:T(8,128)} fusion(bf16[384,768]{1,0:T(8,128)(2,1)S(1)} %collective-permute-done, f32[512,128]{0,1:T(8,128)S(1)} %get-tuple-element.82, f32[512]{0:T(512)S(1)} %get-tuple-element.32, pred[512]{0:T(512)(128)(4,1)S(1)} %get-tuple-element.12), kind=kOutput, calls=%fused_computation.147 | convolution fusion | flops 100859904 | bytes 2034176 | tf_op jit(solution)/shard_map/dot_general | solution.py:48
  61.0 1.5 %fusion.45 = f32[512,768]{1,0:T(8,128)} fusion(bf16[384,768]{1,0:T(8,128)(2,1)S(1)} %collective-permute-done, f32[512,128]{0,1:T(8,128)S(1)} %get-tuple-element.80, f32[512]{0:T(512)S(1)} %get-tuple-element.32, pred[512]{0:T(512)(128)(4,1)S(1)} %get-tuple-element.11), kind=kOutput, calls=%fused_computation.144 | convolution fusion | flops 100859904 | bytes 2034176 | tf_op jit(solution)/shard_map/dot_general | solution.py:48
  62.6 1.6 %fusion.42 = f32[512,768]{1,0:T(8,128)} fusion(bf16[384,768]{1,0:T(8,128)(2,1)S(1)} %collective-permute-done.1, f32[512,128]{0,1:T(8,128)S(1)} %get-tuple-element.78, f32[512]{0:T(512)S(1)} %get-tuple-element.32, pred[512]{0:T(512)(128)(4,1)S(1)} %get-tuple-element.10), kind=kOutput, calls=%fused_computation.141 | convolution fusion | flops 100859904 | bytes 2034176 | tf_op jit(solution)/shard_map/dot_general | solution.py:48
  64.2 1.5 %fusion.39 = f32[512,768]{1,0:T(8,128)} fusion(bf16[384,768]{1,0:T(8,128)(2,1)S(1)} %collective-permute-done.1, f32[512,128]{0,1:T(8,128)S(1)} %get-tuple-element.76, f32[512]{0:T(512)S(1)} %get-tuple-element.32, pred[512]{0:T(512)(128)(4,1)S(1)} %get-tuple-element.17), kind=kOutput, calls=%fused_computation.138 | convolution fusion | flops 100859904 | bytes 2034176 | tf_op jit(solution)/shard_map/dot_general | solution.py:48
  65.7 1.5 %fusion.36 = f32[512,768]{1,0:T(8,128)} fusion(bf16[384,768]{1,0:T(8,128)(2,1)S(1)} %collective-permute-done.1, f32[512,128]{0,1:T(8,128)S(1)} %get-tuple-element.74, f32[512]{0:T(512)S(1)} %get-tuple-element.32, pred[512]{0:T(512)(128)(4,1)S(1)} %get-tuple-element.9), kind=kOutput, calls=%fused_computation.135 | convolution fusion | flops 100859904 | bytes 2034176 | tf_op jit(solution)/shard_map/dot_general | solution.py:48
  67.3 1.6 %fusion.33 = f32[512,768]{1,0:T(8,128)} fusion(bf16[384,768]{1,0:T(8,128)(2,1)S(1)} %collective-permute-done.2, f32[512,128]{0,1:T(8,128)S(1)} %get-tuple-element.72, f32[512]{0:T(512)S(1)} %get-tuple-element.32, pred[512]{0:T(512)(128)(4,1)S(1)} %get-tuple-element.24), kind=kOutput, calls=%fused_computation.132 | convolution fusion | flops 100859904 | bytes 2034176 | tf_op jit(solution)/shard_map/dot_general | solution.py:48
  68.9 1.6 %fusion.30 = f32[512,768]{1,0:T(8,128)} fusion(bf16[384,768]{1,0:T(8,128)(2,1)S(1)} %collective-permute-done.2, f32[512,128]{0,1:T(8,128)S(1)} %get-tuple-element.70, f32[512]{0:T(512)S(1)} %get-tuple-element.32, pred[512]{0:T(512)(128)(4,1)S(1)} %get-tuple-element.19), kind=kOutput, calls=%fused_computation.129 | convolution fusion | flops 100859904 | bytes 2034176 | tf_op jit(solution)/shard_map/dot_general | solution.py:48
  70.5 1.5 %fusion.27 = f32[512,768]{1,0:T(8,128)} fusion(bf16[384,768]{1,0:T(8,128)(2,1)S(1)} %collective-permute-done.2, f32[512,128]{0,1:T(8,128)S(1)} %get-tuple-element.68, f32[512]{0:T(512)S(1)} %get-tuple-element.32, pred[512]{0:T(512)(128)(4,1)S(1)} %get-tuple-element.20), kind=kOutput, calls=%fused_computation.126 | convolution fusion | flops 100859904 | bytes 2034176 | tf_op jit(solution)/shard_map/dot_general | solution.py:48
  72.0 1.5 %fusion.24 = f32[512,768]{1,0:T(8,128)} fusion(bf16[384,768]{1,0:T(8,128)(2,1)S(1)} %collective-permute-done.3, f32[512,128]{0,1:T(8,128)S(1)} %get-tuple-element.66, f32[512]{0:T(512)S(1)} %get-tuple-element.32, pred[512]{0:T(512)(128)(4,1)S(1)} %get-tuple-element.26), kind=kOutput, calls=%fused_computation.123 | convolution fusion | flops 100859904 | bytes 2034176 | tf_op jit(solution)/shard_map/dot_general | solution.py:48
  73.5 1.6 %fusion.21 = f32[512,768]{1,0:T(8,128)} fusion(bf16[384,768]{1,0:T(8,128)(2,1)S(1)} %collective-permute-done.3, f32[512,128]{0,1:T(8,128)S(1)} %get-tuple-element.64, f32[512]{0:T(512)S(1)} %get-tuple-element.32, pred[512]{0:T(512)(128)(4,1)S(1)} %get-tuple-element.21), kind=kOutput, calls=%fused_computation.120 | convolution fusion | flops 100859904 | bytes 2034176 | tf_op jit(solution)/shard_map/dot_general | solution.py:48
  75.1 1.6 %fusion.13 = f32[512,768]{1,0:T(8,128)} fusion(bf16[384,768]{1,0:T(8,128)(2,1)S(1)} %collective-permute-done.4, f32[512,128]{0,1:T(8,128)S(1)} %get-tuple-element.60, f32[512]{0:T(512)S(1)} %get-tuple-element.32, pred[512]{0:T(512)(128)(4,1)S(1)} %get-tuple-element.25), kind=kOutput, calls=%fused_computation.114 | convolution fusion | flops 100859904 | bytes 2034176 | tf_op jit(solution)/shard_map/dot_general | solution.py:48
  76.7 1.5 %fusion.10 = f32[512,768]{1,0:T(8,128)} fusion(bf16[384,768]{1,0:T(8,128)(2,1)S(1)} %collective-permute-done.4, f32[512,128]{0,1:T(8,128)S(1)} %get-tuple-element.58, f32[512]{0:T(512)S(1)} %get-tuple-element.32, pred[512]{0:T(512)(128)(4,1)S(1)} %get-tuple-element.23), kind=kOutput, calls=%fused_computation.111 | convolution fusion | flops 100859904 | bytes 2034176 | tf_op jit(solution)/shard_map/dot_general | solution.py:48
  78.5 1.5 %fusion.7 = f32[512,768]{1,0:T(8,128)} fusion(bf16[384,768]{1,0:T(8,128)(2,1)S(1)} %collective-permute-done.4, f32[512,128]{0,1:T(8,128)S(1)} %get-tuple-element.56, f32[512]{0:T(512)S(1)} %get-tuple-element.32, pred[512]{0:T(512)(128)(4,1)S(1)} %get-tuple-element.18), kind=kOutput, calls=%fused_computation.108 | convolution fusion | flops 100859904 | bytes 2034176 | tf_op jit(solution)/shard_map/dot_general | solution.py:48
  80.1 0.4 fusion.60
  80.5 1.7 %fusion.57 = f32[512,768]{1,0:T(8,128)} fusion(bf16[384,768]{1,0:T(8,128)(2,1)S(1)} %copy-done.3, f32[512,128]{0,1:T(8,128)S(1)} %get-tuple-element.88, f32[512]{0:T(512)S(1)} %get-tuple-element.32, s32[512]{0:T(512)S(1)} %copy-done.4, s32[128]{0:T(128)S(1)} %iota_add_fusion.1, pred[512]{0:T(512)(128)(4,1)S(1)} %get-tuple-element.54), kind=kOutput, calls=%fused_computation.156 | convolution fusion | flops 101056512 | bytes 2036736 | tf_op jit(solution)/shard_map/dot_general | solution.py:48
  82.2 1.6 %fusion.54 = f32[512,768]{1,0:T(8,128)} fusion(bf16[384,768]{1,0:T(8,128)(2,1)S(1)} %copy-done.3, f32[512,128]{0,1:T(8,128)S(1)} %get-tuple-element.86, f32[512]{0:T(512)S(1)} %get-tuple-element.32, s32[512]{0:T(512)S(1)} %copy-done.4, s32[128]{0:T(128)S(1)} %iota_add_fusion, pred[512]{0:T(512)(128)(4,1)S(1)} %get-tuple-element.50), kind=kOutput, calls=%fused_computation.153 | convolution fusion | flops 101056512 | bytes 2036736 | tf_op jit(solution)/shard_map/dot_general | solution.py:48
  83.8 1.1 maximum_add_fusion.1
  84.9 1.2 collective-permute-start.8
  86.2 1.1 convolution_multiply_fusion.17
  87.2 45.1 %psum.7 = f32[]{:T(128)} all-reduce(f32[]{:T(128)} %get-tuple-element.31), channel_id=1, replica_groups=mesh['row'=4,'col'=4,'rep'=2] {'row','col'}, use_global_device_ids=true, to_apply=%region_40.41 | all-reduce | flops 1 | bytes 8 | tf_op jit(solution)/shard_map/psum | solution.py:155
  133.0 11.0 %add_multiply_fusion = f32[512,768]{1,0:T(8,128)} fusion(f32[512,768]{1,0:T(8,128)} %fusion.7, f32[512,768]{1,0:T(8,128)} %fusion.13, f32[512,768]{1,0:T(8,128)} %fusion.10, f32[512,768]{1,0:T(8,128)} %fusion.24, f32[512,768]{1,0:T(8,128)} %fusion.21, f32[512,768]{1,0:T(8,128)} %fusion.27, f32[512,768]{1,0:T(8,128)} %fusion.33, f32[512,768]{1,0:T(8,128)} %fusion.30, ...), kind=kOutput, calls=%fused_computation | convolution fusion | flops 107937792 | bytes 28772864 | tf_op jit(solution)/shard_map/dot_general | solution.py:48
  144.1 3.7 %fusion = f32[384,768]{1,0:T(8,128)} fusion(f32[128,768]{1,0:T(8,128)S(1)} %convolution_multiply_fusion.15, f32[128,768]{1,0:T(8,128)S(1)} %convolution_multiply_fusion.16, f32[128,768]{1,0:T(8,128)S(1)} %copy-done.1, f32[384,768]{1,0:T(8,128)} %collective-permute-done.8, f32[384,768]{1,0:T(8,128)} %collective-permute-done.9, ...), kind=kLoop, calls=%fused_computation.20 | loop fusion | flops 1769472 | bytes 7077888 | tf_op jit(solution)/shard_map/add | solution.py:184
  (43 shorter events, 3.9 us)
Async XLA Ops:
  0.6 8.5 %copy-start = (bf16[512,768]{1,0:T(8,128)(2,1)S(1)}, bf16[512,768]{1,0:T(8,128)(2,1)}, u32[]{:S(2)}) copy-start(bf16[512,768]{1,0:T(8,128)(2,1)} %param.5) | copy-start | bytes 2359300
  0.6 11.2 %copy-start.3 = (bf16[384,768]{1,0:T(8,128)(2,1)S(1)}, bf16[384,768]{1,0:T(8,128)(2,1)}, u32[]{:S(2)}) copy-start(bf16[384,768]{1,0:T(8,128)(2,1)} %param.6) | copy-start | bytes 1769476
  0.7 19.2 %collective-permute-start.1 = (bf16[384,768]{1,0:T(8,128)(2,1)}, bf16[384,768]{1,0:T(8,128)(2,1)S(1)}, u32[]{:S(2)}, u32[]{:S(2)}) collective-permute-start(bf16[384,768]{1,0:T(8,128)(2,1)} %param.6), channel_id=1, source_target_pairs={{8,0},{16,8},{24,16},{0,24},{9,1},{17,9},{25,17},{1,25},{10,2},{18... | collective-permute-start | bytes 1769480 | tf_op jit(solution)/shard_map/ppermute | solution.py:15
  5.8 26.3 %collective-permute-start = (bf16[384,768]{1,0:T(8,128)(2,1)}, bf16[384,768]{1,0:T(8,128)(2,1)S(1)}, u32[]{:S(2)}, u32[]{:S(2)}) collective-permute-start(bf16[384,768]{1,0:T(8,128)(2,1)} %param.6), channel_id=1, source_target_pairs={{24,0},{0,8},{8,16},{16,24},{25,1},{1,9},{9,17},{17,25},{26,2},{2,... | collective-permute-start | bytes 1769480 | tf_op jit(solution)/shard_map/ppermute | solution.py:15
  5.8 27.6 %collective-permute-start.4 = (bf16[384,768]{1,0:T(8,128)(2,1)}, bf16[384,768]{1,0:T(8,128)(2,1)S(1)}, u32[]{:S(2)}, u32[]{:S(2)}) collective-permute-start(bf16[384,768]{1,0:T(8,128)(2,1)} %param.6), channel_id=1, source_target_pairs={{2,0},{4,2},{6,4},{0,6},{3,1},{5,3},{7,5},{1,7},{10,8},{12,10},{14... | collective-permute-start | bytes 1769480 | tf_op jit(solution)/shard_map/ppermute | solution.py:15
  6.5 28.1 %collective-permute-start.2 = (bf16[384,768]{1,0:T(8,128)(2,1)}, bf16[384,768]{1,0:T(8,128)(2,1)S(1)}, u32[]{:S(2)}, u32[]{:S(2)}) collective-permute-start(bf16[384,768]{1,0:T(8,128)(2,1)} %param.6), channel_id=1, source_target_pairs={{6,0},{0,2},{2,4},{4,6},{7,1},{1,3},{3,5},{5,7},{14,8},{8,10},{10,... | collective-permute-start | bytes 1769480 | tf_op jit(solution)/shard_map/ppermute | solution.py:15
  34.6 9.4 %collective-permute-start.3 = (bf16[384,768]{1,0:T(8,128)(2,1)S(1)}, bf16[384,768]{1,0:T(8,128)(2,1)S(1)}, u32[]{:S(2)}, u32[]{:S(2)}) collective-permute-start(bf16[384,768]{1,0:T(8,128)(2,1)S(1)} %collective-permute-done.2), channel_id=1, source_target_pairs={{6,0},{0,2},{2,4},{4,6},{7,1},{1,3},{3,5},{5,7},{14,8},{8,10},{10,... | collective-permute-start | bytes 1769480 | tf_op jit(solution)/shard_map/ppermute | solution.py:15
  44.0 29.6 %copy-start.2 = (bf16[384,768]{1,0:T(8,128)(2,1)}, bf16[384,768]{1,0:T(8,128)(2,1)S(1)}, u32[]{:S(2)}) copy-start(bf16[384,768]{1,0:T(8,128)(2,1)S(1)} %collective-permute-done.3) | copy-start | bytes 1769476
  45.4 0.7 copy-start.4
  52.9 91.1 %collective-permute-start.5 = (f32[384,768]{1,0:T(8,128)}, f32[384,768]{1,0:T(8,128)}, u32[]{:S(2)}, u32[]{:S(2)}) collective-permute-start(f32[384,768]{1,0:T(8,128)} %pad_maximum_fusion), channel_id=1, source_target_pairs={{8,0},{16,8},{24,16},{0,24},{9,1},{17,9},{25,17},{1,25},{10,2},{18... | collective-permute-start | bytes 3538952 | tf_op jit(solution)/shard_map/ppermute | solution.py:15
  55.8 88.2 %collective-permute-start.6 = (f32[384,768]{1,0:T(8,128)}, f32[384,768]{1,0:T(8,128)}, u32[]{:S(2)}, u32[]{:S(2)}) collective-permute-start(f32[384,768]{1,0:T(8,128)} %pad_maximum_fusion.1), channel_id=1, source_target_pairs={{24,0},{0,8},{8,16},{16,24},{25,1},{1,9},{9,17},{17,25},{26,2},{2,... | collective-permute-start | bytes 3538952 | tf_op jit(solution)/shard_map/ppermute | solution.py:15
  56.2 27.6 %collective-permute-start.7 = (f32[384,768]{1,0:T(8,128)S(1)}, f32[384,768]{1,0:T(8,128)S(1)}, u32[]{:S(2)}, u32[]{:S(2)}) collective-permute-start(f32[384,768]{1,0:T(8,128)S(1)} %pad_maximum_fusion.2), channel_id=1, source_target_pairs={{2,0},{4,2},{6,4},{0,6},{3,1},{5,3},{7,5},{1,7},{10,8},{12,10},{14... | collective-permute-start | bytes 3538952 | tf_op jit(solution)/shard_map/ppermute | solution.py:15
  57.4 86.7 %collective-permute-start.9 = (f32[384,768]{1,0:T(8,128)}, f32[384,768]{1,0:T(8,128)}, u32[]{:S(2)}, u32[]{:S(2)}) collective-permute-start(f32[384,768]{1,0:T(8,128)} %pad_maximum_fusion.3), channel_id=1, source_target_pairs={{6,0},{0,2},{2,4},{4,6},{7,1},{1,3},{3,5},{5,7},{14,8},{8,10},{10,... | collective-permute-start | bytes 3538952 | tf_op jit(solution)/shard_map/ppermute | solution.py:15
  84.9 59.1 %collective-permute-start.8 = (f32[384,768]{1,0:T(8,128)}, f32[384,768]{1,0:T(8,128)}, u32[]{:S(2)}, u32[]{:S(2)}) collective-permute-start(f32[384,768]{1,0:T(8,128)} %maximum_add_fusion.1), channel_id=1, source_target_pairs={{2,0},{4,2},{6,4},{0,6},{3,1},{5,3},{7,5},{1,7},{10,8},{12,10},{14... | collective-permute-start | bytes 3538952 | tf_op jit(solution)/shard_map/ppermute | solution.py:15
  133.0 11.1 %copy-start.1 = (f32[128,768]{1,0:T(8,128)S(1)}, f32[128,768]{1,0:T(8,128)}, u32[]{:S(2)}) copy-start(f32[128,768]{1,0:T(8,128)} %convolution_multiply_fusion.17) | copy-start | bytes 1179652
where the time goes:
time: 149 us
  matrix products  51.8 us (35%)
  blocking collectives  45.1 us (30%)
  waiting for transfers between devices  26.7 us (18%)
  other arithmetic  12.8 us (9%)
  starting transfers between devices  9.7 us (7%)
  between operations  2.79 us (2%)
    psum x1, blocking collectives, local(): loss_total = lax.psum(jnp.sum(log_total - positive_score), ('row', 'col'))  45.1 us
    dot_general x18, matrix products, backward_block(): toward = jnp.dot(weights, block_rows, preferred_element_type=jnp.float32)  36.6 us
    ppermute x10, waiting for transfers between devices, from_behind(): return lax.ppermute(block, axis, route)  26.7 us
    ppermute x10, starting transfers between devices, from_behind(): return lax.ppermute(block, axis, route)  9.7 us
    dot_general x18, matrix products, block_scores(): lax.dot_general(query_rows, block_rows, (((1,), (1,)), ((), ())), preferr...  9.2 us
    dot_general x18, matrix products, backward_block(): lax.dot_general(weights, query_rows, (((0,), (0,)), ((), ())), preferred_...  5.95 us
    add x1, other arithmetic, local(): grad_passages = own_gradient + returned + arrived  3.72 us
    concatenate x4, other arithmetic, cell_backward(): return (toward_sum, jnp.concatenate(pieces, axis=0))  3.45 us
  transfers between devices with their start and end apart: 10, of which 3 were waited for; matrix products, arithmetic and copies ran while one was open for 35% of the time, Pallas kernels for 0%

commit v1 on v0

v1 whole, which is shorter than its diff:
```python
import functools
import math

import jax
import jax.numpy as jnp
from jax import lax
from jax.experimental import pallas as pl
from jax.experimental.pallas import tpu as pltpu
from jax.sharding import PartitionSpec as P

BLK = 128
LOWEST = -1e30
LOG2E = math.log2(math.e)
VMEM_LIMIT = 24 << 20


def whole():
    return pl.BlockSpec(memory_space=pltpu.VMEM)


def call(kernel, name, outs, ins, flops, exps=0):
    moved = sum(a.size * a.dtype.itemsize for a in (*outs, *ins))
    return pl.pallas_call(
        kernel,
        name=name,
        out_shape=tuple(outs),
        in_specs=[whole() for _ in ins],
        out_specs=tuple(whole() for _ in outs),
        compiler_params=pltpu.CompilerParams(vmem_limit_bytes=VMEM_LIMIT),
        cost_estimate=pl.CostEstimate(flops=flops, bytes_accessed=moved, transcendentals=exps),
    )(*ins)


def send(array, axis, pairs):
    return lax.ppermute(array, axis, pairs)


def block_stats(scores, block_at, scale):
    part = scores[block_at * BLK : (block_at + 1) * BLK]
    highest = jnp.max(part, axis=0, keepdims=True)
    raised = jnp.exp2((part - highest) * (scale * LOG2E))
    return part, highest, raised, jnp.sum(raised, axis=0, keepdims=True)


def scores_of(q_ref, p_ref):
    return lax.dot_general(
        p_ref[...], q_ref[...], (((1,), (1,)), ((), ())), preferred_element_type=jnp.float32
    )


def scores_body(scale, blocks, own, *refs):
    if own:
        q_ref, p_ref, pos_ref, e_ref, stats_ref = refs
    else:
        q_ref, p_ref, e_ref, stats_ref = refs
    scores = scores_of(q_ref, p_ref)
    stats_ref[...] = jnp.zeros_like(stats_ref)
    picked = None
    for block_at in range(blocks):
        part, highest, raised, summed = block_stats(scores, block_at, scale)
        e_ref[block_at * BLK : (block_at + 1) * BLK, :] = raised
        stats_ref[block_at : block_at + 1, :] = highest * scale
        stats_ref[blocks + block_at : blocks + block_at + 1, :] = summed
        if own:
            rows = lax.broadcasted_iota(jnp.int32, part.shape, 0) + block_at * BLK
            hit = jnp.sum(jnp.where(rows == pos_ref[...], part, 0.0), axis=0, keepdims=True)
            picked = hit if picked is None else picked + hit
    if own:
        stats_ref[2 * blocks : 2 * blocks + 1, :] = picked * scale


def weights_of(e_ref, f, blocks, pos):
    parts = []
    for block_at in range(blocks):
        part = e_ref[block_at * BLK : (block_at + 1) * BLK, :] * f[block_at : block_at + 1, :]
        if pos is not None:
            rows = lax.broadcasted_iota(jnp.int32, part.shape, 0) + block_at * BLK
            part = part - jnp.where(rows == pos, 1.0, 0.0)
        parts.append(part.astype(jnp.bfloat16))
    return jnp.concatenate(parts, axis=0)


def last_body(scale, blocks, cells, first, *refs):
    q_ref, p_ref, e_first_ref, vis_ref = refs[:4]
    stats_refs = refs[4 : 4 + cells - 1]
    e_ref, f_ref, g_ref, w_ref, loss_ref = refs[4 + cells - 1 :]
    scores = scores_of(q_ref, p_ref)
    tops, sums = [], []
    for block_at in range(blocks):
        _, highest, raised, summed = block_stats(scores, block_at, scale)
        e_ref[block_at * BLK : (block_at + 1) * BLK, :] = raised
        tops.append(highest * scale)
        sums.append(summed)
    all_tops = [s[0:blocks, :] for s in stats_refs] + [jnp.concatenate(tops, axis=0)]
    all_sums = [s[blocks : 2 * blocks, :] for s in stats_refs] + [jnp.concatenate(sums, axis=0)]
    seen = [vis_ref[cell * 8 : cell * 8 + blocks, :] > 0 for cell in range(cells)]
    highest = None
    for cell in range(cells):
        top = jnp.max(jnp.where(seen[cell], all_tops[cell], LOWEST), axis=0, keepdims=True)
        highest = top if highest is None else jnp.maximum(highest, top)
    total = None
    for cell in range(cells):
        gap = jnp.where(seen[cell], all_tops[cell] - highest, LOWEST)
        part = jnp.sum(all_sums[cell] * jnp.exp(gap), axis=0, keepdims=True)
        total = part if total is None else total + part
    log_total = highest + jnp.log(total)
    factors = []
    f_ref[...] = jnp.zeros_like(f_ref)
    for cell in range(cells):
        factor = jnp.exp(jnp.where(seen[cell], all_tops[cell] - log_total, LOWEST))
        f_ref[cell * 8 : cell * 8 + blocks, :] = factor
        factors.append(factor)
    positive_score = stats_refs[0][2 * blocks : 2 * blocks + 1, :]
    lost = jnp.sum(log_total - positive_score, axis=1, keepdims=True)
    loss_ref[...] = jnp.broadcast_to(lost, loss_ref.shape)
    weights = weights_of(e_first_ref, factors[first], blocks, None)
    w_ref[...] = weights
    gradient = jnp.dot(weights, q_ref[...], preferred_element_type=jnp.float32) * scale
    g_ref[...] = gradient.astype(g_ref.dtype)


def gradient_body(scale, blocks, cell, own, added, *refs):
    refs = list(refs)
    q_ref, e_ref, f_ref = refs[:3]
    del refs[:3]
    pos = refs.pop(0)[...] if own else None
    more_ref = refs.pop(0) if added else None
    g_ref, w_ref = refs
    weights = weights_of(e_ref, f_ref[cell * 8 : cell * 8 + 8, :], blocks, pos)
    w_ref[...] = weights
    gradient = jnp.dot(weights, q_ref[...], preferred_element_type=jnp.float32) * scale
    if added:
        gradient = gradient + more_ref[...].astype(jnp.float32)
    g_ref[...] = gradient.astype(g_ref.dtype)


def toward_body(scale, cells, *refs):
    w_refs, p_refs, out_ref = refs[:cells], refs[cells : 2 * cells], refs[2 * cells]
    total = None
    for w_ref, p_ref in zip(w_refs, p_refs):
        part = lax.dot_general(
            w_ref[...], p_ref[...], (((0,), (0,)), ((), ())), preferred_element_type=jnp.float32
        )
        total = part if total is None else total + part
    out_ref[...] = total * scale


def row_plan(n_row, reach):
    plan = []
    if reach == 1 and n_row % 2 == 0:
        even_up = [(i, i ^ 1) for i in range(n_row)]
        odd_up = [(i, (i + 1) % n_row if i % 2 else (i - 1) % n_row) for i in range(n_row)]
        plan.append((even_up, even_up, (2, 1)))
        plan.append((odd_up, odd_up, (1, 2)))
        return plan
    offsets = list(range(-reach, 0)) + list(range(1, reach + 1))
    for group_at, offset in enumerate(offsets):
        there = [((i + offset) % n_row, i) for i in range(n_row)]
        back = [(i, (i + offset) % n_row) for i in range(n_row)]
        plan.append((there, back, (group_at + 1, group_at + 1)))
    return plan


def sum_over(array, axis):
    size = lax.axis_size(axis)
    if size & (size - 1):
        return lax.psum(array, axis)
    step = 1
    while step < size:
        array = array + send(array, axis, [(i, i ^ step) for i in range(size)])
        step *= 2
    return array


def local(queries, passages, positive, block_mask, roster):
    n_row = lax.axis_size("row")
    n_col = lax.axis_size("col")
    reach = min(2, (n_row - 1) // 2)
    count, width = queries.shape
    held = passages.shape[0]
    blocks = held // BLK
    scale = width ** (-0.5)
    odd_row = lax.axis_index("row") % 2 == 1
    odd_col = lax.axis_index("col") % 2 == 1
    f32, bf16 = jnp.float32, jnp.bfloat16

    rows = row_plan(n_row, reach)
    near = [send(passages, "row", there) for there, _, _ in rows]

    swap = [(i, i ^ 1) for i in range(n_col)]
    col_cells = []
    paired = n_col % 2 == 0
    if paired:
        col_cells.append((send(passages, "col", swap), 1, n_col - 1))
        for apart in range(1, n_col // 2):
            far = send(passages, "col", [(i, (i + 2 * apart) % n_col) for i in range(n_col)])
            cross = send(far, "col", swap)
            col_cells.append((far, 2 * apart, 2 * apart))
            col_cells.append((cross, 2 * apart + 1, 2 * apart - 1))
    else:
        for stride in range(1, n_col):
            far = send(passages, "col", [(i, (i + stride) % n_col) for i in range(n_col)])
            col_cells.append((far, stride, stride))

    mask_t = block_mask.T
    roster_t = roster.T
    pos = positive.reshape(1, count)
    ids = jnp.arange(blocks, dtype=jnp.int32)[:, None]
    pad = jnp.zeros((8 - blocks, count), f32)

    def padded(flags):
        return jnp.concatenate([flags.astype(f32), pad], axis=0)

    def group_rows(group):
        return mask_t[group * blocks : (group + 1) * blocks] == 1

    seen = [padded(group_rows(0) | (pos // BLK == ids))]
    for _, odd, even in col_cells:
        seen.append(
            padded(jnp.where(odd_col, roster_t[odd - 1][None], roster_t[even - 1][None]) == ids)
        )
    for _, _, (even, odd) in rows:
        seen.append(padded(jnp.where(odd_row, group_rows(odd), group_rows(even))))
    vis = jnp.concatenate(seen, axis=0)

    cell_rows = [passages] + [cell[0] for cell in col_cells] + near
    cells = len(cell_rows)
    e_shape = jax.ShapeDtypeStruct((held, count), f32)
    w_shape = jax.ShapeDtypeStruct((held, count), bf16)
    s_shape = jax.ShapeDtypeStruct((8, count), f32)
    g_wire = jax.ShapeDtypeStruct((held, width), bf16)
    g_wide = jax.ShapeDtypeStruct((held, width), f32)
    dot_flops = 2 * held * count * width

    raised, stats = [], []
    for cell in range(cells - 1):
        own = cell == 0
        ins = (queries, cell_rows[cell]) + ((pos,) if own else ())
        e, s = call(
            functools.partial(scores_body, scale, blocks, own),
            f"scores_{cell}",
            (e_shape, s_shape),
            ins,
            dot_flops,
            held * count,
        )
        raised.append(e)
        stats.append(s)

    first = cells - len(rows)
    last = cells - 1
    f_shape = jax.ShapeDtypeStruct((8 * cells, count), f32)
    loss_shape = jax.ShapeDtypeStruct((8, BLK), f32)
    e, factors, g_first, w_first, lost = call(
        functools.partial(last_body, scale, blocks, cells, first),
        "last",
        (e_shape, f_shape, g_wire, w_shape, loss_shape),
        (queries, cell_rows[last], raised[first], vis, *stats),
        2 * dot_flops,
        held * count,
    )
    raised.append(e)
    weights = {first: w_first}

    def gradient_of(cell, shape, added=None):
        own = cell == 0
        ins = (queries, raised[cell], factors)
        ins += ((pos,) if own else ()) + (() if added is None else (added,))
        g, w = call(
            functools.partial(gradient_body, scale, blocks, cell, own, added is not None),
            f"gradient_{cell}",
            (shape, w_shape),
            ins,
            dot_flops,
        )
        weights[cell] = w
        return g

    returned = []
    for at, (_, back, _) in enumerate(rows):
        g = g_first if at == 0 else gradient_of(first + at, g_wire)
        returned.append(send(g, "row", back))

    if paired:
        handed = []
        for apart in range(1, n_col // 2):
            handed.append(send(gradient_of(1 + 2 * apart, g_wire), "col", swap))
        for apart in range(1, n_col // 2):
            g = gradient_of(2 * apart, g_wire, handed[apart - 1])
            back = [(i, (i - 2 * apart) % n_col) for i in range(n_col)]
            returned.append(send(g, "col", back))
        returned.append(send(gradient_of(1, g_wire), "col", swap))
    else:
        for stride in range(1, n_col):
            back = [(i, (i - stride) % n_col) for i in range(n_col)]
            returned.append(send(gradient_of(stride, g_wire), "col", back))
    g_own = gradient_of(0, g_wide)

    (toward,) = call(
        functools.partial(toward_body, scale, cells),
        "toward",
        (jax.ShapeDtypeStruct((count, width), f32),),
        (*[weights[cell] for cell in range(cells)], *cell_rows),
        cells * dot_flops,
    )

    loss_total = sum_over(sum_over(lost, "col"), "row")
    loss = loss_total[0, :1] / (count * n_row * n_col)

    near_count = len(rows)
    grad_passages = g_own
    for g in returned[near_count:] + returned[:near_count]:
        grad_passages = grad_passages + g.astype(f32)
    return (loss, toward, grad_passages)


def solution(mesh):
    return jax.shard_map(
        local,
        mesh=mesh,
        in_specs=(
            P(("rep", "row", "col"), None),
            P(("rep", "row", "col"), None),
            P(("rep", "row", "col")),
            P(("rep", "row", "col"), None),
            P(("rep", "row", "col"), None),
        ),
        out_specs=(P("rep"), P(("rep", "row", "col"), None), P(("rep", "row", "col"), None)),
        check_vma=False,
    )
```

time: 149 us -> 78.4 us (0.53)
  matrix products: 51.8 us -> 0 us
  blocking collectives: 45.1 us -> 0 us
  waiting for transfers between devices: 26.7 us -> 42.2 us
  Pallas kernels: 0 us -> 10.6 us
  other arithmetic: 12.8 us -> 3.71 us
  starting transfers between devices: 9.7 us -> 15.5 us
  local copies, waits for them, and re-layouts: 0.03 us -> 3.53 us
    dot_general x54 -> x0, matrix products: 51.8 us -> none  [the longest x18 36.6 us: backward_block(): toward = jnp.dot(weights, block_rows, preferred_element_type=jnp.float32)]
    psum x1 -> x0, blocking collectives: 45.1 us -> none  [local(): loss_total = lax.psum(jnp.sum(log_total - positive_score), ('row', 'col'))]
    ppermute x10 -> x14, waiting for transfers between devices: 26.7 us -> 42.2 us  [send(): return lax.ppermute(array, axis, pairs)]
    pallas_call x0 -> x12, Pallas kernels: none -> 10.6 us  [call(): pl.pallas_call(kernel, name=name, out_shape=tuple(outs), in_specs=[whole(...]
    ppermute x10 -> x14, starting transfers between devices: 9.7 us -> 15.5 us  [send(): return lax.ppermute(array, axis, pairs)]
    add x4 -> x5, other arithmetic: 4.88 us -> 1.34 us  [the longest x1 1.32 us: local(): grad_passages = grad_passages + g.astype(f32)]
    concatenate x4 -> x0, other arithmetic: 3.45 us -> none  [cell_backward(): return (toward_sum, jnp.concatenate(pieces, axis=0))]
    unnamed x10, local copies, waits for them, and re-layouts: 0.03 us -> 2.89 us
  transfers between devices with their start and end apart: 10 -> 14, of which waited for: 3 -> 6; matrix products, arithmetic and copies ran while one was open for 35% -> 4% of each run, Pallas kernels for 0% -> 11%
where the time goes in v1:
time: 78.4 us; the launch traced here: 78.1 us
  waiting for transfers between devices  42.2 us (54%)
  starting transfers between devices  15.5 us (20%)
  Pallas kernels  10.6 us (14%)
  other arithmetic  3.71 us (5%)
  local copies, waits for them, and re-layouts  3.53 us (5%)
  between operations  2.56 us (3%)
    ppermute x14, waiting for transfers between devices, send(): return lax.ppermute(array, axis, pairs)  42.2 us
    ppermute x14, starting transfers between devices, send(): return lax.ppermute(array, axis, pairs)  15.5 us
    pallas_call x12, Pallas kernels, call(): pl.pallas_call(kernel, name=name, out_shape=tuple(outs), in_specs=[whole(...  10.6 us
    unnamed x10, local copies, waits for them, and re-layouts  2.89 us
  transfers between devices with their start and end apart: 14, of which 6 were waited for; matrix products, arithmetic and copies ran while one was open for 4% of the time, Pallas kernels for 11%

profile of v1, /device:TPU:0, one launch (start us, length us, event | category | flops | bytes accessed | tf_op | source)
XLA Modules:
  0.0 78.1 jit_solution(13045257914810442749)
XLA Ops:
  0.6 3.1 %collective-permute-start.3 = (bf16[384,768]{1,0:T(8,128)(2,1)}, bf16[384,768]{1,0:T(8,128)(2,1)S(1)}, u32[]{:S(2)}, u32[]{:S(2)}) collective-permute-start(bf16[384,768]{1,0:T(8,128)(2,1)} %refs_6_.1), channel_id=1, source_target_pairs={{0,4},{2,6},{4,0},{6,2},{1,5},{3,7},{5,1},{7,3},{8,12},{10,14},{12... | collective-permute-start | bytes 1769480 | tf_op jit(solution)/shard_map/ppermute | solution.py:35
  3.7 1.6 %collective-permute-start.1 = (bf16[384,768]{1,0:T(8,128)(2,1)}, bf16[384,768]{1,0:T(8,128)(2,1)S(1)}, u32[]{:S(2)}, u32[]{:S(2)}) collective-permute-start(bf16[384,768]{1,0:T(8,128)(2,1)} %refs_6_.1), channel_id=1, source_target_pairs={{0,8},{8,0},{16,24},{24,16},{1,9},{9,1},{17,25},{25,17},{2,10},{10... | collective-permute-start | bytes 1769480 | tf_op jit(solution)/shard_map/ppermute | solution.py:35
  5.3 0.0 collective-permute-start.2
  5.3 2.5 %collective-permute-start = (bf16[384,768]{1,0:T(8,128)(2,1)}, bf16[384,768]{1,0:T(8,128)(2,1)S(1)}, u32[]{:S(2)}, u32[]{:S(2)}) collective-permute-start(bf16[384,768]{1,0:T(8,128)(2,1)} %refs_6_.1), channel_id=1, source_target_pairs={{0,24},{8,16},{16,8},{24,0},{1,25},{9,17},{17,9},{25,1},{2,26},{10... | collective-permute-start | bytes 1769480 | tf_op jit(solution)/shard_map/ppermute | solution.py:35
  7.7 0.7 add_select_fusion
  8.4 0.8 %select_convert_fusion = (f32[3,512]{1,0:T(4,128)S(1)}, pred[3,512]{1,0:T(4,128)(4,1)S(1)}, pred[3,512]{1,0:T(4,128)(4,1)S(1)}, f32[3,512]{1,0:T(4,128)S(1)}) fusion(pred[]{:T(512)S(6)} %eq.95, s32[9,512]{1,0:T(8,128)} %bitcast.9, s32[512]{0:T(512)S(1)} %add_select_fusion), kind=kLoop, calls=%fused_computation.13 | loop fusion | flops 12288 | bytes 35841 | tf_op jit(solution)/shard_map/convert_element_type | solution.py:212
  9.3 7.9 %collective-permute-done.3.refs_1_.refs_8_ = bf16[384,768]{1,0:T(8,128)(2,1)S(1)} collective-permute-done((bf16[384,768]{1,0:T(8,128)(2,1)}, bf16[384,768]{1,0:T(8,128)(2,1)S(1)}, u32[]{:S(2)}, u32[]{:S(2)}) %collective-permute-start.3) | collective-permute-done | bytes 589856 | tf_op jit(solution)/shard_map/ppermute | solution.py:35
  17.2 0.0 collective-permute-start.4
  17.2 0.8 %broadcast_select_fusion = (s32[1,512]{1,0:T(1,128)S(1)}, s32[1,512]{1,0:T(1,128)S(1)}, s32[1,512]{1,0:T(1,128)S(1)}) fusion(pred[]{:T(512)S(6)} %eq.82, s32[3,512]{1,0:T(4,128)} %bitcast.13), kind=kLoop, calls=%fused_computation.15 | loop fusion | flops 1024 | bytes 12289 | tf_op jit(solution)/shard_map/jit(_where)/select_n | solution.py:220
  18.1 0.1 concatenate.3.refs_3_
  18.2 0.0 copy-start
  18.2 1.1 %copy-done = bf16[512,768]{1,0:T(8,128)(2,1)S(1)} copy-done((bf16[512,768]{1,0:T(8,128)(2,1)S(1)}, bf16[512,768]{1,0:T(8,128)(2,1)}, u32[]{:S(2)}) %copy-start) | copy-done | bytes 786456
  19.4 0.0 copy-start.1
  19.4 1.1 %copy-done.1 = bf16[384,768]{1,0:T(8,128)(2,1)S(1)} copy-done((bf16[384,768]{1,0:T(8,128)(2,1)S(1)}, bf16[384,768]{1,0:T(8,128)(2,1)}, u32[]{:S(2)}) %copy-start.1) | copy-done | bytes 589848
  20.4 0.0 copy-start.3
  20.4 0.7 copy-done.3
  21.1 0.7 scores_0.1
  21.8 0.6 scores_2.1
  22.4 0.0 collective-permute-done.1.refs_1_.refs_10_
  22.4 0.6 scores_4.1
  23.0 0.0 collective-permute-done.2.refs_1_.refs_7_
  23.0 0.6 scores_1.1
  23.7 0.0 collective-permute-done.4.refs_1_.refs_9_
  23.7 0.6 scores_3.1
  24.3 9.2 %collective-permute-done.refs_1_.refs_11_ = bf16[384,768]{1,0:T(8,128)(2,1)S(1)} collective-permute-done((bf16[384,768]{1,0:T(8,128)(2,1)}, bf16[384,768]{1,0:T(8,128)(2,1)S(1)}, u32[]{:S(2)}, u32[]{:S(2)}) %collective-permute-start) | collective-permute-done | bytes 589856 | tf_op jit(solution)/shard_map/ppermute | solution.py:35
  33.5 1.2 %last.1 = (f32[384,512]{1,0:T(8,128)S(1)}, f32[48,512]{1,0:T(8,128)S(1)}, bf16[384,768]{1,0:T(8,128)(2,1)S(1)}, bf16[384,512]{1,0:T(8,128)(2,1)S(1)}, f32[8,128]{1,0:T(8,128)S(1)}) custom-call(bf16[512,768]{1,0:T(8,128)(2,1)S(1)} %copy-done, bf16[384,768]{1,0:T(8,128)(2,1)S(1)} %collective-permute-done.refs_1_.refs_11_, ...), custom_call_target="tpu_custom_call" | custom-call | flops 603979776 | bytes 4214784 | tf_op jit(solution)/shard_map/last/pallas_call | solution.py:23
  34.6 0.5 gradient_3.1
  35.1 0.1 collective-permute-start.9
  35.2 0.5 gradient_5.1
  35.7 3.4 %collective-permute-start.13 = (bf16[384,768]{1,0:T(8,128)(2,1)S(1)}, bf16[384,768]{1,0:T(8,128)(2,1)S(1)}, u32[]{:S(2)}, u32[]{:S(2)}) collective-permute-start(bf16[384,768]{1,0:T(8,128)(2,1)S(1)} %get-tuple-element.52), channel_id=1, source_target_pairs={{0,24},{8,16},{16,8},{24,0},{1,25},{9,17},{17,9},{25,1},{2,26},{10... | collective-permute-start | bytes 1769480 | tf_op jit(solution)/shard_map/ppermute | solution.py:35
  39.1 0.5 gradient_1.1
  39.6 0.0 copy-start.4
  39.6 0.3 collective-permute-start.11
  39.9 0.2 collective-permute-start.12
  40.1 0.0 collective-permute-done.9.refs_3_
  40.1 0.5 gradient_2.1
  40.6 0.0 copy-start.2
  40.6 0.6 collective-permute-start.10
  41.2 0.0 collective-permute-start.5
  41.2 1.2 %collective-permute-done.5 = f32[8,128]{1,0:T(8,128)S(1)} collective-permute-done((f32[8,128]{1,0:T(8,128)S(1)}, f32[8,128]{1,0:T(8,128)S(1)}, u32[]{:S(2)}, u32[]{:S(2)}) %collective-permute-start.5) | collective-permute-done | bytes 4128 | tf_op jit(solution)/shard_map/ppermute | solution.py:35
  42.3 1.5 %collective-permute-start.6 = (f32[8,128]{1,0:T(8,128)S(1)}, f32[8,128]{1,0:T(8,128)S(1)}, u32[]{:S(2)}, u32[]{:S(2)}) collective-permute-start(f32[8,128]{1,0:T(8,128)S(1)} %add.35), channel_id=1, source_target_pairs={{0,4},{2,6},{4,0},{6,2},{1,5},{3,7},{5,1},{7,3},{8,12},{10,14},{12... | collective-permute-start | bytes 12296 | tf_op jit(solution)/shard_map/ppermute | solution.py:35
  43.8 12.2 %collective-permute-done.6 = f32[8,128]{1,0:T(8,128)S(1)} collective-permute-done((f32[8,128]{1,0:T(8,128)S(1)}, f32[8,128]{1,0:T(8,128)S(1)}, u32[]{:S(2)}, u32[]{:S(2)}) %collective-permute-start.6) | collective-permute-done | bytes 4128 | tf_op jit(solution)/shard_map/ppermute | solution.py:35
  56.1 1.7 %collective-permute-start.7 = (f32[8,128]{1,0:T(8,128)S(1)}, f32[8,128]{1,0:T(8,128)S(1)}, u32[]{:S(2)}, u32[]{:S(2)}) collective-permute-start(f32[8,128]{1,0:T(8,128)S(1)} %add.36), channel_id=1, source_target_pairs={{0,8},{8,0},{16,24},{24,16},{1,9},{9,1},{17,25},{25,17},{2,10},{10... | collective-permute-start | bytes 12296 | tf_op jit(solution)/shard_map/ppermute | solution.py:35
  57.8 8.3 %collective-permute-done.7 = f32[8,128]{1,0:T(8,128)S(1)} collective-permute-done((f32[8,128]{1,0:T(8,128)S(1)}, f32[8,128]{1,0:T(8,128)S(1)}, u32[]{:S(2)}, u32[]{:S(2)}) %collective-permute-start.7) | collective-permute-done | bytes 4128 | tf_op jit(solution)/shard_map/ppermute | solution.py:35
  66.1 0.6 collective-permute-start.8
  66.7 0.0 copy-done.4
  66.7 0.5 gradient_0.1
  67.2 3.4 %collective-permute-done.8 = f32[8,128]{1,0:T(8,128)S(1)} collective-permute-done((f32[8,128]{1,0:T(8,128)S(1)}, f32[8,128]{1,0:T(8,128)S(1)}, u32[]{:S(2)}, u32[]{:S(2)}) %collective-permute-start.8) | collective-permute-done | bytes 4128 | tf_op jit(solution)/shard_map/ppermute | solution.py:35
  70.6 0.5 slice.32
  71.8 0.0 copy-done.2
  71.8 3.8 %toward.1 = f32[512,768]{1,0:T(8,128)} custom-call(bf16[384,512]{1,0:T(8,128)(2,1)S(1)} %get-tuple-element.37.refs_0_, bf16[384,512]{1,0:T(8,128)(2,1)S(1)} %get-tuple-element.39.refs_1_, bf16[384,512]{1,0:T(8,128)(2,1)S(1)} %get-tuple-element.43.refs_2_, bf16[384,512]{1,0:T(8,128)(2,1)S(1)} %get-tuple-element.44.refs_3_, ...), custom_call_target="tpu_custom_call" | custom-call | flops 1811939328 | bytes 7471104 | tf_op jit(solution)/shard_map/toward/pallas_call | solution.py:23
  75.6 0.0 collective-permute-done.13
  75.6 0.0 collective-permute-done.11
  75.6 0.0 collective-permute-done.12
  75.6 0.0 collective-permute-done.10
  75.6 1.3 %convert_add_fusion = f32[384,768]{1,0:T(8,128)} fusion(bf16[384,768]{1,0:T(8,128)(2,1)S(1)} %collective-permute-done.13, bf16[384,768]{1,0:T(8,128)(2,1)S(1)} %collective-permute-done.12, bf16[384,768]{1,0:T(8,128)(2,1)S(1)} %collective-permute-done.11, f32[384,768]{1,0:T(8,128)S(1)} %get-tuple-element.48, bf16[384,768]{1,0:T(8,128)(2,1)S(1)} %collective-permute-done.10), kind=kLoop, calls=%fused_computation | loop fusion | flops 2359296 | bytes 4718592 | tf_op jit(solution)/shard_map/add | solution.py:313
  (7 shorter events, 0.0 us)
Async XLA Ops:
  0.6 16.6 %collective-permute-start.3 = (bf16[384,768]{1,0:T(8,128)(2,1)}, bf16[384,768]{1,0:T(8,128)(2,1)S(1)}, u32[]{:S(2)}, u32[]{:S(2)}) collective-permute-start(bf16[384,768]{1,0:T(8,128)(2,1)} %refs_6_.1), channel_id=1, source_target_pairs={{0,4},{2,6},{4,0},{6,2},{1,5},{3,7},{5,1},{7,3},{8,12},{10,14},{12... | collective-permute-start | bytes 1769480 | tf_op jit(solution)/shard_map/ppermute | solution.py:35
  3.7 18.7 %collective-permute-start.1 = (bf16[384,768]{1,0:T(8,128)(2,1)}, bf16[384,768]{1,0:T(8,128)(2,1)S(1)}, u32[]{:S(2)}, u32[]{:S(2)}) collective-permute-start(bf16[384,768]{1,0:T(8,128)(2,1)} %refs_6_.1), channel_id=1, source_target_pairs={{0,8},{8,0},{16,24},{24,16},{1,9},{9,1},{17,25},{25,17},{2,10},{10... | collective-permute-start | bytes 1769480 | tf_op jit(solution)/shard_map/ppermute | solution.py:35
  5.3 17.8 %collective-permute-start.2 = (bf16[384,768]{1,0:T(8,128)(2,1)}, bf16[384,768]{1,0:T(8,128)(2,1)S(1)}, u32[]{:S(2)}, u32[]{:S(2)}) collective-permute-start(bf16[384,768]{1,0:T(8,128)(2,1)} %refs_6_.1), channel_id=1, source_target_pairs={{0,2},{2,0},{4,6},{6,4},{1,3},{3,1},{5,7},{7,5},{8,10},{10,8},{12,... | collective-permute-start | bytes 1769480 | tf_op jit(solution)/shard_map/ppermute | solution.py:35
  5.3 28.2 %collective-permute-start = (bf16[384,768]{1,0:T(8,128)(2,1)}, bf16[384,768]{1,0:T(8,128)(2,1)S(1)}, u32[]{:S(2)}, u32[]{:S(2)}) collective-permute-start(bf16[384,768]{1,0:T(8,128)(2,1)} %refs_6_.1), channel_id=1, source_target_pairs={{0,24},{8,16},{16,8},{24,0},{1,25},{9,17},{17,9},{25,1},{2,26},{10... | collective-permute-start | bytes 1769480 | tf_op jit(solution)/shard_map/ppermute | solution.py:35
  17.2 6.4 %collective-permute-start.4 = (bf16[384,768]{1,0:T(8,128)(2,1)S(1)}, bf16[384,768]{1,0:T(8,128)(2,1)S(1)}, u32[]{:S(2)}, u32[]{:S(2)}) collective-permute-start(bf16[384,768]{1,0:T(8,128)(2,1)S(1)} %collective-permute-done.3.refs_1_.refs_8_), channel_id=1, source_target_pairs={{0,2},{2,0},{4,6},{6,4},{1,3},{3,1},{5,7},{7,5},{8,10},{10,8},{12,... | collective-permute-start | bytes 1769480 | tf_op jit(solution)/shard_map/ppermute | solution.py:35
  18.2 1.1 %copy-start = (bf16[512,768]{1,0:T(8,128)(2,1)S(1)}, bf16[512,768]{1,0:T(8,128)(2,1)}, u32[]{:S(2)}) copy-start(bf16[512,768]{1,0:T(8,128)(2,1)} %refs_0_.21) | copy-start | bytes 2359300
  19.4 1.1 %copy-start.1 = (bf16[384,768]{1,0:T(8,128)(2,1)S(1)}, bf16[384,768]{1,0:T(8,128)(2,1)}, u32[]{:S(2)}) copy-start(bf16[384,768]{1,0:T(8,128)(2,1)} %refs_6_.1) | copy-start | bytes 1769476
  20.4 0.7 copy-start.3
  35.1 5.0 %collective-permute-start.9 = (bf16[384,768]{1,0:T(8,128)(2,1)S(1)}, bf16[384,768]{1,0:T(8,128)(2,1)S(1)}, u32[]{:S(2)}, u32[]{:S(2)}) collective-permute-start(bf16[384,768]{1,0:T(8,128)(2,1)S(1)} %get-tuple-element.42), channel_id=1, source_target_pairs={{0,2},{2,0},{4,6},{6,4},{1,3},{3,1},{5,7},{7,5},{8,10},{10,8},{12,... | collective-permute-start | bytes 1769480 | tf_op jit(solution)/shard_map/ppermute | solution.py:35
  35.7 39.9 %collective-permute-start.13 = (bf16[384,768]{1,0:T(8,128)(2,1)S(1)}, bf16[384,768]{1,0:T(8,128)(2,1)S(1)}, u32[]{:S(2)}, u32[]{:S(2)}) collective-permute-start(bf16[384,768]{1,0:T(8,128)(2,1)S(1)} %get-tuple-element.52), channel_id=1, source_target_pairs={{0,24},{8,16},{16,8},{24,0},{1,25},{9,17},{17,9},{25,1},{2,26},{10... | collective-permute-start | bytes 1769480 | tf_op jit(solution)/shard_map/ppermute | solution.py:35
  39.6 27.1 %copy-start.4 = (s32[512]{0:T(512)S(1)}, s32[512]{0:T(512)}, u32[]{:S(2)}) copy-start(s32[512]{0:T(512)} %param.7) | copy-start | bytes 6148
  39.6 36.0 %collective-permute-start.11 = (bf16[384,768]{1,0:T(8,128)(2,1)S(1)}, bf16[384,768]{1,0:T(8,128)(2,1)S(1)}, u32[]{:S(2)}, u32[]{:S(2)}) collective-permute-start(bf16[384,768]{1,0:T(8,128)(2,1)S(1)} %get-tuple-element.50), channel_id=1, source_target_pairs={{0,2},{2,0},{4,6},{6,4},{1,3},{3,1},{5,7},{7,5},{8,10},{10,8},{12,... | collective-permute-start | bytes 1769480 | tf_op jit(solution)/shard_map/ppermute | solution.py:35
  39.9 35.7 %collective-permute-start.12 = (bf16[384,768]{1,0:T(8,128)(2,1)S(1)}, bf16[384,768]{1,0:T(8,128)(2,1)S(1)}, u32[]{:S(2)}, u32[]{:S(2)}) collective-permute-start(bf16[384,768]{1,0:T(8,128)(2,1)S(1)} %get-tuple-element.51), channel_id=1, source_target_pairs={{0,8},{8,0},{16,24},{24,16},{1,9},{9,1},{17,25},{25,17},{2,10},{10... | collective-permute-start | bytes 1769480 | tf_op jit(solution)/shard_map/ppermute | solution.py:35
  40.6 31.2 %copy-start.2 = (bf16[384,768]{1,0:T(8,128)(2,1)S(1)}, bf16[384,768]{1,0:T(8,128)(2,1)}, u32[]{:S(2)}) copy-start(bf16[384,768]{1,0:T(8,128)(2,1)} %refs_6_.1) | copy-start | bytes 1769476
  40.6 35.0 %collective-permute-start.10 = (bf16[384,768]{1,0:T(8,128)(2,1)S(1)}, bf16[384,768]{1,0:T(8,128)(2,1)S(1)}, u32[]{:S(2)}, u32[]{:S(2)}) collective-permute-start(bf16[384,768]{1,0:T(8,128)(2,1)S(1)} %get-tuple-element.49), channel_id=1, source_target_pairs={{0,4},{2,6},{4,0},{6,2},{1,5},{3,7},{5,1},{7,3},{8,12},{10,14},{12... | collective-permute-start | bytes 1769480 | tf_op jit(solution)/shard_map/ppermute | solution.py:35
  41.2 1.2 %collective-permute-start.5 = (f32[8,128]{1,0:T(8,128)S(1)}, f32[8,128]{1,0:T(8,128)S(1)}, u32[]{:S(2)}, u32[]{:S(2)}) collective-permute-start(f32[8,128]{1,0:T(8,128)S(1)} %get-tuple-element.34), channel_id=1, source_target_pairs={{0,2},{2,0},{4,6},{6,4},{1,3},{3,1},{5,7},{7,5},{8,10},{10,8},{12,... | collective-permute-start | bytes 12296 | tf_op jit(solution)/shard_map/ppermute | solution.py:35
  42.3 13.8 %collective-permute-start.6 = (f32[8,128]{1,0:T(8,128)S(1)}, f32[8,128]{1,0:T(8,128)S(1)}, u32[]{:S(2)}, u32[]{:S(2)}) collective-permute-start(f32[8,128]{1,0:T(8,128)S(1)} %add.35), channel_id=1, source_target_pairs={{0,4},{2,6},{4,0},{6,2},{1,5},{3,7},{5,1},{7,3},{8,12},{10,14},{12... | collective-permute-start | bytes 12296 | tf_op jit(solution)/shard_map/ppermute | solution.py:35
  56.1 10.0 %collective-permute-start.7 = (f32[8,128]{1,0:T(8,128)S(1)}, f32[8,128]{1,0:T(8,128)S(1)}, u32[]{:S(2)}, u32[]{:S(2)}) collective-permute-start(f32[8,128]{1,0:T(8,128)S(1)} %add.36), channel_id=1, source_target_pairs={{0,8},{8,0},{16,24},{24,16},{1,9},{9,1},{17,25},{25,17},{2,10},{10... | collective-permute-start | bytes 12296 | tf_op jit(solution)/shard_map/ppermute | solution.py:35
  66.1 4.5 %collective-permute-start.8 = (f32[8,128]{1,0:T(8,128)S(1)}, f32[8,128]{1,0:T(8,128)S(1)}, u32[]{:S(2)}, u32[]{:S(2)}) collective-permute-start(f32[8,128]{1,0:T(8,128)S(1)} %add.37), channel_id=1, source_target_pairs={{0,16},{8,24},{16,0},{24,8},{1,17},{9,25},{17,1},{25,9},{2,18},{10... | collective-permute-start | bytes 12296 | tf_op jit(solution)/shard_map/ppermute | solution.py:35

commit v2 on v1

--- a/solution.py
+++ b/solution.py
@@ -8,31 +8,29 @@
 from jax.experimental.pallas import tpu as pltpu
 from jax.sharding import PartitionSpec as P
 
+
 BLK = 128
 LOWEST = -1e30
 LOG2E = math.log2(math.e)
 VMEM_LIMIT = 24 << 20
+CHUNKS = 4
 
 
 def whole():
     return pl.BlockSpec(memory_space=pltpu.VMEM)
 
 
-def call(kernel, name, outs, ins, flops, exps=0):
+def call(kernel, outs, ins, flops, exps=0, out_specs=None, scratch=()):
     moved = sum(a.size * a.dtype.itemsize for a in (*outs, *ins))
     return pl.pallas_call(
         kernel,
-        name=name,
         out_shape=tuple(outs),
         in_specs=[whole() for _ in ins],
-        out_specs=tuple(whole() for _ in outs),
+        out_specs=out_specs or tuple(whole() for _ in outs),
+        scratch_shapes=scratch,
         compiler_params=pltpu.CompilerParams(vmem_limit_bytes=VMEM_LIMIT),
         cost_estimate=pl.CostEstimate(flops=flops, bytes_accessed=moved, transcendentals=exps),
     )(*ins)
-
-
-def send(array, axis, pairs):
-    return lax.ppermute(array, axis, pairs)
 
 
 def block_stats(scores, block_at, scale):
@@ -145,6 +143,32 @@
     out_ref[...] = total * scale
 
 
+def gather_body(*refs):
+    total = refs[0][...]
+    for ref in refs[1:-1]:
+        total = total + ref[...].astype(jnp.float32)
+    refs[-1][...] = total
+
+
+def final_body(share, parts, base_ref, more_ref, *refs):
+    lost_refs = refs[:parts]
+    loss_ref, out_ref, held_ref, sem = refs[parts:]
+    chunk = held_ref.shape[0] // CHUNKS
+    copies = []
+    for at in range(CHUNKS):
+        rows = pl.ds(at * chunk, chunk)
+        held_ref[rows, :] = base_ref[rows, :] + more_ref[rows, :].astype(jnp.float32)
+        copy = pltpu.make_async_copy(held_ref.at[rows, :], out_ref.at[rows, :], sem.at[at])
+        copy.start()
+        copies.append(copy)
+    total = lost_refs[0][...]
+    for ref in lost_refs[1:]:
+        total = total + ref[...]
+    loss_ref[0] = jnp.max(total) * share
+    for copy in copies:
+        copy.wait()
+
+
 def row_plan(n_row, reach):
     plan = []
     if reach == 1 and n_row % 2 == 0:
@@ -161,18 +185,29 @@
     return plan
 
 
-def sum_over(array, axis):
+def sum_steps(array, axis):
     size = lax.axis_size(axis)
     if size & (size - 1):
         return lax.psum(array, axis)
     step = 1
     while step < size:
-        array = array + send(array, axis, [(i, i ^ step) for i in range(size)])
+        pairs = [(i, i ^ step) for i in range(size)]
+        array = array + lax.ppermute(array, axis, pairs)
         step *= 2
     return array
 
 
-def local(queries, passages, positive, block_mask, roster):
+def from_all(array, axis):
+    size = lax.axis_size(axis)
+    if size > 4:
+        return [sum_steps(array, axis)]
+    shifts = range(1, size)
+    return [array] + [
+        lax.ppermute(array, axis, [(i, (i + s) % size) for i in range(size)]) for s in shifts
+    ]
+
+
+def local_loss(queries, passages, positive, block_mask, roster):
     n_row = lax.axis_size("row")
     n_col = lax.axis_size("col")
     reach = min(2, (n_row - 1) // 2)
@@ -185,21 +220,23 @@
     f32, bf16 = jnp.float32, jnp.bfloat16
 
     rows = row_plan(n_row, reach)
-    near = [send(passages, "row", there) for there, _, _ in rows]
+    near = [lax.ppermute(passages, "row", there) for there, _, _ in rows]
 
     swap = [(i, i ^ 1) for i in range(n_col)]
     col_cells = []
     paired = n_col % 2 == 0
     if paired:
-        col_cells.append((send(passages, "col", swap), 1, n_col - 1))
+        col_cells.append((lax.ppermute(passages, "col", swap), 1, n_col - 1))
         for apart in range(1, n_col // 2):
-            far = send(passages, "col", [(i, (i + 2 * apart) % n_col) for i in range(n_col)])
-            cross = send(far, "col", swap)
+            there = [(i, (i + 2 * apart) % n_col) for i in range(n_col)]
+            far = lax.ppermute(passages, "col", there)
+            cross = lax.ppermute(far, "col", swap)
             col_cells.append((far, 2 * apart, 2 * apart))
             col_cells.append((cross, 2 * apart + 1, 2 * apart - 1))
     else:
         for stride in range(1, n_col):
-            far = send(passages, "col", [(i, (i + stride) % n_col) for i in range(n_col)])
+            there = [(i, (i + stride) % n_col) for i in range(n_col)]
+            far = lax.ppermute(passages, "col", there)
             col_cells.append((far, stride, stride))
 
     mask_t = block_mask.T
@@ -238,7 +275,6 @@
         ins = (queries, cell_rows[cell]) + ((pos,) if own else ())
         e, s = call(
             functools.partial(scores_body, scale, blocks, own),
-            f"scores_{cell}",
             (e_shape, s_shape),
             ins,
             dot_flops,
@@ -253,7 +289,6 @@
     loss_shape = jax.ShapeDtypeStruct((8, BLK), f32)
     e, factors, g_first, w_first, lost = call(
         functools.partial(last_body, scale, blocks, cells, first),
-        "last",
         (e_shape, f_shape, g_wire, w_shape, loss_shape),
         (queries, cell_rows[last], raised[first], vis, *stats),
         2 * dot_flops,
@@ -268,7 +303,6 @@
         ins += ((pos,) if own else ()) + (() if added is None else (added,))
         g, w = call(
             functools.partial(gradient_body, scale, blocks, cell, own, added is not None),
-            f"gradient_{cell}",
             (shape, w_shape),
             ins,
             dot_flops,
@@ -276,47 +310,55 @@
         weights[cell] = w
         return g
 
-    returned = []
+    near_back = []
     for at, (_, back, _) in enumerate(rows):
         g = g_first if at == 0 else gradient_of(first + at, g_wire)
-        returned.append(send(g, "row", back))
-
+        near_back.append(lax.ppermute(g, "row", back))
+
+    lost_col = sum_steps(lost, "col")
+    lost_parts = from_all(lost_col, "row")
+
+    col_back = []
     if paired:
         handed = []
         for apart in range(1, n_col // 2):
-            handed.append(send(gradient_of(1 + 2 * apart, g_wire), "col", swap))
+            g = gradient_of(1 + 2 * apart, g_wire)
+            handed.append(lax.ppermute(g, "col", swap))
         for apart in range(1, n_col // 2):
             g = gradient_of(2 * apart, g_wire, handed[apart - 1])
             back = [(i, (i - 2 * apart) % n_col) for i in range(n_col)]
-            returned.append(send(g, "col", back))
-        returned.append(send(gradient_of(1, g_wire), "col", swap))
+            col_back.append(lax.ppermute(g, "col", back))
+        col_back.append(lax.ppermute(gradient_of(1, g_wire), "col", swap))
     else:
         for stride in range(1, n_col):
             back = [(i, (i - stride) % n_col) for i in range(n_col)]
-            returned.append(send(gradient_of(stride, g_wire), "col", back))
+            g = gradient_of(stride, g_wire)
+            col_back.append(lax.ppermute(g, "col", back))
     g_own = gradient_of(0, g_wide)
 
     (toward,) = call(
         functools.partial(toward_body, scale, cells),
-        "toward",
         (jax.ShapeDtypeStruct((count, width), f32),),
         (*[weights[cell] for cell in range(cells)], *cell_rows),
         cells * dot_flops,
     )
 
-    loss_total = sum_over(sum_over(lost, "col"), "row")
-    loss = loss_total[0, :1] / (count * n_row * n_col)
-
-    near_count = len(rows)
-    grad_passages = g_own
-    for g in returned[near_count:] + returned[:near_count]:
-        grad_passages = grad_passages + g.astype(f32)
+    (base,) = call(gather_body, (g_wide,), (g_own, *col_back, *near_back[:-1]), 0)
+    share = 1.0 / (count * n_row * n_col)
+    loss, grad_passages = call(
+        functools.partial(final_body, share, len(lost_parts)),
+        (jax.ShapeDtypeStruct((1,), f32), g_wide),
+        (base, near_back[-1], *lost_parts),
+        0,
+        out_specs=(pl.BlockSpec(memory_space=pltpu.SMEM), pl.BlockSpec(memory_space=pl.ANY)),
+        scratch=(pltpu.VMEM((held, width), f32), pltpu.SemaphoreType.DMA((CHUNKS,))),
+    )
     return (loss, toward, grad_passages)
 
 
 def solution(mesh):
     return jax.shard_map(
-        local,
+        local_loss,
         mesh=mesh,
         in_specs=(
             P(("rep", "row", "col"), None),

time: 78.4 us -> 71.7 us (0.915)
  waiting for transfers between devices: 42.2 us -> 36.9 us
  Pallas kernels: 10.6 us -> 12.4 us
  between operations: 2.56 us -> 0.76 us
  other arithmetic: 3.71 us -> 2.38 us
    ppermute x14 -> x15, waiting for transfers between devices: 42.2 us -> 36.9 us  [the longest x2 11.1 us: sum_steps(): array = array + lax.ppermute(array, axis, pairs)]
    pallas_call x12 -> x14, Pallas kernels: 10.6 us -> 12.4 us  [call(): pl.pallas_call(kernel, out_shape=tuple(outs), in_specs=[whole() for _ in...]
    add x5 -> x2, other arithmetic: 1.34 us -> 0.01 us  [sum_steps(): array = array + lax.ppermute(array, axis, pairs)]
    ppermute x14 -> x15, starting transfers between devices: 15.5 us -> 15.9 us  [the longest x3 3.88 us: from_all(): lax.ppermute(array, axis, [(i, (i + s) % size) for i in range(size)])]
  transfers between devices with their start and end apart: 14 -> 15, of which waited for: 6 -> 6; matrix products, arithmetic and copies ran while one was open for 4% -> 4% of each run, Pallas kernels for 11% -> 13%
where the time goes in v2:
time: 71.7 us; the launch traced here: 71.3 us
  waiting for transfers between devices  36.9 us (51%)
  starting transfers between devices  15.9 us (22%)
  Pallas kernels  12.4 us (17%)
  local copies, waits for them, and re-layouts  3.02 us (4%)
  other arithmetic  2.38 us (3%)
  between operations  0.76 us (1%)
    pallas_call x14, Pallas kernels, call(): pl.pallas_call(kernel, out_shape=tuple(outs), in_specs=[whole() for _ in...  12.4 us
    ppermute x2, waiting for transfers between devices, sum_steps(): array = array + lax.ppermute(array, axis, pairs)  11.1 us
    ppermute x2, waiting for transfers between devices, local_loss(): near = [lax.ppermute(passages, 'row', there) for there, _, _ in rows]  10.9 us
    ppermute x1, waiting for transfers between devices, local_loss(): far = lax.ppermute(passages, 'col', there)  8.39 us
    ppermute x3, waiting for transfers between devices, from_all(): lax.ppermute(array, axis, [(i, (i + s) % size) for i in range(size)])  6.45 us
    ppermute x3, starting transfers between devices, from_all(): lax.ppermute(array, axis, [(i, (i + s) % size) for i in range(size)])  3.88 us
    ppermute x2, starting transfers between devices, local_loss(): near = [lax.ppermute(passages, 'row', there) for there, _, _ in rows]  3.6 us
    ppermute x1, starting transfers between devices, local_loss(): far = lax.ppermute(passages, 'col', there)  3.06 us
  transfers between devices with their start and end apart: 15, of which 6 were waited for; matrix products, arithmetic and copies ran while one was open for 4% of the time, Pallas kernels for 13%

profile of v2, /device:TPU:0, one launch (start us, length us, event | category | flops | bytes accessed | tf_op | source)
XLA Modules:
  0.0 71.3 jit_solution(9580763408290865650)
XLA Ops:
  0.6 3.1 %collective-permute-start.3 = (bf16[384,768]{1,0:T(8,128)(2,1)}, bf16[384,768]{1,0:T(8,128)(2,1)S(1)}, u32[]{:S(2)}, u32[]{:S(2)}) collective-permute-start(bf16[384,768]{1,0:T(8,128)(2,1)} %refs_6_.1), channel_id=1, source_target_pairs={{0,4},{2,6},{4,0},{6,2},{1,5},{3,7},{5,1},{7,3},{8,12},{10,14},{12... | collective-permute-start | bytes 1769480 | tf_op jit(solution)/shard_map/ppermute | solution.py:232
  3.7 3.6 %collective-permute-start = (bf16[384,768]{1,0:T(8,128)(2,1)}, bf16[384,768]{1,0:T(8,128)(2,1)S(1)}, u32[]{:S(2)}, u32[]{:S(2)}) collective-permute-start(bf16[384,768]{1,0:T(8,128)(2,1)} %refs_6_.1), channel_id=1, source_target_pairs={{0,24},{8,16},{16,8},{24,0},{1,25},{9,17},{17,9},{25,1},{2,26},{10... | collective-permute-start | bytes 1769480 | tf_op jit(solution)/shard_map/ppermute | solution.py:223
  7.3 0.0 collective-permute-start.1
  7.3 0.0 collective-permute-start.2
  7.3 0.7 add_select_fusion
  8.0 0.8 %select_convert_fusion = (f32[3,512]{1,0:T(4,128)S(1)}, pred[3,512]{1,0:T(4,128)(4,1)S(1)}, pred[3,512]{1,0:T(4,128)(4,1)S(1)}, f32[3,512]{1,0:T(4,128)S(1)}) fusion(pred[]{:T(512)S(6)} %eq.95, s32[9,512]{1,0:T(8,128)} %bitcast.8, s32[512]{0:T(512)S(1)} %add_select_fusion), kind=kLoop, calls=%fused_computation.12 | loop fusion | flops 12288 | bytes 35841 | tf_op jit(solution)/shard_map/convert_element_type | solution.py:249
  8.8 8.4 %collective-permute-done.3.refs_1_.refs_8_ = bf16[384,768]{1,0:T(8,128)(2,1)S(1)} collective-permute-done((bf16[384,768]{1,0:T(8,128)(2,1)}, bf16[384,768]{1,0:T(8,128)(2,1)S(1)}, u32[]{:S(2)}, u32[]{:S(2)}) %collective-permute-start.3) | collective-permute-done | bytes 589856 | tf_op jit(solution)/shard_map/ppermute | solution.py:232
  17.2 0.0 collective-permute-start.4
  17.2 0.8 %broadcast_select_fusion = (s32[1,512]{1,0:T(1,128)S(1)}, s32[1,512]{1,0:T(1,128)S(1)}, s32[1,512]{1,0:T(1,128)S(1)}) fusion(pred[]{:T(512)S(6)} %eq.82, s32[3,512]{1,0:T(4,128)} %bitcast.12), kind=kLoop, calls=%fused_computation.14 | loop fusion | flops 1024 | bytes 12289 | tf_op jit(solution)/shard_map/jit(_where)/select_n | solution.py:257
  18.1 0.1 concatenate.3.refs_3_
  18.2 0.0 copy-start
  18.2 1.1 %copy-done = bf16[512,768]{1,0:T(8,128)(2,1)S(1)} copy-done((bf16[512,768]{1,0:T(8,128)(2,1)S(1)}, bf16[512,768]{1,0:T(8,128)(2,1)}, u32[]{:S(2)}) %copy-start) | copy-done | bytes 786456
  19.4 0.0 copy-start.1
  19.4 1.1 %copy-done.1 = bf16[384,768]{1,0:T(8,128)(2,1)S(1)} copy-done((bf16[384,768]{1,0:T(8,128)(2,1)S(1)}, bf16[384,768]{1,0:T(8,128)(2,1)}, u32[]{:S(2)}) %copy-start.1) | copy-done | bytes 589848
  20.4 0.0 copy-start.3
  20.4 0.7 copy-done.3
  21.1 0.7 shard_map.76
  21.8 0.6 shard_map.79
  22.4 10.9 %collective-permute-done.1.refs_1_.refs_10_ = bf16[384,768]{1,0:T(8,128)(2,1)S(1)} collective-permute-done((bf16[384,768]{1,0:T(8,128)(2,1)}, bf16[384,768]{1,0:T(8,128)(2,1)S(1)}, u32[]{:S(2)}, u32[]{:S(2)}) %collective-permute-start.1) | collective-permute-done | bytes 589856 | tf_op jit(solution)/shard_map/ppermute | solution.py:223
  33.3 0.6 shard_map.77
  33.9 0.0 collective-permute-done.2.refs_1_.refs_7_
  34.0 0.6 shard_map.78
  34.6 0.0 collective-permute-done.4.refs_1_.refs_9_
  34.6 0.6 shard_map.80
  35.2 0.0 collective-permute-done.refs_1_.refs_11_
  35.2 1.2 %shard_map.81 = (f32[384,512]{1,0:T(8,128)S(1)}, f32[48,512]{1,0:T(8,128)S(1)}, bf16[384,768]{1,0:T(8,128)(2,1)S(1)}, bf16[384,512]{1,0:T(8,128)(2,1)S(1)}, f32[8,128]{1,0:T(8,128)S(1)}) custom-call(bf16[512,768]{1,0:T(8,128)(2,1)S(1)} %copy-done, bf16[384,768]{1,0:T(8,128)(2,1)S(1)} %collective-permute-done.refs_1_.refs_11_, ...), custom_call_target="tpu_custom_call" | custom-call | flops 603979776 | bytes 4214784 | tf_op jit(solution)/shard_map/pallas_call | solution.py:25
  36.4 0.5 shard_map.83
  36.9 0.1 collective-permute-start.5
  37.0 0.5 shard_map.85
  37.4 0.6 collective-permute-start.7
  38.0 1.7 %collective-permute-start.8 = (bf16[384,768]{1,0:T(8,128)(2,1)S(1)}, bf16[384,768]{1,0:T(8,128)(2,1)S(1)}, u32[]{:S(2)}, u32[]{:S(2)}) collective-permute-start(bf16[384,768]{1,0:T(8,128)(2,1)S(1)} %get-tuple-element.45), channel_id=1, source_target_pairs={{0,8},{8,0},{16,24},{24,16},{1,9},{9,1},{17,25},{25,17},{2,10},{10... | collective-permute-start | bytes 1769480 | tf_op jit(solution)/shard_map/ppermute | solution.py:316
  39.7 0.0 collective-permute-done.5.refs_3_
  39.7 0.5 shard_map.84
  40.2 0.0 copy-start.4
  40.2 0.6 collective-permute-start.6
  40.7 0.5 shard_map.87
  41.2 0.0 copy-start.2
  41.2 1.0 %collective-permute-start.9 = (bf16[384,768]{1,0:T(8,128)(2,1)S(1)}, bf16[384,768]{1,0:T(8,128)(2,1)S(1)}, u32[]{:S(2)}, u32[]{:S(2)}) collective-permute-start(bf16[384,768]{1,0:T(8,128)(2,1)S(1)} %get-tuple-element.47), channel_id=1, source_target_pairs={{0,24},{8,16},{16,8},{24,0},{1,25},{9,17},{17,9},{25,1},{2,26},{10... | collective-permute-start | bytes 1769480 | tf_op jit(solution)/shard_map/ppermute | solution.py:316
  42.2 0.0 collective-permute-start.10
  42.2 1.2 %collective-permute-done.10 = f32[8,128]{1,0:T(8,128)S(1)} collective-permute-done((f32[8,128]{1,0:T(8,128)S(1)}, f32[8,128]{1,0:T(8,128)S(1)}, u32[]{:S(2)}, u32[]{:S(2)}) %collective-permute-start.10) | collective-permute-done | bytes 4128 | tf_op jit(solution)/shard_map/ppermute | solution.py:195
  43.4 1.5 %collective-permute-start.11 = (f32[8,128]{1,0:T(8,128)S(1)}, f32[8,128]{1,0:T(8,128)S(1)}, u32[]{:S(2)}, u32[]{:S(2)}) collective-permute-start(f32[8,128]{1,0:T(8,128)S(1)} %add.17), channel_id=1, source_target_pairs={{0,4},{2,6},{4,0},{6,2},{1,5},{3,7},{5,1},{7,3},{8,12},{10,14},{12... | collective-permute-start | bytes 12296 | tf_op jit(solution)/shard_map/ppermute | solution.py:195
  44.9 0.0 copy-done.4
  44.9 0.5 shard_map.82
  45.4 9.9 %collective-permute-done.11 = f32[8,128]{1,0:T(8,128)S(1)} collective-permute-done((f32[8,128]{1,0:T(8,128)S(1)}, f32[8,128]{1,0:T(8,128)S(1)}, u32[]{:S(2)}, u32[]{:S(2)}) %collective-permute-start.11) | collective-permute-done | bytes 4128 | tf_op jit(solution)/shard_map/ppermute | solution.py:195
  55.4 1.3 %collective-permute-start.12 = (f32[8,128]{1,0:T(8,128)S(1)}, f32[8,128]{1,0:T(8,128)S(1)}, u32[]{:S(2)}, u32[]{:S(2)}) collective-permute-start(f32[8,128]{1,0:T(8,128)S(1)} %add.18.refs_0_), channel_id=1, source_target_pairs={{0,8},{8,16},{16,24},{24,0},{1,9},{9,17},{17,25},{25,1},{2,10},{10... | collective-permute-start | bytes 12296 | tf_op jit(solution)/shard_map/ppermute | solution.py:206
  56.6 0.0 collective-permute-done.7.refs_2_
  56.6 0.5 collective-permute-start.13
  57.2 0.0 collective-permute-done.8.refs_3_
  57.2 2.1 %collective-permute-start.14 = (f32[8,128]{1,0:T(8,128)S(1)}, f32[8,128]{1,0:T(8,128)S(1)}, u32[]{:S(2)}, u32[]{:S(2)}) collective-permute-start(f32[8,128]{1,0:T(8,128)S(1)} %add.18.refs_0_), channel_id=1, source_target_pairs={{0,24},{8,0},{16,8},{24,16},{1,25},{9,1},{17,9},{25,17},{2,26},{10... | collective-permute-start | bytes 12296 | tf_op jit(solution)/shard_map/ppermute | solution.py:206
  59.2 0.0 copy-done.2
  59.2 3.8 %shard_map.89 = f32[512,768]{1,0:T(8,128)} custom-call(bf16[384,512]{1,0:T(8,128)(2,1)S(1)} %get-tuple-element.50.refs_0_, bf16[384,512]{1,0:T(8,128)(2,1)S(1)} %get-tuple-element.51.refs_1_, bf16[384,512]{1,0:T(8,128)(2,1)S(1)} %get-tuple-element.52.refs_2_, bf16[384,512]{1,0:T(8,128)(2,1)S(1)} %get-tuple-element.53.refs_3_, ...), custom_call_target="tpu_custom_call" | custom-call | flops 1811939328 | bytes 7471104 | tf_op jit(solution)/shard_map/pallas_call | solution.py:25
  63.0 0.0 collective-permute-done.6.refs_1_
  63.0 0.2 shard_map.86.base_ref
  63.3 3.0 %collective-permute-done.12.refs_1_ = f32[8,128]{1,0:T(8,128)S(1)} collective-permute-done((f32[8,128]{1,0:T(8,128)S(1)}, f32[8,128]{1,0:T(8,128)S(1)}, u32[]{:S(2)}, u32[]{:S(2)}) %collective-permute-start.12) | collective-permute-done | bytes 4128 | tf_op jit(solution)/shard_map/ppermute | solution.py:206
  66.2 3.5 %collective-permute-done.13.refs_2_ = f32[8,128]{1,0:T(8,128)S(1)} collective-permute-done((f32[8,128]{1,0:T(8,128)S(1)}, f32[8,128]{1,0:T(8,128)S(1)}, u32[]{:S(2)}, u32[]{:S(2)}) %collective-permute-start.13) | collective-permute-done | bytes 4128 | tf_op jit(solution)/shard_map/ppermute | solution.py:206
  69.7 0.0 collective-permute-done.14.refs_3_
  69.7 0.0 collective-permute-done.9.more_ref
  69.7 1.6 %shard_map.88 = (f32[1]{0:T(128)}, f32[384,768]{1,0:T(8,128)}) custom-call(f32[384,768]{1,0:T(8,128)S(1)} %shard_map.86.base_ref, bf16[384,768]{1,0:T(8,128)(2,1)S(1)} %collective-permute-done.9.more_ref, f32[8,128]{1,0:T(8,128)S(1)} %add.18.refs_0_, f32[8,128]{1,0:T(8,128)S(1)} %collective-permute-done.12.refs_1_, ...), custom_call_target="tpu_custom_call" | custom-call | bytes 2965508 | tf_op jit(solution)/shard_map/pallas_call | solution.py:25
  (5 shorter events, 0.0 us)
Async XLA Ops:
  0.6 16.6 %collective-permute-start.3 = (bf16[384,768]{1,0:T(8,128)(2,1)}, bf16[384,768]{1,0:T(8,128)(2,1)S(1)}, u32[]{:S(2)}, u32[]{:S(2)}) collective-permute-start(bf16[384,768]{1,0:T(8,128)(2,1)} %refs_6_.1), channel_id=1, source_target_pairs={{0,4},{2,6},{4,0},{6,2},{1,5},{3,7},{5,1},{7,3},{8,12},{10,14},{12... | collective-permute-start | bytes 1769480 | tf_op jit(solution)/shard_map/ppermute | solution.py:232
  3.7 31.5 %collective-permute-start = (bf16[384,768]{1,0:T(8,128)(2,1)}, bf16[384,768]{1,0:T(8,128)(2,1)S(1)}, u32[]{:S(2)}, u32[]{:S(2)}) collective-permute-start(bf16[384,768]{1,0:T(8,128)(2,1)} %refs_6_.1), channel_id=1, source_target_pairs={{0,24},{8,16},{16,8},{24,0},{1,25},{9,17},{17,9},{25,1},{2,26},{10... | collective-permute-start | bytes 1769480 | tf_op jit(solution)/shard_map/ppermute | solution.py:223
  7.3 26.0 %collective-permute-start.1 = (bf16[384,768]{1,0:T(8,128)(2,1)}, bf16[384,768]{1,0:T(8,128)(2,1)S(1)}, u32[]{:S(2)}, u32[]{:S(2)}) collective-permute-start(bf16[384,768]{1,0:T(8,128)(2,1)} %refs_6_.1), channel_id=1, source_target_pairs={{0,8},{8,0},{16,24},{24,16},{1,9},{9,1},{17,25},{25,17},{2,10},{10... | collective-permute-start | bytes 1769480 | tf_op jit(solution)/shard_map/ppermute | solution.py:223
  7.3 26.7 %collective-permute-start.2 = (bf16[384,768]{1,0:T(8,128)(2,1)}, bf16[384,768]{1,0:T(8,128)(2,1)S(1)}, u32[]{:S(2)}, u32[]{:S(2)}) collective-permute-start(bf16[384,768]{1,0:T(8,128)(2,1)} %refs_6_.1), channel_id=1, source_target_pairs={{0,2},{2,0},{4,6},{6,4},{1,3},{3,1},{5,7},{7,5},{8,10},{10,8},{12,... | collective-permute-start | bytes 1769480 | tf_op jit(solution)/shard_map/ppermute | solution.py:229
  17.2 17.3 %collective-permute-start.4 = (bf16[384,768]{1,0:T(8,128)(2,1)S(1)}, bf16[384,768]{1,0:T(8,128)(2,1)S(1)}, u32[]{:S(2)}, u32[]{:S(2)}) collective-permute-start(bf16[384,768]{1,0:T(8,128)(2,1)S(1)} %collective-permute-done.3.refs_1_.refs_8_), channel_id=1, source_target_pairs={{0,2},{2,0},{4,6},{6,4},{1,3},{3,1},{5,7},{7,5},{8,10},{10,8},{12,... | collective-permute-start | bytes 1769480 | tf_op jit(solution)/shard_map/ppermute | solution.py:233
  18.2 1.1 %copy-start = (bf16[512,768]{1,0:T(8,128)(2,1)S(1)}, bf16[512,768]{1,0:T(8,128)(2,1)}, u32[]{:S(2)}) copy-start(bf16[512,768]{1,0:T(8,128)(2,1)} %refs_0_.21) | copy-start | bytes 2359300
  19.4 1.1 %copy-start.1 = (bf16[384,768]{1,0:T(8,128)(2,1)S(1)}, bf16[384,768]{1,0:T(8,128)(2,1)}, u32[]{:S(2)}) copy-start(bf16[384,768]{1,0:T(8,128)(2,1)} %refs_6_.1) | copy-start | bytes 1769476
  20.4 0.7 copy-start.3
  36.9 2.8 %collective-permute-start.5 = (bf16[384,768]{1,0:T(8,128)(2,1)S(1)}, bf16[384,768]{1,0:T(8,128)(2,1)S(1)}, u32[]{:S(2)}, u32[]{:S(2)}) collective-permute-start(bf16[384,768]{1,0:T(8,128)(2,1)S(1)} %get-tuple-element.41), channel_id=1, source_target_pairs={{0,2},{2,0},{4,6},{6,4},{1,3},{3,1},{5,7},{7,5},{8,10},{10,8},{12,... | collective-permute-start | bytes 1769480 | tf_op jit(solution)/shard_map/ppermute | solution.py:326
  37.4 19.2 %collective-permute-start.7 = (bf16[384,768]{1,0:T(8,128)(2,1)S(1)}, bf16[384,768]{1,0:T(8,128)(2,1)S(1)}, u32[]{:S(2)}, u32[]{:S(2)}) collective-permute-start(bf16[384,768]{1,0:T(8,128)(2,1)S(1)} %get-tuple-element.44), channel_id=1, source_target_pairs={{0,2},{2,0},{4,6},{6,4},{1,3},{3,1},{5,7},{7,5},{8,10},{10,8},{12,... | collective-permute-start | bytes 1769480 | tf_op jit(solution)/shard_map/ppermute | solution.py:331
  38.0 19.2 %collective-permute-start.8 = (bf16[384,768]{1,0:T(8,128)(2,1)S(1)}, bf16[384,768]{1,0:T(8,128)(2,1)S(1)}, u32[]{:S(2)}, u32[]{:S(2)}) collective-permute-start(bf16[384,768]{1,0:T(8,128)(2,1)S(1)} %get-tuple-element.45), channel_id=1, source_target_pairs={{0,8},{8,0},{16,24},{24,16},{1,9},{9,1},{17,25},{25,17},{2,10},{10... | collective-permute-start | bytes 1769480 | tf_op jit(solution)/shard_map/ppermute | solution.py:316
  40.2 4.7 %copy-start.4 = (s32[512]{0:T(512)S(1)}, s32[512]{0:T(512)}, u32[]{:S(2)}) copy-start(s32[512]{0:T(512)} %param.7) | copy-start | bytes 6148
  40.2 22.9 %collective-permute-start.6 = (bf16[384,768]{1,0:T(8,128)(2,1)S(1)}, bf16[384,768]{1,0:T(8,128)(2,1)S(1)}, u32[]{:S(2)}, u32[]{:S(2)}) collective-permute-start(bf16[384,768]{1,0:T(8,128)(2,1)S(1)} %get-tuple-element.42), channel_id=1, source_target_pairs={{0,4},{2,6},{4,0},{6,2},{1,5},{3,7},{5,1},{7,3},{8,12},{10,14},{12... | collective-permute-start | bytes 1769480 | tf_op jit(solution)/shard_map/ppermute | solution.py:330
  41.2 18.0 %copy-start.2 = (bf16[384,768]{1,0:T(8,128)(2,1)S(1)}, bf16[384,768]{1,0:T(8,128)(2,1)}, u32[]{:S(2)}) copy-start(bf16[384,768]{1,0:T(8,128)(2,1)} %refs_6_.1) | copy-start | bytes 1769476
  41.2 28.5 %collective-permute-start.9 = (bf16[384,768]{1,0:T(8,128)(2,1)S(1)}, bf16[384,768]{1,0:T(8,128)(2,1)S(1)}, u32[]{:S(2)}, u32[]{:S(2)}) collective-permute-start(bf16[384,768]{1,0:T(8,128)(2,1)S(1)} %get-tuple-element.47), channel_id=1, source_target_pairs={{0,24},{8,16},{16,8},{24,0},{1,25},{9,17},{17,9},{25,1},{2,26},{10... | collective-permute-start | bytes 1769480 | tf_op jit(solution)/shard_map/ppermute | solution.py:316
  42.2 1.2 %collective-permute-start.10 = (f32[8,128]{1,0:T(8,128)S(1)}, f32[8,128]{1,0:T(8,128)S(1)}, u32[]{:S(2)}, u32[]{:S(2)}) collective-permute-start(f32[8,128]{1,0:T(8,128)S(1)} %get-tuple-element.48), channel_id=1, source_target_pairs={{0,2},{2,0},{4,6},{6,4},{1,3},{3,1},{5,7},{7,5},{8,10},{10,8},{12,... | collective-permute-start | bytes 12296 | tf_op jit(solution)/shard_map/ppermute | solution.py:195
  43.4 12.0 %collective-permute-start.11 = (f32[8,128]{1,0:T(8,128)S(1)}, f32[8,128]{1,0:T(8,128)S(1)}, u32[]{:S(2)}, u32[]{:S(2)}) collective-permute-start(f32[8,128]{1,0:T(8,128)S(1)} %add.17), channel_id=1, source_target_pairs={{0,4},{2,6},{4,0},{6,2},{1,5},{3,7},{5,1},{7,3},{8,12},{10,14},{12... | collective-permute-start | bytes 12296 | tf_op jit(solution)/shard_map/ppermute | solution.py:195
  55.4 10.9 %collective-permute-start.12 = (f32[8,128]{1,0:T(8,128)S(1)}, f32[8,128]{1,0:T(8,128)S(1)}, u32[]{:S(2)}, u32[]{:S(2)}) collective-permute-start(f32[8,128]{1,0:T(8,128)S(1)} %add.18.refs_0_), channel_id=1, source_target_pairs={{0,8},{8,16},{16,24},{24,0},{1,9},{9,17},{17,25},{25,1},{2,10},{10... | collective-permute-start | bytes 12296 | tf_op jit(solution)/shard_map/ppermute | solution.py:206
  56.6 13.1 %collective-permute-start.13 = (f32[8,128]{1,0:T(8,128)S(1)}, f32[8,128]{1,0:T(8,128)S(1)}, u32[]{:S(2)}, u32[]{:S(2)}) collective-permute-start(f32[8,128]{1,0:T(8,128)S(1)} %add.18.refs_0_), channel_id=1, source_target_pairs={{0,16},{8,24},{16,0},{24,8},{1,17},{9,25},{17,1},{25,9},{2,18},{10... | collective-permute-start | bytes 12296 | tf_op jit(solution)/shard_map/ppermute | solution.py:206
  57.2 12.6 %collective-permute-start.14 = (f32[8,128]{1,0:T(8,128)S(1)}, f32[8,128]{1,0:T(8,128)S(1)}, u32[]{:S(2)}, u32[]{:S(2)}) collective-permute-start(f32[8,128]{1,0:T(8,128)S(1)} %add.18.refs_0_), channel_id=1, source_target_pairs={{0,24},{8,0},{16,8},{24,16},{1,25},{9,1},{17,9},{25,17},{2,26},{10... | collective-permute-start | bytes 12296 | tf_op jit(solution)/shard_map/ppermute | solution.py:206

commit v3 on v2

--- a/solution.py
+++ b/solution.py
@@ -20,14 +20,17 @@
     return pl.BlockSpec(memory_space=pltpu.VMEM)
 
 
-def call(kernel, outs, ins, flops, exps=0, out_specs=None, scratch=()):
+def call(kernel, outs, ins, flops, exps=0, out_specs=None, scratch=(), alias=None):
     moved = sum(a.size * a.dtype.itemsize for a in (*outs, *ins))
     return pl.pallas_call(
         kernel,
         out_shape=tuple(outs),
-        in_specs=[whole() for _ in ins],
+        in_specs=[
+            pl.BlockSpec(memory_space=pl.ANY) if at == alias else whole() for at in range(len(ins))
+        ],
         out_specs=out_specs or tuple(whole() for _ in outs),
         scratch_shapes=scratch,
+        input_output_aliases={} if alias is None else {alias: len(outs) - 1},
         compiler_params=pltpu.CompilerParams(vmem_limit_bytes=VMEM_LIMIT),
         cost_estimate=pl.CostEstimate(flops=flops, bytes_accessed=moved, transcendentals=exps),
     )(*ins)
@@ -81,7 +84,7 @@
 def last_body(scale, blocks, cells, first, *refs):
     q_ref, p_ref, e_first_ref, vis_ref = refs[:4]
     stats_refs = refs[4 : 4 + cells - 1]
-    e_ref, f_ref, g_ref, w_ref, loss_ref = refs[4 + cells - 1 :]
+    e_ref, f_ref, head_ref, tail_ref, w_ref, loss_ref = refs[4 + cells - 1 :]
     scores = scores_of(q_ref, p_ref)
     tops, sums = [], []
     for block_at in range(blocks):
@@ -113,8 +116,22 @@
     loss_ref[...] = jnp.broadcast_to(lost, loss_ref.shape)
     weights = weights_of(e_first_ref, factors[first], blocks, None)
     w_ref[...] = weights
-    gradient = jnp.dot(weights, q_ref[...], preferred_element_type=jnp.float32) * scale
-    g_ref[...] = gradient.astype(g_ref.dtype)
+    put_pieces((head_ref, tail_ref), weights, q_ref, scale)
+
+
+def put_pieces(pieces, weights, q_ref, scale):
+    at = 0
+    for ref in pieces:
+        part = weights[at : at + ref.shape[0]]
+        gradient = jnp.dot(part, q_ref[...], preferred_element_type=jnp.float32) * scale
+        ref[...] = gradient.astype(ref.dtype)
+        at += ref.shape[0]
+
+
+def pieces_body(scale, blocks, cell, q_ref, e_ref, f_ref, head_ref, tail_ref, w_ref):
+    weights = weights_of(e_ref, f_ref[cell * 8 : cell * 8 + 8, :], blocks, None)
+    w_ref[...] = weights
+    put_pieces((head_ref, tail_ref), weights, q_ref, scale)
 
 
 def gradient_body(scale, blocks, cell, own, added, *refs):
@@ -143,22 +160,43 @@
     out_ref[...] = total * scale
 
 
-def gather_body(*refs):
-    total = refs[0][...]
-    for ref in refs[1:-1]:
-        total = total + ref[...].astype(jnp.float32)
-    refs[-1][...] = total
-
-
-def final_body(share, parts, base_ref, more_ref, *refs):
-    lost_refs = refs[:parts]
-    loss_ref, out_ref, held_ref, sem = refs[parts:]
+def gather_body(wholes, *refs):
+    out_ref, rest_ref, held_ref, sem = refs[-4:]
+    heads = refs[wholes:-4]
     chunk = held_ref.shape[0] // CHUNKS
     copies = []
     for at in range(CHUNKS):
         rows = pl.ds(at * chunk, chunk)
-        held_ref[rows, :] = base_ref[rows, :] + more_ref[rows, :].astype(jnp.float32)
+        total = refs[0][rows, :]
+        for ref in (*refs[1:wholes], *heads):
+            total = total + ref[rows, :].astype(jnp.float32)
+        held_ref[rows, :] = total
         copy = pltpu.make_async_copy(held_ref.at[rows, :], out_ref.at[rows, :], sem.at[at])
+        copy.start()
+        copies.append(copy)
+    rows = pl.ds(held_ref.shape[0], rest_ref.shape[0])
+    total = refs[0][rows, :]
+    for ref in refs[1:wholes]:
+        total = total + ref[rows, :].astype(jnp.float32)
+    rest_ref[...] = total
+    for copy in copies:
+        copy.wait()
+
+
+def final_body(share, tails, parts, rest_ref, *refs):
+    tail_refs, lost_refs = refs[:tails], refs[tails : tails + parts]
+    loss_ref, out_ref, held_ref, sem = refs[tails + parts + 1 :]
+    first = out_ref.shape[0] - held_ref.shape[0]
+    chunk = held_ref.shape[0] // CHUNKS
+    copies = []
+    for at in range(CHUNKS):
+        rows = pl.ds(at * chunk, chunk)
+        total = rest_ref[rows, :]
+        for ref in tail_refs:
+            total = total + ref[rows, :].astype(jnp.float32)
+        held_ref[rows, :] = total
+        there = out_ref.at[pl.ds(first + at * chunk, chunk), :]
+        copy = pltpu.make_async_copy(held_ref.at[rows, :], there, sem.at[at])
         copy.start()
         copies.append(copy)
     total = lost_refs[0][...]
@@ -287,9 +325,13 @@
     last = cells - 1
     f_shape = jax.ShapeDtypeStruct((8 * cells, count), f32)
     loss_shape = jax.ShapeDtypeStruct((8, BLK), f32)
-    e, factors, g_first, w_first, lost = call(
+    tail = BLK if blocks > 1 else 0
+    assert tail
+    head_shape = jax.ShapeDtypeStruct((held - tail, width), bf16)
+    tail_shape = jax.ShapeDtypeStruct((tail, width), bf16)
+    e, factors, g_head, g_tail, w_first, lost = call(
         functools.partial(last_body, scale, blocks, cells, first),
-        (e_shape, f_shape, g_wire, w_shape, loss_shape),
+        (e_shape, f_shape, head_shape, tail_shape, w_shape, loss_shape),
         (queries, cell_rows[last], raised[first], vis, *stats),
         2 * dot_flops,
         held * count,
@@ -310,10 +352,19 @@
         weights[cell] = w
         return g
 
-    near_back = []
+    heads, tails = [(g_head, g_tail)], []
+    for at in range(1, len(rows)):
+        cell = first + at
+        g_head, g_tail, weights[cell] = call(
+            functools.partial(pieces_body, scale, blocks, cell),
+            (head_shape, tail_shape, w_shape),
+            (queries, raised[cell], factors),
+            dot_flops,
+        )
+        heads.append((g_head, g_tail))
     for at, (_, back, _) in enumerate(rows):
-        g = g_first if at == 0 else gradient_of(first + at, g_wire)
-        near_back.append(lax.ppermute(g, "row", back))
+        tails.append(lax.ppermute(heads[at][1], "row", back))
+        heads[at] = lax.ppermute(heads[at][0], "row", back)
 
     lost_col = sum_steps(lost, "col")
     lost_parts = from_all(lost_col, "row")
@@ -343,15 +394,27 @@
         cells * dot_flops,
     )
 
-    (base,) = call(gather_body, (g_wide,), (g_own, *col_back, *near_back[:-1]), 0)
+    wides = (g_own, *col_back)
+    wire_sems = pltpu.SemaphoreType.DMA((CHUNKS,))
+    rest_shape = jax.ShapeDtypeStruct((tail, width), f32)
+    out_spec = pl.BlockSpec(memory_space=pl.ANY)
+    written, rest = call(
+        functools.partial(gather_body, len(wides)),
+        (g_wide, rest_shape),
+        (*wides, *heads),
+        0,
+        out_specs=(out_spec, whole()),
+        scratch=(pltpu.VMEM((held - tail, width), f32), wire_sems),
+    )
     share = 1.0 / (count * n_row * n_col)
     loss, grad_passages = call(
-        functools.partial(final_body, share, len(lost_parts)),
+        functools.partial(final_body, share, len(tails), len(lost_parts)),
         (jax.ShapeDtypeStruct((1,), f32), g_wide),
-        (base, near_back[-1], *lost_parts),
+        (rest, *tails, *lost_parts, written),
         0,
-        out_specs=(pl.BlockSpec(memory_space=pltpu.SMEM), pl.BlockSpec(memory_space=pl.ANY)),
-        scratch=(pltpu.VMEM((held, width), f32), pltpu.SemaphoreType.DMA((CHUNKS,))),
+        out_specs=(pl.BlockSpec(memory_space=pltpu.SMEM), out_spec),
+        scratch=(pltpu.VMEM((tail, width), f32), wire_sems),
+        alias=1 + len(tails) + len(lost_parts),
     )
     return (loss, toward, grad_passages)
 

time: 71.7 us -> 73.7 us (1.028)
  starting transfers between devices: 15.9 us -> 25.8 us
  waiting for transfers between devices: 36.9 us -> 28.5 us
    ppermute x2 -> x4, starting transfers between devices: 2.62 us -> 12.1 us  [the longest x2 8.45 us: local_loss(): tails.append(lax.ppermute(heads[at][1], 'row', back))]
    ppermute x3, waiting for transfers between devices: 6.45 us -> 0.01 us  [from_all(): lax.ppermute(array, axis, [(i, (i + s) % size) for i in range(size)])]
    ppermute x2, waiting for transfers between devices: 11.1 us -> 9.3 us  [sum_steps(): array = array + lax.ppermute(array, axis, pairs)]
    ppermute x2, waiting for transfers between devices: 10.9 us -> 9.16 us  [local_loss(): near = [lax.ppermute(passages, 'row', there) for there, _, _ in rows]]
    ppermute x2 -> x4, waiting for transfers between devices: 0.01 us -> 1.13 us  [the longest x2 1.12 us: local_loss(): heads[at] = lax.ppermute(heads[at][0], 'row', back)]
    ppermute x1, waiting for transfers between devices: 0.01 us -> 0.94 us  [local_loss(): handed.append(lax.ppermute(g, 'col', swap))]
  transfers between devices with their start and end apart: 15 -> 17, of which waited for: 6 -> 6; matrix products, arithmetic and copies ran while one was open for 4% -> 3% of each run, Pallas kernels for 13% -> 13%
where the time goes in v3:
time: 73.7 us; the launch traced here: 73.3 us
  waiting for transfers between devices  28.5 us (39%)
  starting transfers between devices  25.8 us (35%)
  Pallas kernels  12.8 us (17%)
  local copies, waits for them, and re-layouts  3.02 us (4%)
  other arithmetic  2.38 us (3%)
  between operations  0.81 us (1%)
    pallas_call x14, Pallas kernels, call(): pl.pallas_call(kernel, out_shape=tuple(outs), in_specs=[pl.BlockSpec(memo...  12.8 us
    ppermute x2, waiting for transfers between devices, sum_steps(): array = array + lax.ppermute(array, axis, pairs)  9.3 us
    ppermute x2, waiting for transfers between devices, local_loss(): near = [lax.ppermute(passages, 'row', there) for there, _, _ in rows]  9.16 us
    ppermute x2, starting transfers between devices, local_loss(): tails.append(lax.ppermute(heads[at][1], 'row', back))  8.45 us
    ppermute x1, waiting for transfers between devices, local_loss(): far = lax.ppermute(passages, 'col', there)  7.94 us
    ppermute x2, starting transfers between devices, local_loss(): near = [lax.ppermute(passages, 'row', there) for there, _, _ in rows]  4.05 us
    ppermute x3, starting transfers between devices, from_all(): lax.ppermute(array, axis, [(i, (i + s) % size) for i in range(size)])  3.88 us
    ppermute x2, starting transfers between devices, local_loss(): heads[at] = lax.ppermute(heads[at][0], 'row', back)  3.62 us
  transfers between devices with their start and end apart: 17, of which 6 were waited for; matrix products, arithmetic and copies ran while one was open for 3% of the time, Pallas kernels for 13%

profile of v3, /device:TPU:0, one launch (start us, length us, event | category | flops | bytes accessed | tf_op | source)
XLA Modules:
  0.0 73.3 jit_solution(5622699862345118748)
XLA Ops:
  0.6 3.1 %collective-permute-start.3 = (bf16[384,768]{1,0:T(8,128)(2,1)}, bf16[384,768]{1,0:T(8,128)(2,1)S(1)}, u32[]{:S(2)}, u32[]{:S(2)}) collective-permute-start(bf16[384,768]{1,0:T(8,128)(2,1)} %refs_6_.1), channel_id=1, source_target_pairs={{0,4},{2,6},{4,0},{6,2},{1,5},{3,7},{5,1},{7,3},{8,12},{10,14},{12... | collective-permute-start | bytes 1769480 | tf_op jit(solution)/shard_map/ppermute | solution.py:270
  3.7 1.6 %collective-permute-start.1 = (bf16[384,768]{1,0:T(8,128)(2,1)}, bf16[384,768]{1,0:T(8,128)(2,1)S(1)}, u32[]{:S(2)}, u32[]{:S(2)}) collective-permute-start(bf16[384,768]{1,0:T(8,128)(2,1)} %refs_6_.1), channel_id=1, source_target_pairs={{0,8},{8,0},{16,24},{24,16},{1,9},{9,1},{17,25},{25,17},{2,10},{10... | collective-permute-start | bytes 1769480 | tf_op jit(solution)/shard_map/ppermute | solution.py:261
  5.3 0.0 collective-permute-start.2
  5.3 2.5 %collective-permute-start = (bf16[384,768]{1,0:T(8,128)(2,1)}, bf16[384,768]{1,0:T(8,128)(2,1)S(1)}, u32[]{:S(2)}, u32[]{:S(2)}) collective-permute-start(bf16[384,768]{1,0:T(8,128)(2,1)} %refs_6_.1), channel_id=1, source_target_pairs={{0,24},{8,16},{16,8},{24,0},{1,25},{9,17},{17,9},{25,1},{2,26},{10... | collective-permute-start | bytes 1769480 | tf_op jit(solution)/shard_map/ppermute | solution.py:261
  7.7 0.7 add_select_fusion
  8.4 0.8 %select_convert_fusion = (f32[3,512]{1,0:T(4,128)S(1)}, pred[3,512]{1,0:T(4,128)(4,1)S(1)}, pred[3,512]{1,0:T(4,128)(4,1)S(1)}, f32[3,512]{1,0:T(4,128)S(1)}) fusion(pred[]{:T(512)S(6)} %eq.95, s32[9,512]{1,0:T(8,128)} %bitcast.8, s32[512]{0:T(512)S(1)} %add_select_fusion), kind=kLoop, calls=%fused_computation.12 | loop fusion | flops 12288 | bytes 35841 | tf_op jit(solution)/shard_map/convert_element_type | solution.py:287
  9.3 7.9 %collective-permute-done.3.refs_1_.refs_8_ = bf16[384,768]{1,0:T(8,128)(2,1)S(1)} collective-permute-done((bf16[384,768]{1,0:T(8,128)(2,1)}, bf16[384,768]{1,0:T(8,128)(2,1)S(1)}, u32[]{:S(2)}, u32[]{:S(2)}) %collective-permute-start.3) | collective-permute-done | bytes 589856 | tf_op jit(solution)/shard_map/ppermute | solution.py:270
  17.2 0.0 collective-permute-start.4
  17.2 0.8 %broadcast_select_fusion = (s32[1,512]{1,0:T(1,128)S(1)}, s32[1,512]{1,0:T(1,128)S(1)}, s32[1,512]{1,0:T(1,128)S(1)}) fusion(pred[]{:T(512)S(6)} %eq.82, s32[3,512]{1,0:T(4,128)} %bitcast.12), kind=kLoop, calls=%fused_computation.14 | loop fusion | flops 1024 | bytes 12289 | tf_op jit(solution)/shard_map/jit(_where)/select_n | solution.py:295
  18.1 0.1 concatenate.3.refs_3_
  18.2 0.0 copy-start
  18.2 1.1 %copy-done = bf16[512,768]{1,0:T(8,128)(2,1)S(1)} copy-done((bf16[512,768]{1,0:T(8,128)(2,1)S(1)}, bf16[512,768]{1,0:T(8,128)(2,1)}, u32[]{:S(2)}) %copy-start) | copy-done | bytes 786456
  19.4 0.0 copy-start.1
  19.4 1.1 %copy-done.1 = bf16[384,768]{1,0:T(8,128)(2,1)S(1)} copy-done((bf16[384,768]{1,0:T(8,128)(2,1)S(1)}, bf16[384,768]{1,0:T(8,128)(2,1)}, u32[]{:S(2)}) %copy-start.1) | copy-done | bytes 589848
  20.4 0.0 copy-start.3
  20.4 0.7 copy-done.3
  21.1 0.7 shard_map.76
  21.8 0.6 shard_map.79
  22.4 0.0 collective-permute-done.1.refs_1_.refs_10_
  22.4 0.6 shard_map.77
  23.0 0.0 collective-permute-done.2.refs_1_.refs_7_
  23.0 0.6 shard_map.78
  23.7 0.0 collective-permute-done.4.refs_1_.refs_9_
  23.7 0.6 shard_map.80
  24.3 9.2 %collective-permute-done.refs_1_.refs_11_ = bf16[384,768]{1,0:T(8,128)(2,1)S(1)} collective-permute-done((bf16[384,768]{1,0:T(8,128)(2,1)}, bf16[384,768]{1,0:T(8,128)(2,1)S(1)}, u32[]{:S(2)}, u32[]{:S(2)}) %collective-permute-start) | collective-permute-done | bytes 589856 | tf_op jit(solution)/shard_map/ppermute | solution.py:261
  33.5 1.1 %shard_map.81 = (f32[384,512]{1,0:T(8,128)S(1)}, f32[48,512]{1,0:T(8,128)S(1)}, bf16[256,768]{1,0:T(8,128)(2,1)S(1)}, bf16[128,768]{1,0:T(8,128)(2,1)S(1)}, bf16...) custom-call(bf16[512,768]{1,0:T(8,128)(2,1)S(1)} %copy-done, bf16[384,768]{1,0:T(8,128)(2,1)S(1)} %collective-permute-done.refs_1_.refs_11_, ...), custom_call_target="tpu_custom_call" | custom-call | flops 603979776 | bytes 4214784 | tf_op jit(solution)/shard_map/pallas_call | solution.py:25
  34.6 0.5 shard_map.83
  35.1 0.1 collective-permute-start.5
  35.2 0.5 shard_map.85
  35.7 0.6 collective-permute-start.7
  36.2 0.9 %collective-permute-done.5.refs_3_ = bf16[384,768]{1,0:T(8,128)(2,1)S(1)} collective-permute-done((bf16[384,768]{1,0:T(8,128)(2,1)S(1)}, bf16[384,768]{1,0:T(8,128)(2,1)S(1)}, u32[]{:S(2)}, u32[]{:S(2)}) %collective-permute-start.5) | collective-permute-done | bytes 589856 | tf_op jit(solution)/shard_map/ppermute | solution.py:377
  37.2 0.5 shard_map.84
  37.6 0.0 copy-start.4
  37.7 0.6 collective-permute-start.6
  38.2 0.5 shard_map.86
  38.7 0.0 copy-start.2
  38.7 3.4 %collective-permute-start.9 = (bf16[256,768]{1,0:T(8,128)(2,1)S(1)}, bf16[256,768]{1,0:T(8,128)(2,1)S(1)}, u32[]{:S(2)}, u32[]{:S(2)}) collective-permute-start(bf16[256,768]{1,0:T(8,128)(2,1)S(1)} %get-tuple-element.51), channel_id=1, source_target_pairs={{0,24},{8,16},{16,8},{24,0},{1,25},{9,17},{17,9},{25,1},{2,26},{10... | collective-permute-start | bytes 1179656 | tf_op jit(solution)/shard_map/ppermute | solution.py:367
  42.2 0.2 collective-permute-start.8
  42.4 0.0 collective-permute-start.12
  42.4 1.2 %collective-permute-done.12 = f32[8,128]{1,0:T(8,128)S(1)} collective-permute-done((f32[8,128]{1,0:T(8,128)S(1)}, f32[8,128]{1,0:T(8,128)S(1)}, u32[]{:S(2)}, u32[]{:S(2)}) %collective-permute-start.12) | collective-permute-done | bytes 4128 | tf_op jit(solution)/shard_map/ppermute | solution.py:233
  43.5 1.5 %collective-permute-start.13 = (f32[8,128]{1,0:T(8,128)S(1)}, f32[8,128]{1,0:T(8,128)S(1)}, u32[]{:S(2)}, u32[]{:S(2)}) collective-permute-start(f32[8,128]{1,0:T(8,128)S(1)} %add.17), channel_id=1, source_target_pairs={{0,4},{2,6},{4,0},{6,2},{1,5},{3,7},{5,1},{7,3},{8,12},{10,14},{12... | collective-permute-start | bytes 12296 | tf_op jit(solution)/shard_map/ppermute | solution.py:233
  45.0 8.1 %collective-permute-done.13 = f32[8,128]{1,0:T(8,128)S(1)} collective-permute-done((f32[8,128]{1,0:T(8,128)S(1)}, f32[8,128]{1,0:T(8,128)S(1)}, u32[]{:S(2)}, u32[]{:S(2)}) %collective-permute-start.13) | collective-permute-done | bytes 4128 | tf_op jit(solution)/shard_map/ppermute | solution.py:233
  53.2 3.4 %collective-permute-start.11 = (bf16[128,768]{1,0:T(8,128)(2,1)S(1)}, bf16[128,768]{1,0:T(8,128)(2,1)S(1)}, u32[]{:S(2)}, u32[]{:S(2)}) collective-permute-start(bf16[128,768]{1,0:T(8,128)(2,1)S(1)} %get-tuple-element.54), channel_id=1, source_target_pairs={{0,24},{8,16},{16,8},{24,0},{1,25},{9,17},{17,9},{25,1},{2,26},{10... | collective-permute-start | bytes 589832 | tf_op jit(solution)/shard_map/ppermute | solution.py:366
  56.6 0.0 collective-permute-done.9.refs_4_
  56.6 5.1 %collective-permute-start.10 = (bf16[128,768]{1,0:T(8,128)(2,1)S(1)}, bf16[128,768]{1,0:T(8,128)(2,1)S(1)}, u32[]{:S(2)}, u32[]{:S(2)}) collective-permute-start(bf16[128,768]{1,0:T(8,128)(2,1)S(1)} %get-tuple-element.53), channel_id=1, source_target_pairs={{0,8},{8,0},{16,24},{24,16},{1,9},{9,1},{17,25},{25,17},{2,10},{10... | collective-permute-start | bytes 589832 | tf_op jit(solution)/shard_map/ppermute | solution.py:366
  61.6 0.0 copy-done.4
  61.6 0.5 shard_map.82
  62.2 1.1 %collective-permute-done.8.refs_3_ = bf16[256,768]{1,0:T(8,128)(2,1)S(1)} collective-permute-done((bf16[256,768]{1,0:T(8,128)(2,1)S(1)}, bf16[256,768]{1,0:T(8,128)(2,1)S(1)}, u32[]{:S(2)}, u32[]{:S(2)}) %collective-permute-start.8) | collective-permute-done | bytes 393248 | tf_op jit(solution)/shard_map/ppermute | solution.py:367
  63.3 0.0 collective-permute-start.14
  63.3 0.0 collective-permute-done.7.refs_2_
  63.3 2.4 %collective-permute-start.15 = (f32[8,128]{1,0:T(8,128)S(1)}, f32[8,128]{1,0:T(8,128)S(1)}, u32[]{:S(2)}, u32[]{:S(2)}) collective-permute-start(f32[8,128]{1,0:T(8,128)S(1)} %add.18.refs_2_), channel_id=1, source_target_pairs={{0,16},{8,24},{16,0},{24,8},{1,17},{9,25},{17,1},{25,9},{2,18},{10... | collective-permute-start | bytes 12296 | tf_op jit(solution)/shard_map/ppermute | solution.py:244
  65.7 0.0 collective-permute-done.6.refs_1_
  65.7 1.5 %collective-permute-start.16 = (f32[8,128]{1,0:T(8,128)S(1)}, f32[8,128]{1,0:T(8,128)S(1)}, u32[]{:S(2)}, u32[]{:S(2)}) collective-permute-start(f32[8,128]{1,0:T(8,128)S(1)} %add.18.refs_2_), channel_id=1, source_target_pairs={{0,24},{8,0},{16,8},{24,16},{1,25},{9,1},{17,9},{25,17},{2,26},{10... | collective-permute-start | bytes 12296 | tf_op jit(solution)/shard_map/ppermute | solution.py:244
  67.2 0.0 copy-done.2
  67.2 3.8 %shard_map.89 = f32[512,768]{1,0:T(8,128)} custom-call(bf16[384,512]{1,0:T(8,128)(2,1)S(1)} %get-tuple-element.58.refs_0_, bf16[384,512]{1,0:T(8,128)(2,1)S(1)} %get-tuple-element.59.refs_1_, bf16[384,512]{1,0:T(8,128)(2,1)S(1)} %get-tuple-element.60.refs_2_, bf16[384,512]{1,0:T(8,128)(2,1)S(1)} %get-tuple-element.61.refs_3_, ...), custom_call_target="tpu_custom_call" | custom-call | flops 1811939328 | bytes 7471104 | tf_op jit(solution)/shard_map/pallas_call | solution.py:25
  71.0 1.0 %shard_map.87 = (f32[384,768]{1,0:T(8,128)}, f32[128,768]{1,0:T(8,128)S(1)}) custom-call(f32[384,768]{1,0:T(8,128)S(1)} %get-tuple-element.42.refs_0_, bf16[384,768]{1,0:T(8,128)(2,1)S(1)} %collective-permute-done.6.refs_1_, bf16[384,768]{1,0:T(8,128)(2,1)S(1)} %collective-permute-done.7.refs_2_, bf16[256,768]{1,0:T(8,128)(2,1)S(1)} %collective-permute-done.8.refs_3_, ...), custom_call_target="tpu_custom_call" | custom-call | bytes 4718592 | tf_op jit(solution)/shard_map/pallas_call | solution.py:25
  71.9 0.0 collective-permute-done.14.refs_3_
  71.9 0.0 collective-permute-done.15.refs_4_
  72.0 0.0 collective-permute-done.16.refs_5_
  72.0 0.0 collective-permute-done.11.refs_1_
  72.0 0.0 collective-permute-done.10.refs_0_
  72.0 1.3 %shard_map.88 = (f32[1]{0:T(128)}, f32[384,768]{1,0:T(8,128)}) custom-call(f32[128,768]{1,0:T(8,128)S(1)} %get-tuple-element.52.rest_ref, bf16[128,768]{1,0:T(8,128)(2,1)S(1)} %collective-permute-done.10.refs_0_, bf16[128,768]{1,0:T(8,128)(2,1)S(1)} %collective-permute-done.11.refs_1_, f32[8,128]{1,0:T(8,128)S(1)} %add.18.refs_2_, ...), custom_call_target="tpu_custom_call", output_to_operand_aliasing={{1}: (7, {})} | custom-call | bytes 3162116 | tf_op jit(solution)/shard_map/pallas_call | solution.py:25
  (5 shorter events, 0.0 us)
Async XLA Ops:
  0.6 16.6 %collective-permute-start.3 = (bf16[384,768]{1,0:T(8,128)(2,1)}, bf16[384,768]{1,0:T(8,128)(2,1)S(1)}, u32[]{:S(2)}, u32[]{:S(2)}) collective-permute-start(bf16[384,768]{1,0:T(8,128)(2,1)} %refs_6_.1), channel_id=1, source_target_pairs={{0,4},{2,6},{4,0},{6,2},{1,5},{3,7},{5,1},{7,3},{8,12},{10,14},{12... | collective-permute-start | bytes 1769480 | tf_op jit(solution)/shard_map/ppermute | solution.py:270
  3.7 18.7 %collective-permute-start.1 = (bf16[384,768]{1,0:T(8,128)(2,1)}, bf16[384,768]{1,0:T(8,128)(2,1)S(1)}, u32[]{:S(2)}, u32[]{:S(2)}) collective-permute-start(bf16[384,768]{1,0:T(8,128)(2,1)} %refs_6_.1), channel_id=1, source_target_pairs={{0,8},{8,0},{16,24},{24,16},{1,9},{9,1},{17,25},{25,17},{2,10},{10... | collective-permute-start | bytes 1769480 | tf_op jit(solution)/shard_map/ppermute | solution.py:261
  5.3 17.8 %collective-permute-start.2 = (bf16[384,768]{1,0:T(8,128)(2,1)}, bf16[384,768]{1,0:T(8,128)(2,1)S(1)}, u32[]{:S(2)}, u32[]{:S(2)}) collective-permute-start(bf16[384,768]{1,0:T(8,128)(2,1)} %refs_6_.1), channel_id=1, source_target_pairs={{0,2},{2,0},{4,6},{6,4},{1,3},{3,1},{5,7},{7,5},{8,10},{10,8},{12,... | collective-permute-start | bytes 1769480 | tf_op jit(solution)/shard_map/ppermute | solution.py:267
  5.3 28.2 %collective-permute-start = (bf16[384,768]{1,0:T(8,128)(2,1)}, bf16[384,768]{1,0:T(8,128)(2,1)S(1)}, u32[]{:S(2)}, u32[]{:S(2)}) collective-permute-start(bf16[384,768]{1,0:T(8,128)(2,1)} %refs_6_.1), channel_id=1, source_target_pairs={{0,24},{8,16},{16,8},{24,0},{1,25},{9,17},{17,9},{25,1},{2,26},{10... | collective-permute-start | bytes 1769480 | tf_op jit(solution)/shard_map/ppermute | solution.py:261
  17.2 6.4 %collective-permute-start.4 = (bf16[384,768]{1,0:T(8,128)(2,1)S(1)}, bf16[384,768]{1,0:T(8,128)(2,1)S(1)}, u32[]{:S(2)}, u32[]{:S(2)}) collective-permute-start(bf16[384,768]{1,0:T(8,128)(2,1)S(1)} %collective-permute-done.3.refs_1_.refs_8_), channel_id=1, source_target_pairs={{0,2},{2,0},{4,6},{6,4},{1,3},{3,1},{5,7},{7,5},{8,10},{10,8},{12,... | collective-permute-start | bytes 1769480 | tf_op jit(solution)/shard_map/ppermute | solution.py:271
  18.2 1.1 %copy-start = (bf16[512,768]{1,0:T(8,128)(2,1)S(1)}, bf16[512,768]{1,0:T(8,128)(2,1)}, u32[]{:S(2)}) copy-start(bf16[512,768]{1,0:T(8,128)(2,1)} %q_ref.1) | copy-start | bytes 2359300
  19.4 1.1 %copy-start.1 = (bf16[384,768]{1,0:T(8,128)(2,1)S(1)}, bf16[384,768]{1,0:T(8,128)(2,1)}, u32[]{:S(2)}) copy-start(bf16[384,768]{1,0:T(8,128)(2,1)} %refs_6_.1) | copy-start | bytes 1769476
  20.4 0.7 copy-start.3
  35.1 2.1 %collective-permute-start.5 = (bf16[384,768]{1,0:T(8,128)(2,1)S(1)}, bf16[384,768]{1,0:T(8,128)(2,1)S(1)}, u32[]{:S(2)}, u32[]{:S(2)}) collective-permute-start(bf16[384,768]{1,0:T(8,128)(2,1)S(1)} %get-tuple-element.45), channel_id=1, source_target_pairs={{0,2},{2,0},{4,6},{6,4},{1,3},{3,1},{5,7},{7,5},{8,10},{10,8},{12,... | collective-permute-start | bytes 1769480 | tf_op jit(solution)/shard_map/ppermute | solution.py:377
  35.7 27.6 %collective-permute-start.7 = (bf16[384,768]{1,0:T(8,128)(2,1)S(1)}, bf16[384,768]{1,0:T(8,128)(2,1)S(1)}, u32[]{:S(2)}, u32[]{:S(2)}) collective-permute-start(bf16[384,768]{1,0:T(8,128)(2,1)S(1)} %get-tuple-element.48), channel_id=1, source_target_pairs={{0,2},{2,0},{4,6},{6,4},{1,3},{3,1},{5,7},{7,5},{8,10},{10,8},{12,... | collective-permute-start | bytes 1769480 | tf_op jit(solution)/shard_map/ppermute | solution.py:382
  37.6 24.0 %copy-start.4 = (s32[512]{0:T(512)S(1)}, s32[512]{0:T(512)}, u32[]{:S(2)}) copy-start(s32[512]{0:T(512)} %param.7) | copy-start | bytes 6148
  37.7 28.0 %collective-permute-start.6 = (bf16[384,768]{1,0:T(8,128)(2,1)S(1)}, bf16[384,768]{1,0:T(8,128)(2,1)S(1)}, u32[]{:S(2)}, u32[]{:S(2)}) collective-permute-start(bf16[384,768]{1,0:T(8,128)(2,1)S(1)} %get-tuple-element.46), channel_id=1, source_target_pairs={{0,4},{2,6},{4,0},{6,2},{1,5},{3,7},{5,1},{7,3},{8,12},{10,14},{12... | collective-permute-start | bytes 1769480 | tf_op jit(solution)/shard_map/ppermute | solution.py:381
  38.7 28.5 %copy-start.2 = (bf16[384,768]{1,0:T(8,128)(2,1)S(1)}, bf16[384,768]{1,0:T(8,128)(2,1)}, u32[]{:S(2)}) copy-start(bf16[384,768]{1,0:T(8,128)(2,1)} %refs_6_.1) | copy-start | bytes 1769476
  38.7 17.8 %collective-permute-start.9 = (bf16[256,768]{1,0:T(8,128)(2,1)S(1)}, bf16[256,768]{1,0:T(8,128)(2,1)S(1)}, u32[]{:S(2)}, u32[]{:S(2)}) collective-permute-start(bf16[256,768]{1,0:T(8,128)(2,1)S(1)} %get-tuple-element.51), channel_id=1, source_target_pairs={{0,24},{8,16},{16,8},{24,0},{1,25},{9,17},{17,9},{25,1},{2,26},{10... | collective-permute-start | bytes 1179656 | tf_op jit(solution)/shard_map/ppermute | solution.py:367
  42.2 21.1 %collective-permute-start.8 = (bf16[256,768]{1,0:T(8,128)(2,1)S(1)}, bf16[256,768]{1,0:T(8,128)(2,1)S(1)}, u32[]{:S(2)}, u32[]{:S(2)}) collective-permute-start(bf16[256,768]{1,0:T(8,128)(2,1)S(1)} %get-tuple-element.49), channel_id=1, source_target_pairs={{0,8},{8,0},{16,24},{24,16},{1,9},{9,1},{17,25},{25,17},{2,10},{10... | collective-permute-start | bytes 1179656 | tf_op jit(solution)/shard_map/ppermute | solution.py:367
  42.4 1.2 %collective-permute-start.12 = (f32[8,128]{1,0:T(8,128)S(1)}, f32[8,128]{1,0:T(8,128)S(1)}, u32[]{:S(2)}, u32[]{:S(2)}) collective-permute-start(f32[8,128]{1,0:T(8,128)S(1)} %get-tuple-element.55), channel_id=1, source_target_pairs={{0,2},{2,0},{4,6},{6,4},{1,3},{3,1},{5,7},{7,5},{8,10},{10,8},{12,... | collective-permute-start | bytes 12296 | tf_op jit(solution)/shard_map/ppermute | solution.py:233
  43.5 9.7 %collective-permute-start.13 = (f32[8,128]{1,0:T(8,128)S(1)}, f32[8,128]{1,0:T(8,128)S(1)}, u32[]{:S(2)}, u32[]{:S(2)}) collective-permute-start(f32[8,128]{1,0:T(8,128)S(1)} %add.17), channel_id=1, source_target_pairs={{0,4},{2,6},{4,0},{6,2},{1,5},{3,7},{5,1},{7,3},{8,12},{10,14},{12... | collective-permute-start | bytes 12296 | tf_op jit(solution)/shard_map/ppermute | solution.py:233
  53.2 18.8 %collective-permute-start.11 = (bf16[128,768]{1,0:T(8,128)(2,1)S(1)}, bf16[128,768]{1,0:T(8,128)(2,1)S(1)}, u32[]{:S(2)}, u32[]{:S(2)}) collective-permute-start(bf16[128,768]{1,0:T(8,128)(2,1)S(1)} %get-tuple-element.54), channel_id=1, source_target_pairs={{0,24},{8,16},{16,8},{24,0},{1,25},{9,17},{17,9},{25,1},{2,26},{10... | collective-permute-start | bytes 589832 | tf_op jit(solution)/shard_map/ppermute | solution.py:366
  56.6 15.4 %collective-permute-start.10 = (bf16[128,768]{1,0:T(8,128)(2,1)S(1)}, bf16[128,768]{1,0:T(8,128)(2,1)S(1)}, u32[]{:S(2)}, u32[]{:S(2)}) collective-permute-start(bf16[128,768]{1,0:T(8,128)(2,1)S(1)} %get-tuple-element.53), channel_id=1, source_target_pairs={{0,8},{8,0},{16,24},{24,16},{1,9},{9,1},{17,25},{25,17},{2,10},{10... | collective-permute-start | bytes 589832 | tf_op jit(solution)/shard_map/ppermute | solution.py:366
  63.3 8.7 %collective-permute-start.14 = (f32[8,128]{1,0:T(8,128)S(1)}, f32[8,128]{1,0:T(8,128)S(1)}, u32[]{:S(2)}, u32[]{:S(2)}) collective-permute-start(f32[8,128]{1,0:T(8,128)S(1)} %add.18.refs_2_), channel_id=1, source_target_pairs={{0,8},{8,16},{16,24},{24,0},{1,9},{9,17},{17,25},{25,1},{2,10},{10... | collective-permute-start | bytes 12296 | tf_op jit(solution)/shard_map/ppermute | solution.py:244
  63.3 8.7 %collective-permute-start.15 = (f32[8,128]{1,0:T(8,128)S(1)}, f32[8,128]{1,0:T(8,128)S(1)}, u32[]{:S(2)}, u32[]{:S(2)}) collective-permute-start(f32[8,128]{1,0:T(8,128)S(1)} %add.18.refs_2_), channel_id=1, source_target_pairs={{0,16},{8,24},{16,0},{24,8},{1,17},{9,25},{17,1},{25,9},{2,18},{10... | collective-permute-start | bytes 12296 | tf_op jit(solution)/shard_map/ppermute | solution.py:244
  65.7 6.3 %collective-permute-start.16 = (f32[8,128]{1,0:T(8,128)S(1)}, f32[8,128]{1,0:T(8,128)S(1)}, u32[]{:S(2)}, u32[]{:S(2)}) collective-permute-start(f32[8,128]{1,0:T(8,128)S(1)} %add.18.refs_2_), channel_id=1, source_target_pairs={{0,24},{8,0},{16,8},{24,16},{1,25},{9,1},{17,9},{25,17},{2,26},{10... | collective-permute-start | bytes 12296 | tf_op jit(solution)/shard_map/ppermute | solution.py:244

commit v4 on v3

--- a/solution.py
+++ b/solution.py
@@ -13,7 +13,7 @@
 LOWEST = -1e30
 LOG2E = math.log2(math.e)
 VMEM_LIMIT = 24 << 20
-CHUNKS = 4
+CHUNKS = 2
 
 
 def whole():
@@ -81,10 +81,10 @@
     return jnp.concatenate(parts, axis=0)
 
 
-def last_body(scale, blocks, cells, first, *refs):
-    q_ref, p_ref, e_first_ref, vis_ref = refs[:4]
-    stats_refs = refs[4 : 4 + cells - 1]
-    e_ref, f_ref, head_ref, tail_ref, w_ref, loss_ref = refs[4 + cells - 1 :]
+def last_body(scale, blocks, cells, *refs):
+    q_ref, p_ref, vis_ref = refs[:3]
+    stats_refs = refs[3 : 3 + cells - 1]
+    f_ref, head_ref, tail_ref, w_ref, loss_ref, e_ref = refs[3 + cells - 1 :]
     scores = scores_of(q_ref, p_ref)
     tops, sums = [], []
     for block_at in range(blocks):
@@ -105,16 +105,14 @@
         part = jnp.sum(all_sums[cell] * jnp.exp(gap), axis=0, keepdims=True)
         total = part if total is None else total + part
     log_total = highest + jnp.log(total)
-    factors = []
     f_ref[...] = jnp.zeros_like(f_ref)
     for cell in range(cells):
         factor = jnp.exp(jnp.where(seen[cell], all_tops[cell] - log_total, LOWEST))
         f_ref[cell * 8 : cell * 8 + blocks, :] = factor
-        factors.append(factor)
     positive_score = stats_refs[0][2 * blocks : 2 * blocks + 1, :]
     lost = jnp.sum(log_total - positive_score, axis=1, keepdims=True)
     loss_ref[...] = jnp.broadcast_to(lost, loss_ref.shape)
-    weights = weights_of(e_first_ref, factors[first], blocks, None)
+    weights = weights_of(e_ref, factor, blocks, None)
     w_ref[...] = weights
     put_pieces((head_ref, tail_ref), weights, q_ref, scale)
 
@@ -185,10 +183,15 @@
 
 def final_body(share, tails, parts, rest_ref, *refs):
     tail_refs, lost_refs = refs[:tails], refs[tails : tails + parts]
-    loss_ref, out_ref, held_ref, sem = refs[tails + parts + 1 :]
+    loss_ref, out_ref, held_ref, sem, loss_sm, loss_sem = refs[tails + parts + 1 :]
+    total = lost_refs[0][...]
+    for ref in lost_refs[1:]:
+        total = total + ref[...]
+    loss_sm[0] = jnp.max(total) * share
+    copies = [pltpu.make_async_copy(loss_sm, loss_ref, loss_sem)]
+    copies[0].start()
     first = out_ref.shape[0] - held_ref.shape[0]
     chunk = held_ref.shape[0] // CHUNKS
-    copies = []
     for at in range(CHUNKS):
         rows = pl.ds(at * chunk, chunk)
         total = rest_ref[rows, :]
@@ -199,26 +202,25 @@
         copy = pltpu.make_async_copy(held_ref.at[rows, :], there, sem.at[at])
         copy.start()
         copies.append(copy)
-    total = lost_refs[0][...]
-    for ref in lost_refs[1:]:
-        total = total + ref[...]
-    loss_ref[0] = jnp.max(total) * share
     for copy in copies:
         copy.wait()
 
 
-def row_plan(n_row, reach):
+def row_plan(n_row, n_col, reach):
+    cells = [(r, c) for r in range(n_row) for c in range(n_col)]
+
+    def pairs(partner):
+        return [(r * n_col + c, partner(r, c) % n_row * n_col + c) for r, c in cells]
+
+    if reach == 1 and n_row % 2 == 0:
+        first = pairs(lambda r, c: r + 1 if (r + c) % 2 == 0 else r - 1)
+        second = pairs(lambda r, c: r - 1 if (r + c) % 2 == 0 else r + 1)
+        return [(first, first, (2, 1)), (second, second, (1, 2))]
     plan = []
-    if reach == 1 and n_row % 2 == 0:
-        even_up = [(i, i ^ 1) for i in range(n_row)]
-        odd_up = [(i, (i + 1) % n_row if i % 2 else (i - 1) % n_row) for i in range(n_row)]
-        plan.append((even_up, even_up, (2, 1)))
-        plan.append((odd_up, odd_up, (1, 2)))
-        return plan
     offsets = list(range(-reach, 0)) + list(range(1, reach + 1))
     for group_at, offset in enumerate(offsets):
-        there = [((i + offset) % n_row, i) for i in range(n_row)]
-        back = [(i, (i + offset) % n_row) for i in range(n_row)]
+        there = pairs(lambda r, c: r - offset)
+        back = pairs(lambda r, c: r + offset)
         plan.append((there, back, (group_at + 1, group_at + 1)))
     return plan
 
@@ -235,14 +237,18 @@
     return array
 
 
+def partners(size, step):
+    if size & (size - 1):
+        return [(i, (i + step) % size) for i in range(size)]
+    return [(i, i ^ step) for i in range(size)]
+
+
 def from_all(array, axis):
     size = lax.axis_size(axis)
     if size > 4:
         return [sum_steps(array, axis)]
     shifts = range(1, size)
-    return [array] + [
-        lax.ppermute(array, axis, [(i, (i + s) % size) for i in range(size)]) for s in shifts
-    ]
+    return [array] + [lax.ppermute(array, axis, partners(size, s)) for s in shifts]
 
 
 def local_loss(queries, passages, positive, block_mask, roster):
@@ -253,12 +259,12 @@
     held = passages.shape[0]
     blocks = held // BLK
     scale = width ** (-0.5)
-    odd_row = lax.axis_index("row") % 2 == 1
     odd_col = lax.axis_index("col") % 2 == 1
+    odd_cell = (lax.axis_index("row") + lax.axis_index("col")) % 2 == 1
     f32, bf16 = jnp.float32, jnp.bfloat16
 
-    rows = row_plan(n_row, reach)
-    near = [lax.ppermute(passages, "row", there) for there, _, _ in rows]
+    rows = row_plan(n_row, n_col, reach)
+    near = [lax.ppermute(passages, ("row", "col"), there) for there, _, _ in rows]
 
     swap = [(i, i ^ 1) for i in range(n_col)]
     col_cells = []
@@ -295,7 +301,7 @@
             padded(jnp.where(odd_col, roster_t[odd - 1][None], roster_t[even - 1][None]) == ids)
         )
     for _, _, (even, odd) in rows:
-        seen.append(padded(jnp.where(odd_row, group_rows(odd), group_rows(even))))
+        seen.append(padded(jnp.where(odd_cell, group_rows(odd), group_rows(even))))
     vis = jnp.concatenate(seen, axis=0)
 
     cell_rows = [passages] + [cell[0] for cell in col_cells] + near
@@ -325,19 +331,18 @@
     last = cells - 1
     f_shape = jax.ShapeDtypeStruct((8 * cells, count), f32)
     loss_shape = jax.ShapeDtypeStruct((8, BLK), f32)
-    tail = BLK if blocks > 1 else 0
-    assert tail
+    tail = BLK
     head_shape = jax.ShapeDtypeStruct((held - tail, width), bf16)
     tail_shape = jax.ShapeDtypeStruct((tail, width), bf16)
-    e, factors, g_head, g_tail, w_first, lost = call(
-        functools.partial(last_body, scale, blocks, cells, first),
-        (e_shape, f_shape, head_shape, tail_shape, w_shape, loss_shape),
-        (queries, cell_rows[last], raised[first], vis, *stats),
+    factors, g_head, g_tail, w_last, lost = call(
+        functools.partial(last_body, scale, blocks, cells),
+        (f_shape, head_shape, tail_shape, w_shape, loss_shape),
+        (queries, cell_rows[last], vis, *stats),
         2 * dot_flops,
         held * count,
-    )
-    raised.append(e)
-    weights = {first: w_first}
+        scratch=(pltpu.VMEM((held, count), f32),),
+    )
+    weights = {last: w_last}
 
     def gradient_of(cell, shape, added=None):
         own = cell == 0
@@ -352,8 +357,8 @@
         weights[cell] = w
         return g
 
-    heads, tails = [(g_head, g_tail)], []
-    for at in range(1, len(rows)):
+    graded = {len(rows) - 1: (g_head, g_tail)}
+    for at in range(len(rows) - 1):
         cell = first + at
         g_head, g_tail, weights[cell] = call(
             functools.partial(pieces_body, scale, blocks, cell),
@@ -361,10 +366,11 @@
             (queries, raised[cell], factors),
             dot_flops,
         )
-        heads.append((g_head, g_tail))
+        graded[at] = (g_head, g_tail)
+    heads, tails = [], []
     for at, (_, back, _) in enumerate(rows):
-        tails.append(lax.ppermute(heads[at][1], "row", back))
-        heads[at] = lax.ppermute(heads[at][0], "row", back)
+        heads.append(lax.ppermute(graded[at][0], ("row", "col"), back))
+        tails.append(lax.ppermute(graded[at][1], ("row", "col"), back))
 
     lost_col = sum_steps(lost, "col")
     lost_parts = from_all(lost_col, "row")
@@ -412,8 +418,8 @@
         (jax.ShapeDtypeStruct((1,), f32), g_wide),
         (rest, *tails, *lost_parts, written),
         0,
-        out_specs=(pl.BlockSpec(memory_space=pltpu.SMEM), out_spec),
-        scratch=(pltpu.VMEM((tail, width), f32), wire_sems),
+        out_specs=(out_spec, out_spec),
+        scratch=(pltpu.VMEM((tail, width), f32), wire_sems, pltpu.SMEM((1,), f32), pltpu.SemaphoreType.DMA),
         alias=1 + len(tails) + len(lost_parts),
     )
     return (loss, toward, grad_passages)

time: 73.7 us -> 74 us (level)
  waiting for transfers between devices: 28.5 us -> 31.6 us
  starting transfers between devices: 25.8 us -> 23.4 us
    ppermute x9, waiting for transfers between devices: 10.3 us -> 12.9 us  [the longest x2 9.86 us: local_loss(): lax.ppermute(passages, ('row', 'col'), there)]
    ppermute x9, starting transfers between devices: 20 us -> 17.6 us  [the longest x2 6 us: local_loss(): tails.append(lax.ppermute(graded[at][1], ('row', 'col'), back))]
  transfers between devices with their start and end apart: 17 -> 17, of which waited for: 6 -> 7; matrix products, arithmetic and copies ran while one was open for 3% -> 3% of each run, Pallas kernels for 13% -> 13%
where the time goes in v4:
time: 74 us; the launch traced here: 73.6 us
  waiting for transfers between devices  31.6 us (43%)
  starting transfers between devices  23.4 us (32%)
  Pallas kernels  12.3 us (17%)
  local copies, waits for them, and re-layouts  3.02 us (4%)
  other arithmetic  2.38 us (3%)
  between operations  0.84 us (1%)
    pallas_call x14, Pallas kernels, call(): pl.pallas_call(kernel, out_shape=tuple(outs), in_specs=[pl.BlockSpec(memo...  12.3 us
    ppermute x2, waiting for transfers between devices, local_loss(): lax.ppermute(passages, ('row', 'col'), there)  9.86 us
    ppermute x2, waiting for transfers between devices, sum_steps(): array = array + lax.ppermute(array, axis, pairs)  9.77 us
    ppermute x1, waiting for transfers between devices, local_loss(): far = lax.ppermute(passages, 'col', there)  7.94 us
    ppermute x2, starting transfers between devices, local_loss(): tails.append(lax.ppermute(graded[at][1], ('row', 'col'), back))  6 us
    ppermute x3, starting transfers between devices, from_all(): lax.ppermute(array, axis, partners(size, s))  4.44 us
    ppermute x2, starting transfers between devices, local_loss(): lax.ppermute(passages, ('row', 'col'), there)  4.05 us
    ppermute x2, starting transfers between devices, local_loss(): heads.append(lax.ppermute(graded[at][0], ('row', 'col'), back))  3.14 us
  transfers between devices with their start and end apart: 17, of which 7 were waited for; matrix products, arithmetic and copies ran while one was open for 3% of the time, Pallas kernels for 13%

profile of v4, /device:TPU:0, one launch (start us, length us, event | category | flops | bytes accessed | tf_op | source)
XLA Modules:
  0.0 73.6 jit_solution(508393190774547040)
XLA Ops:
  0.6 3.1 %collective-permute-start.2 = (bf16[384,768]{1,0:T(8,128)(2,1)}, bf16[384,768]{1,0:T(8,128)(2,1)S(1)}, u32[]{:S(2)}, u32[]{:S(2)}) collective-permute-start(bf16[384,768]{1,0:T(8,128)(2,1)} %refs_6_.1), channel_id=1, source_target_pairs={{0,4},{2,6},{4,0},{6,2},{1,5},{3,7},{5,1},{7,3},{8,12},{10,14},{12... | collective-permute-start | bytes 1769480 | tf_op jit(solution)/shard_map/ppermute | solution.py:276
  3.7 0.0 collective-permute-start.1
  3.7 1.6 %collective-permute-start.4 = (bf16[384,768]{1,0:T(8,128)(2,1)}, bf16[384,768]{1,0:T(8,128)(2,1)S(1)}, u32[]{:S(2)}, u32[]{:S(2)}) collective-permute-start(bf16[384,768]{1,0:T(8,128)(2,1)} %refs_6_.1), channel_id=1, source_target_pairs={{0,8},{2,26},{4,12},{6,30},{8,0},{10,18},{12,4},{14,22},{16,24},{1... | collective-permute-start | bytes 1769480 | tf_op jit(solution)/shard_map/ppermute | solution.py:267
  5.3 2.5 %collective-permute-start = (bf16[384,768]{1,0:T(8,128)(2,1)}, bf16[384,768]{1,0:T(8,128)(2,1)S(1)}, u32[]{:S(2)}, u32[]{:S(2)}) collective-permute-start(bf16[384,768]{1,0:T(8,128)(2,1)} %refs_6_.1), channel_id=1, source_target_pairs={{0,24},{2,10},{4,28},{6,14},{8,16},{10,2},{12,20},{14,6},{16,8},{1... | collective-permute-start | bytes 1769480 | tf_op jit(solution)/shard_map/ppermute | solution.py:267
  7.7 0.7 add_select_fusion
  8.4 0.8 %select_convert_fusion = (f32[3,512]{1,0:T(4,128)S(1)}, pred[3,512]{1,0:T(4,128)(4,1)S(1)}, pred[3,512]{1,0:T(4,128)(4,1)S(1)}, f32[3,512]{1,0:T(4,128)S(1)}) fusion(pred[]{:T(512)S(6)} %eq.95, s32[9,512]{1,0:T(8,128)} %bitcast.8, s32[512]{0:T(512)S(1)} %add_select_fusion), kind=kLoop, calls=%fused_computation.12 | loop fusion | flops 12288 | bytes 35841 | tf_op jit(solution)/shard_map/convert_element_type | solution.py:293
  9.3 7.9 %collective-permute-done.2.refs_1_.refs_8_ = bf16[384,768]{1,0:T(8,128)(2,1)S(1)} collective-permute-done((bf16[384,768]{1,0:T(8,128)(2,1)}, bf16[384,768]{1,0:T(8,128)(2,1)S(1)}, u32[]{:S(2)}, u32[]{:S(2)}) %collective-permute-start.2) | collective-permute-done | bytes 589856 | tf_op jit(solution)/shard_map/ppermute | solution.py:276
  17.2 0.0 collective-permute-start.3
  17.2 0.8 %broadcast_select_fusion = (s32[1,512]{1,0:T(1,128)S(1)}, s32[1,512]{1,0:T(1,128)S(1)}, s32[1,512]{1,0:T(1,128)S(1)}) fusion(pred[]{:T(512)S(6)} %eq.82, s32[3,512]{1,0:T(4,128)} %bitcast.12), kind=kLoop, calls=%fused_computation.14 | loop fusion | flops 1024 | bytes 12289 | tf_op jit(solution)/shard_map/jit(_where)/select_n | solution.py:301
  18.1 0.1 concatenate.3.refs_2_
  18.2 0.0 copy-start
  18.2 1.1 %copy-done = bf16[512,768]{1,0:T(8,128)(2,1)S(1)} copy-done((bf16[512,768]{1,0:T(8,128)(2,1)S(1)}, bf16[512,768]{1,0:T(8,128)(2,1)}, u32[]{:S(2)}) %copy-start) | copy-done | bytes 786456
  19.4 0.0 copy-start.1
  19.4 1.1 %copy-done.1 = bf16[384,768]{1,0:T(8,128)(2,1)S(1)} copy-done((bf16[384,768]{1,0:T(8,128)(2,1)S(1)}, bf16[384,768]{1,0:T(8,128)(2,1)}, u32[]{:S(2)}) %copy-start.1) | copy-done | bytes 589848
  20.4 0.0 copy-start.3
  20.4 0.7 copy-done.3
  21.1 0.7 shard_map.76
  21.8 0.6 shard_map.78
  22.4 0.0 collective-permute-done.1.refs_1_.refs_7_
  22.4 0.6 shard_map.77
  23.0 4.0 %collective-permute-done.4.refs_1_.refs_10_ = bf16[384,768]{1,0:T(8,128)(2,1)S(1)} collective-permute-done((bf16[384,768]{1,0:T(8,128)(2,1)}, bf16[384,768]{1,0:T(8,128)(2,1)S(1)}, u32[]{:S(2)}, u32[]{:S(2)}) %collective-permute-start.4) | collective-permute-done | bytes 589856 | tf_op jit(solution)/shard_map/ppermute | solution.py:267
  27.1 0.6 shard_map.80
  27.7 0.0 collective-permute-done.3.refs_1_.refs_9_
  27.7 0.6 shard_map.79
  28.3 5.8 %collective-permute-done.refs_1_.refs_11_ = bf16[384,768]{1,0:T(8,128)(2,1)S(1)} collective-permute-done((bf16[384,768]{1,0:T(8,128)(2,1)}, bf16[384,768]{1,0:T(8,128)(2,1)S(1)}, u32[]{:S(2)}, u32[]{:S(2)}) %collective-permute-start) | collective-permute-done | bytes 589856 | tf_op jit(solution)/shard_map/ppermute | solution.py:267
  34.1 1.1 %shard_map.81 = (f32[48,512]{1,0:T(8,128)S(1)}, bf16[256,768]{1,0:T(8,128)(2,1)S(1)}, bf16[128,768]{1,0:T(8,128)(2,1)S(1)}, bf16[384,512]{1,0:T(8,128)(2,1)S(1)}, f32[8,128]{1,0:T(8,128)S(1)}) custom-call(bf16[512,768]{1,0:T(8,128)(2,1)S(1)} %copy-done, bf16[384,768]{1,0:T(8,128)(2,1)S(1)} %collective-permute-done.refs_1_.refs_11_, ...), custom_call_target="tpu_custom_call" | custom-call | flops 603979776 | bytes 2641920 | tf_op jit(solution)/shard_map/pallas_call | solution.py:25
  35.3 0.5 shard_map.83
  35.8 0.1 collective-permute-start.5
  35.9 0.5 shard_map.85
  36.3 0.6 collective-permute-start.7
  36.9 0.9 %collective-permute-done.5.refs_3_ = bf16[384,768]{1,0:T(8,128)(2,1)S(1)} collective-permute-done((bf16[384,768]{1,0:T(8,128)(2,1)S(1)}, bf16[384,768]{1,0:T(8,128)(2,1)S(1)}, u32[]{:S(2)}, u32[]{:S(2)}) %collective-permute-start.5) | collective-permute-done | bytes 589856 | tf_op jit(solution)/shard_map/ppermute | solution.py:383
  37.8 0.5 shard_map.84
  38.3 0.0 copy-start.4
  38.3 0.6 collective-permute-start.6
  38.9 0.5 shard_map.86
  39.4 0.0 copy-start.2
  39.4 0.1 collective-permute-start.8
  39.5 3.1 %collective-permute-start.9 = (bf16[256,768]{1,0:T(8,128)(2,1)S(1)}, bf16[256,768]{1,0:T(8,128)(2,1)S(1)}, u32[]{:S(2)}, u32[]{:S(2)}) collective-permute-start(bf16[256,768]{1,0:T(8,128)(2,1)S(1)} %get-tuple-element.49), channel_id=1, source_target_pairs={{0,24},{2,10},{4,28},{6,14},{8,16},{10,2},{12,20},{14,6},{16,8},{1... | collective-permute-start | bytes 1179656 | tf_op jit(solution)/shard_map/ppermute | solution.py:372
  42.6 0.0 collective-permute-start.12
  42.6 1.2 %collective-permute-done.12 = f32[8,128]{1,0:T(8,128)S(1)} collective-permute-done((f32[8,128]{1,0:T(8,128)S(1)}, f32[8,128]{1,0:T(8,128)S(1)}, u32[]{:S(2)}, u32[]{:S(2)}) %collective-permute-start.12) | collective-permute-done | bytes 4128 | tf_op jit(solution)/shard_map/ppermute | solution.py:235
  43.7 1.5 %collective-permute-start.13 = (f32[8,128]{1,0:T(8,128)S(1)}, f32[8,128]{1,0:T(8,128)S(1)}, u32[]{:S(2)}, u32[]{:S(2)}) collective-permute-start(f32[8,128]{1,0:T(8,128)S(1)} %add.21), channel_id=1, source_target_pairs={{0,4},{2,6},{4,0},{6,2},{1,5},{3,7},{5,1},{7,3},{8,12},{10,14},{12... | collective-permute-start | bytes 12296 | tf_op jit(solution)/shard_map/ppermute | solution.py:235
  45.3 8.6 %collective-permute-done.13 = f32[8,128]{1,0:T(8,128)S(1)} collective-permute-done((f32[8,128]{1,0:T(8,128)S(1)}, f32[8,128]{1,0:T(8,128)S(1)}, u32[]{:S(2)}, u32[]{:S(2)}) %collective-permute-start.13) | collective-permute-done | bytes 4128 | tf_op jit(solution)/shard_map/ppermute | solution.py:235
  53.9 0.0 collective-permute-start.10
  53.9 3.0 %collective-permute-done.8.refs_3_ = bf16[256,768]{1,0:T(8,128)(2,1)S(1)} collective-permute-done((bf16[256,768]{1,0:T(8,128)(2,1)S(1)}, bf16[256,768]{1,0:T(8,128)(2,1)S(1)}, u32[]{:S(2)}, u32[]{:S(2)}) %collective-permute-start.8) | collective-permute-done | bytes 393248 | tf_op jit(solution)/shard_map/ppermute | solution.py:372
  56.9 6.0 %collective-permute-start.11 = (bf16[128,768]{1,0:T(8,128)(2,1)S(1)}, bf16[128,768]{1,0:T(8,128)(2,1)S(1)}, u32[]{:S(2)}, u32[]{:S(2)}) collective-permute-start(bf16[128,768]{1,0:T(8,128)(2,1)S(1)} %get-tuple-element.52), channel_id=1, source_target_pairs={{0,24},{2,10},{4,28},{6,14},{8,16},{10,2},{12,20},{14,6},{16,8},{1... | collective-permute-start | bytes 589832 | tf_op jit(solution)/shard_map/ppermute | solution.py:373
  62.9 0.0 copy-done.4
  62.9 0.5 shard_map.82
  63.4 0.0 collective-permute-done.9.refs_4_
  63.5 0.1 collective-permute-start.14
  63.5 0.0 collective-permute-done.7.refs_2_
  63.5 0.5 collective-permute-start.15
  64.1 0.0 collective-permute-done.6.refs_1_
  64.1 3.8 %collective-permute-start.16 = (f32[8,128]{1,0:T(8,128)S(1)}, f32[8,128]{1,0:T(8,128)S(1)}, u32[]{:S(2)}, u32[]{:S(2)}) collective-permute-start(f32[8,128]{1,0:T(8,128)S(1)} %add.22.refs_2_), channel_id=1, source_target_pairs={{0,24},{8,16},{16,8},{24,0},{1,25},{9,17},{17,9},{25,1},{2,26},{10... | collective-permute-start | bytes 12296 | tf_op jit(solution)/shard_map/ppermute | solution.py:251
  67.9 0.0 copy-done.2
  67.9 3.8 %shard_map.89 = f32[512,768]{1,0:T(8,128)} custom-call(bf16[384,512]{1,0:T(8,128)(2,1)S(1)} %get-tuple-element.56.refs_0_, bf16[384,512]{1,0:T(8,128)(2,1)S(1)} %get-tuple-element.57.refs_1_, bf16[384,512]{1,0:T(8,128)(2,1)S(1)} %get-tuple-element.58.refs_2_, bf16[384,512]{1,0:T(8,128)(2,1)S(1)} %get-tuple-element.59.refs_3_, ...), custom_call_target="tpu_custom_call" | custom-call | flops 1811939328 | bytes 7471104 | tf_op jit(solution)/shard_map/pallas_call | solution.py:25
  71.7 1.0 %shard_map.87 = (f32[384,768]{1,0:T(8,128)}, f32[128,768]{1,0:T(8,128)S(1)}) custom-call(f32[384,768]{1,0:T(8,128)S(1)} %get-tuple-element.40.refs_0_, bf16[384,768]{1,0:T(8,128)(2,1)S(1)} %collective-permute-done.6.refs_1_, bf16[384,768]{1,0:T(8,128)(2,1)S(1)} %collective-permute-done.7.refs_2_, bf16[256,768]{1,0:T(8,128)(2,1)S(1)} %collective-permute-done.8.refs_3_, ...), custom_call_target="tpu_custom_call" | custom-call | bytes 4718592 | tf_op jit(solution)/shard_map/pallas_call | solution.py:25
  72.7 0.0 collective-permute-done.14.refs_3_
  72.7 0.0 collective-permute-done.15.refs_4_
  72.7 0.0 collective-permute-done.16.refs_5_
  72.7 0.0 collective-permute-done.10.refs_0_
  72.8 0.0 collective-permute-done.11.refs_1_
  72.8 0.8 %shard_map.88 = (f32[1]{0:T(128)}, f32[384,768]{1,0:T(8,128)}) custom-call(f32[128,768]{1,0:T(8,128)S(1)} %get-tuple-element.50.rest_ref, bf16[128,768]{1,0:T(8,128)(2,1)S(1)} %collective-permute-done.10.refs_0_, bf16[128,768]{1,0:T(8,128)(2,1)S(1)} %collective-permute-done.11.refs_1_, f32[8,128]{1,0:T(8,128)S(1)} %add.22.refs_2_, ...), custom_call_target="tpu_custom_call", output_to_operand_aliasing={{1}: (7, {})} | custom-call | bytes 3162116 | tf_op jit(solution)/shard_map/pallas_call | solution.py:25
  (5 shorter events, 0.0 us)
Async XLA Ops:
  0.6 16.6 %collective-permute-start.2 = (bf16[384,768]{1,0:T(8,128)(2,1)}, bf16[384,768]{1,0:T(8,128)(2,1)S(1)}, u32[]{:S(2)}, u32[]{:S(2)}) collective-permute-start(bf16[384,768]{1,0:T(8,128)(2,1)} %refs_6_.1), channel_id=1, source_target_pairs={{0,4},{2,6},{4,0},{6,2},{1,5},{3,7},{5,1},{7,3},{8,12},{10,14},{12... | collective-permute-start | bytes 1769480 | tf_op jit(solution)/shard_map/ppermute | solution.py:276
  3.7 18.7 %collective-permute-start.1 = (bf16[384,768]{1,0:T(8,128)(2,1)}, bf16[384,768]{1,0:T(8,128)(2,1)S(1)}, u32[]{:S(2)}, u32[]{:S(2)}) collective-permute-start(bf16[384,768]{1,0:T(8,128)(2,1)} %refs_6_.1), channel_id=1, source_target_pairs={{0,2},{2,0},{4,6},{6,4},{1,3},{3,1},{5,7},{7,5},{8,10},{10,8},{12,... | collective-permute-start | bytes 1769480 | tf_op jit(solution)/shard_map/ppermute | solution.py:273
  3.7 23.4 %collective-permute-start.4 = (bf16[384,768]{1,0:T(8,128)(2,1)}, bf16[384,768]{1,0:T(8,128)(2,1)S(1)}, u32[]{:S(2)}, u32[]{:S(2)}) collective-permute-start(bf16[384,768]{1,0:T(8,128)(2,1)} %refs_6_.1), channel_id=1, source_target_pairs={{0,8},{2,26},{4,12},{6,30},{8,0},{10,18},{12,4},{14,22},{16,24},{1... | collective-permute-start | bytes 1769480 | tf_op jit(solution)/shard_map/ppermute | solution.py:267
  5.3 28.9 %collective-permute-start = (bf16[384,768]{1,0:T(8,128)(2,1)}, bf16[384,768]{1,0:T(8,128)(2,1)S(1)}, u32[]{:S(2)}, u32[]{:S(2)}) collective-permute-start(bf16[384,768]{1,0:T(8,128)(2,1)} %refs_6_.1), channel_id=1, source_target_pairs={{0,24},{2,10},{4,28},{6,14},{8,16},{10,2},{12,20},{14,6},{16,8},{1... | collective-permute-start | bytes 1769480 | tf_op jit(solution)/shard_map/ppermute | solution.py:267
  17.2 10.5 %collective-permute-start.3 = (bf16[384,768]{1,0:T(8,128)(2,1)S(1)}, bf16[384,768]{1,0:T(8,128)(2,1)S(1)}, u32[]{:S(2)}, u32[]{:S(2)}) collective-permute-start(bf16[384,768]{1,0:T(8,128)(2,1)S(1)} %collective-permute-done.2.refs_1_.refs_8_), channel_id=1, source_target_pairs={{0,2},{2,0},{4,6},{6,4},{1,3},{3,1},{5,7},{7,5},{8,10},{10,8},{12,... | collective-permute-start | bytes 1769480 | tf_op jit(solution)/shard_map/ppermute | solution.py:277
  18.2 1.1 %copy-start = (bf16[512,768]{1,0:T(8,128)(2,1)S(1)}, bf16[512,768]{1,0:T(8,128)(2,1)}, u32[]{:S(2)}) copy-start(bf16[512,768]{1,0:T(8,128)(2,1)} %q_ref.1) | copy-start | bytes 2359300
  19.4 1.1 %copy-start.1 = (bf16[384,768]{1,0:T(8,128)(2,1)S(1)}, bf16[384,768]{1,0:T(8,128)(2,1)}, u32[]{:S(2)}) copy-start(bf16[384,768]{1,0:T(8,128)(2,1)} %refs_6_.1) | copy-start | bytes 1769476
  20.4 0.7 copy-start.3
  35.8 2.1 %collective-permute-start.5 = (bf16[384,768]{1,0:T(8,128)(2,1)S(1)}, bf16[384,768]{1,0:T(8,128)(2,1)S(1)}, u32[]{:S(2)}, u32[]{:S(2)}) collective-permute-start(bf16[384,768]{1,0:T(8,128)(2,1)S(1)} %get-tuple-element.43), channel_id=1, source_target_pairs={{0,2},{2,0},{4,6},{6,4},{1,3},{3,1},{5,7},{7,5},{8,10},{10,8},{12,... | collective-permute-start | bytes 1769480 | tf_op jit(solution)/shard_map/ppermute | solution.py:383
  36.3 27.2 %collective-permute-start.7 = (bf16[384,768]{1,0:T(8,128)(2,1)S(1)}, bf16[384,768]{1,0:T(8,128)(2,1)S(1)}, u32[]{:S(2)}, u32[]{:S(2)}) collective-permute-start(bf16[384,768]{1,0:T(8,128)(2,1)S(1)} %get-tuple-element.46), channel_id=1, source_target_pairs={{0,2},{2,0},{4,6},{6,4},{1,3},{3,1},{5,7},{7,5},{8,10},{10,8},{12,... | collective-permute-start | bytes 1769480 | tf_op jit(solution)/shard_map/ppermute | solution.py:388
  38.3 24.6 %copy-start.4 = (s32[512]{0:T(512)S(1)}, s32[512]{0:T(512)}, u32[]{:S(2)}) copy-start(s32[512]{0:T(512)} %param.7) | copy-start | bytes 6148
  38.3 25.7 %collective-permute-start.6 = (bf16[384,768]{1,0:T(8,128)(2,1)S(1)}, bf16[384,768]{1,0:T(8,128)(2,1)S(1)}, u32[]{:S(2)}, u32[]{:S(2)}) collective-permute-start(bf16[384,768]{1,0:T(8,128)(2,1)S(1)} %get-tuple-element.44), channel_id=1, source_target_pairs={{0,4},{2,6},{4,0},{6,2},{1,5},{3,7},{5,1},{7,3},{8,12},{10,14},{12... | collective-permute-start | bytes 1769480 | tf_op jit(solution)/shard_map/ppermute | solution.py:387
  39.4 28.5 %copy-start.2 = (bf16[384,768]{1,0:T(8,128)(2,1)S(1)}, bf16[384,768]{1,0:T(8,128)(2,1)}, u32[]{:S(2)}) copy-start(bf16[384,768]{1,0:T(8,128)(2,1)} %refs_6_.1) | copy-start | bytes 1769476
  39.4 17.5 %collective-permute-start.8 = (bf16[256,768]{1,0:T(8,128)(2,1)S(1)}, bf16[256,768]{1,0:T(8,128)(2,1)S(1)}, u32[]{:S(2)}, u32[]{:S(2)}) collective-permute-start(bf16[256,768]{1,0:T(8,128)(2,1)S(1)} %get-tuple-element.48), channel_id=1, source_target_pairs={{0,8},{2,26},{4,12},{6,30},{8,0},{10,18},{12,4},{14,22},{16,24},{1... | collective-permute-start | bytes 1179656 | tf_op jit(solution)/shard_map/ppermute | solution.py:372
  39.5 23.9 %collective-permute-start.9 = (bf16[256,768]{1,0:T(8,128)(2,1)S(1)}, bf16[256,768]{1,0:T(8,128)(2,1)S(1)}, u32[]{:S(2)}, u32[]{:S(2)}) collective-permute-start(bf16[256,768]{1,0:T(8,128)(2,1)S(1)} %get-tuple-element.49), channel_id=1, source_target_pairs={{0,24},{2,10},{4,28},{6,14},{8,16},{10,2},{12,20},{14,6},{16,8},{1... | collective-permute-start | bytes 1179656 | tf_op jit(solution)/shard_map/ppermute | solution.py:372
  42.6 1.2 %collective-permute-start.12 = (f32[8,128]{1,0:T(8,128)S(1)}, f32[8,128]{1,0:T(8,128)S(1)}, u32[]{:S(2)}, u32[]{:S(2)}) collective-permute-start(f32[8,128]{1,0:T(8,128)S(1)} %get-tuple-element.53), channel_id=1, source_target_pairs={{0,2},{2,0},{4,6},{6,4},{1,3},{3,1},{5,7},{7,5},{8,10},{10,8},{12,... | collective-permute-start | bytes 12296 | tf_op jit(solution)/shard_map/ppermute | solution.py:235
  43.7 10.1 %collective-permute-start.13 = (f32[8,128]{1,0:T(8,128)S(1)}, f32[8,128]{1,0:T(8,128)S(1)}, u32[]{:S(2)}, u32[]{:S(2)}) collective-permute-start(f32[8,128]{1,0:T(8,128)S(1)} %add.21), channel_id=1, source_target_pairs={{0,4},{2,6},{4,0},{6,2},{1,5},{3,7},{5,1},{7,3},{8,12},{10,14},{12... | collective-permute-start | bytes 12296 | tf_op jit(solution)/shard_map/ppermute | solution.py:235
  53.9 18.9 %collective-permute-start.10 = (bf16[128,768]{1,0:T(8,128)(2,1)S(1)}, bf16[128,768]{1,0:T(8,128)(2,1)S(1)}, u32[]{:S(2)}, u32[]{:S(2)}) collective-permute-start(bf16[128,768]{1,0:T(8,128)(2,1)S(1)} %get-tuple-element.51), channel_id=1, source_target_pairs={{0,8},{2,26},{4,12},{6,30},{8,0},{10,18},{12,4},{14,22},{16,24},{1... | collective-permute-start | bytes 589832 | tf_op jit(solution)/shard_map/ppermute | solution.py:373
  56.9 15.8 %collective-permute-start.11 = (bf16[128,768]{1,0:T(8,128)(2,1)S(1)}, bf16[128,768]{1,0:T(8,128)(2,1)S(1)}, u32[]{:S(2)}, u32[]{:S(2)}) collective-permute-start(bf16[128,768]{1,0:T(8,128)(2,1)S(1)} %get-tuple-element.52), channel_id=1, source_target_pairs={{0,24},{2,10},{4,28},{6,14},{8,16},{10,2},{12,20},{14,6},{16,8},{1... | collective-permute-start | bytes 589832 | tf_op jit(solution)/shard_map/ppermute | solution.py:373
  63.5 9.3 %collective-permute-start.14 = (f32[8,128]{1,0:T(8,128)S(1)}, f32[8,128]{1,0:T(8,128)S(1)}, u32[]{:S(2)}, u32[]{:S(2)}) collective-permute-start(f32[8,128]{1,0:T(8,128)S(1)} %add.22.refs_2_), channel_id=1, source_target_pairs={{0,8},{8,0},{16,24},{24,16},{1,9},{9,1},{17,25},{25,17},{2,10},{10... | collective-permute-start | bytes 12296 | tf_op jit(solution)/shard_map/ppermute | solution.py:251
  63.5 9.2 %collective-permute-start.15 = (f32[8,128]{1,0:T(8,128)S(1)}, f32[8,128]{1,0:T(8,128)S(1)}, u32[]{:S(2)}, u32[]{:S(2)}) collective-permute-start(f32[8,128]{1,0:T(8,128)S(1)} %add.22.refs_2_), channel_id=1, source_target_pairs={{0,16},{8,24},{16,0},{24,8},{1,17},{9,25},{17,1},{25,9},{2,18},{10... | collective-permute-start | bytes 12296 | tf_op jit(solution)/shard_map/ppermute | solution.py:251
  64.1 8.7 %collective-permute-start.16 = (f32[8,128]{1,0:T(8,128)S(1)}, f32[8,128]{1,0:T(8,128)S(1)}, u32[]{:S(2)}, u32[]{:S(2)}) collective-permute-start(f32[8,128]{1,0:T(8,128)S(1)} %add.22.refs_2_), channel_id=1, source_target_pairs={{0,24},{8,16},{16,8},{24,0},{1,25},{9,17},{17,9},{25,1},{2,26},{10... | collective-permute-start | bytes 12296 | tf_op jit(solution)/shard_map/ppermute | solution.py:251

commit v5 on v4

--- a/solution.py
+++ b/solution.py
@@ -49,11 +49,46 @@
     )
 
 
+def vis_body(blocks, col_strides, row_groups, mask_ref, roster_ref, pos_ref, out_ref):
+    odd_row = (lax.axis_index("row") + lax.axis_index("col")) % 2
+    odd_col = lax.axis_index("col") % 2
+    height = out_ref.shape[0]
+    strides = [jnp.where(odd_col == 1, odd, even) - 1 for odd, even in col_strides]
+    groups = [jnp.where(odd_row == 1, odd, even) for even, odd in row_groups]
+    first_row = 1 + len(strides)
+
+    def chosen(flags_ref, columns):
+        shape = (height, flags_ref.shape[0])
+        cell = lax.broadcasted_iota(jnp.int32, shape, 0) // 8
+        block = lax.broadcasted_iota(jnp.int32, shape, 0) % 8
+        wanted = jnp.full(shape, -1, jnp.int32)
+        for at, column, step in columns:
+            wanted = jnp.where(cell == at, column + step * block, wanted)
+        picks = lax.broadcasted_iota(jnp.int32, shape, 1) == wanted
+        picks = jnp.where(picks & (block < blocks), 1.0, 0.0)
+        return lax.dot_general(
+            picks,
+            flags_ref[...].astype(jnp.float32),
+            (((1,), (0,)), ((), ())),
+            preferred_element_type=jnp.float32,
+        )
+
+    masked = [(0, 0, 1)]
+    masked += [(first_row + at, group * blocks, 1) for at, group in enumerate(groups)]
+    seen = chosen(mask_ref, masked)
+    drawn = chosen(roster_ref, [(1 + at, stride, 0) for at, stride in enumerate(strides)])
+    cell = lax.broadcasted_iota(jnp.int32, seen.shape, 0) // 8
+    block = lax.broadcasted_iota(jnp.int32, seen.shape, 0) % 8
+    inside = block < blocks
+    column = (cell >= 1) & (cell < first_row)
+    held = (cell == 0) & (pos_ref[...] // BLK == block)
+    visited = column & (drawn.astype(jnp.int32) == block)
+    out_ref[...] = jnp.where(inside & (held | visited | (seen > 0.5)), 1.0, 0.0)
+
+
 def scores_body(scale, blocks, own, *refs):
-    if own:
-        q_ref, p_ref, pos_ref, e_ref, stats_ref = refs
-    else:
-        q_ref, p_ref, e_ref, stats_ref = refs
+    q_ref, p_ref, pos_ref = refs[0], refs[1], refs[2]
+    e_ref, stats_ref = refs[-2:]
     scores = scores_of(q_ref, p_ref)
     stats_ref[...] = jnp.zeros_like(stats_ref)
     picked = None
@@ -82,9 +117,9 @@
 
 
 def last_body(scale, blocks, cells, *refs):
+    f_ref, head_ref, w_ref, loss_ref, e_ref = refs[-5:]
     q_ref, p_ref, vis_ref = refs[:3]
-    stats_refs = refs[3 : 3 + cells - 1]
-    f_ref, head_ref, tail_ref, w_ref, loss_ref, e_ref = refs[3 + cells - 1 :]
+    stats_refs = refs[3:-5]
     scores = scores_of(q_ref, p_ref)
     tops, sums = [], []
     for block_at in range(blocks):
@@ -114,7 +149,7 @@
     loss_ref[...] = jnp.broadcast_to(lost, loss_ref.shape)
     weights = weights_of(e_ref, factor, blocks, None)
     w_ref[...] = weights
-    put_pieces((head_ref, tail_ref), weights, q_ref, scale)
+    put_pieces((head_ref,), weights, q_ref, scale)
 
 
 def put_pieces(pieces, weights, q_ref, scale):
@@ -124,6 +159,12 @@
         gradient = jnp.dot(part, q_ref[...], preferred_element_type=jnp.float32) * scale
         ref[...] = gradient.astype(ref.dtype)
         at += ref.shape[0]
+
+
+def tail_body(scale, q_ref, w_ref, tail_ref):
+    part = w_ref[w_ref.shape[0] - tail_ref.shape[0] :, :]
+    gradient = jnp.dot(part, q_ref[...], preferred_element_type=jnp.float32) * scale
+    tail_ref[...] = gradient.astype(tail_ref.dtype)
 
 
 def pieces_body(scale, blocks, cell, q_ref, e_ref, f_ref, head_ref, tail_ref, w_ref):
@@ -259,8 +300,6 @@
     held = passages.shape[0]
     blocks = held // BLK
     scale = width ** (-0.5)
-    odd_col = lax.axis_index("col") % 2 == 1
-    odd_cell = (lax.axis_index("row") + lax.axis_index("col")) % 2 == 1
     f32, bf16 = jnp.float32, jnp.bfloat16
 
     rows = row_plan(n_row, n_col, reach)
@@ -283,26 +322,18 @@
             far = lax.ppermute(passages, "col", there)
             col_cells.append((far, stride, stride))
 
-    mask_t = block_mask.T
-    roster_t = roster.T
     pos = positive.reshape(1, count)
-    ids = jnp.arange(blocks, dtype=jnp.int32)[:, None]
-    pad = jnp.zeros((8 - blocks, count), f32)
-
-    def padded(flags):
-        return jnp.concatenate([flags.astype(f32), pad], axis=0)
-
-    def group_rows(group):
-        return mask_t[group * blocks : (group + 1) * blocks] == 1
-
-    seen = [padded(group_rows(0) | (pos // BLK == ids))]
-    for _, odd, even in col_cells:
-        seen.append(
-            padded(jnp.where(odd_col, roster_t[odd - 1][None], roster_t[even - 1][None]) == ids)
-        )
-    for _, _, (even, odd) in rows:
-        seen.append(padded(jnp.where(odd_cell, group_rows(odd), group_rows(even))))
-    vis = jnp.concatenate(seen, axis=0)
+    (vis,) = call(
+        functools.partial(
+            vis_body,
+            blocks,
+            [(odd, even) for _, odd, even in col_cells],
+            [groups for _, _, groups in rows],
+        ),
+        (jax.ShapeDtypeStruct((8 * (1 + len(col_cells) + len(rows)), count), f32),),
+        (block_mask.T, roster.T, pos),
+        0,
+    )
 
     cell_rows = [passages] + [cell[0] for cell in col_cells] + near
     cells = len(cell_rows)
@@ -331,12 +362,12 @@
     last = cells - 1
     f_shape = jax.ShapeDtypeStruct((8 * cells, count), f32)
     loss_shape = jax.ShapeDtypeStruct((8, BLK), f32)
-    tail = BLK
+    tail = BLK // 2
     head_shape = jax.ShapeDtypeStruct((held - tail, width), bf16)
     tail_shape = jax.ShapeDtypeStruct((tail, width), bf16)
-    factors, g_head, g_tail, w_last, lost = call(
+    factors, g_head, w_last, lost = call(
         functools.partial(last_body, scale, blocks, cells),
-        (f_shape, head_shape, tail_shape, w_shape, loss_shape),
+        (f_shape, head_shape, w_shape, loss_shape),
         (queries, cell_rows[last], vis, *stats),
         2 * dot_flops,
         held * count,
@@ -357,6 +388,9 @@
         weights[cell] = w
         return g
 
+    (g_tail,) = call(
+        functools.partial(tail_body, scale), (tail_shape,), (queries, w_last), dot_flops // blocks
+    )
     graded = {len(rows) - 1: (g_head, g_tail)}
     for at in range(len(rows) - 1):
         cell = first + at
@@ -419,7 +453,12 @@
         (rest, *tails, *lost_parts, written),
         0,
         out_specs=(out_spec, out_spec),
-        scratch=(pltpu.VMEM((tail, width), f32), wire_sems, pltpu.SMEM((1,), f32), pltpu.SemaphoreType.DMA),
+        scratch=(
+            pltpu.VMEM((tail, width), f32),
+            wire_sems,
+            pltpu.SMEM((1,), f32),
+            pltpu.SemaphoreType.DMA,
+        ),
         alias=1 + len(tails) + len(lost_parts),
     )
     return (loss, toward, grad_passages)

time: 74 us -> 77.1 us (1.042)
  waiting for transfers between devices: 31.6 us -> 39.9 us
  starting transfers between devices: 23.4 us -> 18.2 us
  other arithmetic: 2.38 us -> 0.01 us
  local copies, waits for them, and re-layouts: 3.02 us -> 5.02 us
    ppermute x2, waiting for transfers between devices: 3.04 us -> 11.5 us  [local_loss(): heads.append(lax.ppermute(graded[at][0], ('row', 'col'), back))]
    ppermute x2, starting transfers between devices: 6 us -> 0.09 us  [local_loss(): tails.append(lax.ppermute(graded[at][1], ('row', 'col'), back))]
    ppermute x1, waiting for transfers between devices: 7.94 us -> 12 us  [local_loss(): far = lax.ppermute(passages, 'col', there)]
    ppermute x2, waiting for transfers between devices: 9.86 us -> 5.98 us  [local_loss(): lax.ppermute(passages, ('row', 'col'), there)]
    unnamed x10 -> x16, local copies, waits for them, and re-layouts: 2.89 us -> 5.02 us
    select_n x2 -> x0, other arithmetic: 1.51 us -> none  [the longest x1 0.82 us: local_loss(): jnp.where(odd_col, roster_t[odd - 1][None], roster_t[even - 1][None]) == ids]
    ppermute x2, starting transfers between devices: 4.05 us -> 5.4 us  [local_loss(): lax.ppermute(passages, ('row', 'col'), there)]
    ppermute x2, starting transfers between devices: 1.52 us -> 0.51 us  [sum_steps(): array = array + lax.ppermute(array, axis, pairs)]
  transfers between devices with their start and end apart: 17 -> 17, of which waited for: 7 -> 7; matrix products, arithmetic and copies ran while one was open for 3% -> 0% of each run, Pallas kernels for 13% -> 14%
where the time goes in v5:
time: 77.1 us; the launch traced here: 76.7 us
  waiting for transfers between devices  39.9 us (52%)
  starting transfers between devices  18.2 us (24%)
  Pallas kernels  12.8 us (17%)
  local copies, waits for them, and re-layouts  5.02 us (7%)
  between operations  0.8 us (1%)
    pallas_call x16, Pallas kernels, call(): pl.pallas_call(kernel, out_shape=tuple(outs), in_specs=[pl.BlockSpec(memo...  12.8 us
    ppermute x1, waiting for transfers between devices, local_loss(): far = lax.ppermute(passages, 'col', there)  12 us
    ppermute x2, waiting for transfers between devices, local_loss(): heads.append(lax.ppermute(graded[at][0], ('row', 'col'), back))  11.5 us
    ppermute x2, waiting for transfers between devices, sum_steps(): array = array + lax.ppermute(array, axis, pairs)  9.53 us
    ppermute x2, waiting for transfers between devices, local_loss(): lax.ppermute(passages, ('row', 'col'), there)  5.98 us
    ppermute x2, starting transfers between devices, local_loss(): lax.ppermute(passages, ('row', 'col'), there)  5.4 us
    unnamed x16, local copies, waits for them, and re-layouts  5.02 us
    ppermute x3, starting transfers between devices, from_all(): lax.ppermute(array, axis, partners(size, s))  4.39 us
  transfers between devices with their start and end apart: 17, of which 7 were waited for; matrix products, arithmetic and copies ran while one was open for 0% of the time, Pallas kernels for 14%

profile of v5, /device:TPU:0, one launch (start us, length us, event | category | flops | bytes accessed | tf_op | source)
XLA Modules:
  0.0 76.7 jit_solution(12961205968063377286)
XLA Ops:
  0.6 3.1 %collective-permute-start.2 = (bf16[384,768]{1,0:T(8,128)(2,1)}, bf16[384,768]{1,0:T(8,128)(2,1)S(1)}, u32[]{:S(2)}, u32[]{:S(2)}) collective-permute-start(bf16[384,768]{1,0:T(8,128)(2,1)} %refs_6_.1), channel_id=1, source_target_pairs={{0,4},{2,6},{4,0},{6,2},{1,5},{3,7},{5,1},{7,3},{8,12},{10,14},{12... | collective-permute-start | bytes 1769480 | tf_op jit(solution)/shard_map/ppermute | solution.py:315
  3.7 0.0 collective-permute-start.1
  3.7 1.6 %collective-permute-start.4 = (bf16[384,768]{1,0:T(8,128)(2,1)}, bf16[384,768]{1,0:T(8,128)(2,1)S(1)}, u32[]{:S(2)}, u32[]{:S(2)}) collective-permute-start(bf16[384,768]{1,0:T(8,128)(2,1)} %refs_6_.1), channel_id=1, source_target_pairs={{0,8},{2,26},{4,12},{6,30},{8,0},{10,18},{12,4},{14,22},{16,24},{1... | collective-permute-start | bytes 1769480 | tf_op jit(solution)/shard_map/ppermute | solution.py:306
  5.3 12.0 %collective-permute-done.2.refs_1_.refs_8_ = bf16[384,768]{1,0:T(8,128)(2,1)S(1)} collective-permute-done((bf16[384,768]{1,0:T(8,128)(2,1)}, bf16[384,768]{1,0:T(8,128)(2,1)S(1)}, u32[]{:S(2)}, u32[]{:S(2)}) %collective-permute-start.2) | collective-permute-done | bytes 589856 | tf_op jit(solution)/shard_map/ppermute | solution.py:315
  17.2 0.0 collective-permute-start.3
  17.2 3.8 %collective-permute-start = (bf16[384,768]{1,0:T(8,128)(2,1)}, bf16[384,768]{1,0:T(8,128)(2,1)S(1)}, u32[]{:S(2)}, u32[]{:S(2)}) collective-permute-start(bf16[384,768]{1,0:T(8,128)(2,1)} %refs_6_.1), channel_id=1, source_target_pairs={{0,24},{2,10},{4,28},{6,14},{8,16},{10,2},{12,20},{14,6},{16,8},{1... | collective-permute-start | bytes 1769480 | tf_op jit(solution)/shard_map/ppermute | solution.py:306
  21.1 0.0 copy-start.3
  21.1 0.8 copy-done.3
  21.8 0.0 copy-start.4
  21.8 0.7 copy-done.4
  22.5 0.0 copy-start.7
  22.5 0.7 copy-done.7
  23.2 0.2 shard_map.77.refs_2_
  23.4 0.0 copy-start
  23.4 1.1 %copy-done = bf16[512,768]{1,0:T(8,128)(2,1)S(1)} copy-done((bf16[512,768]{1,0:T(8,128)(2,1)S(1)}, bf16[512,768]{1,0:T(8,128)(2,1)}, u32[]{:S(2)}) %copy-start) | copy-done | bytes 786456
  24.5 0.0 copy-start.1
  24.5 1.1 %copy-done.1 = bf16[384,768]{1,0:T(8,128)(2,1)S(1)} copy-done((bf16[384,768]{1,0:T(8,128)(2,1)S(1)}, bf16[384,768]{1,0:T(8,128)(2,1)}, u32[]{:S(2)}) %copy-start.1) | copy-done | bytes 589848
  25.6 0.7 copy-done.5
  26.3 0.7 shard_map.76
  26.9 0.6 shard_map.79
  27.6 0.0 collective-permute-done.1.refs_1_.refs_7_
  27.6 0.6 shard_map.78
  28.2 0.0 collective-permute-done.4.refs_1_.refs_10_
  28.2 0.6 shard_map.81
  28.8 0.0 collective-permute-done.3.refs_1_.refs_9_
  28.8 0.6 shard_map.80
  29.4 6.0 %collective-permute-done.refs_1_.refs_11_ = bf16[384,768]{1,0:T(8,128)(2,1)S(1)} collective-permute-done((bf16[384,768]{1,0:T(8,128)(2,1)}, bf16[384,768]{1,0:T(8,128)(2,1)S(1)}, u32[]{:S(2)}, u32[]{:S(2)}) %collective-permute-start) | collective-permute-done | bytes 589856 | tf_op jit(solution)/shard_map/ppermute | solution.py:306
  35.4 1.1 %shard_map.82 = (f32[48,512]{1,0:T(8,128)S(1)}, bf16[320,768]{1,0:T(8,128)(2,1)S(1)}, bf16[384,512]{1,0:T(8,128)(2,1)S(1)}, f32[8,128]{1,0:T(8,128)S(1)}) custom-call(bf16[512,768]{1,0:T(8,128)(2,1)S(1)} %copy-done, bf16[384,768]{1,0:T(8,128)(2,1)S(1)} %collective-permute-done.refs_1_.refs_11_, f32[48,512]{1,0:T(8,128)S(1)} %shard_map.77.refs_2_, ...), custom_call_target="tpu_custom_call" | custom-call | flops 603979776 | bytes 2543616 | tf_op jit(solution)/shard_map/pallas_call | solution.py:25
  36.5 0.5 shard_map.84
  37.0 0.1 collective-permute-start.5
  37.1 0.5 shard_map.86
  37.6 0.6 collective-permute-start.7
  38.1 0.9 %collective-permute-done.5.refs_3_ = bf16[384,768]{1,0:T(8,128)(2,1)S(1)} collective-permute-done((bf16[384,768]{1,0:T(8,128)(2,1)S(1)}, bf16[384,768]{1,0:T(8,128)(2,1)S(1)}, u32[]{:S(2)}, u32[]{:S(2)}) %collective-permute-start.5) | collective-permute-done | bytes 589856 | tf_op jit(solution)/shard_map/ppermute | solution.py:417
  39.1 0.5 shard_map.85
  39.6 0.0 copy-start.6
  39.6 1.6 %collective-permute-start.6 = (bf16[384,768]{1,0:T(8,128)(2,1)S(1)}, bf16[384,768]{1,0:T(8,128)(2,1)S(1)}, u32[]{:S(2)}, u32[]{:S(2)}) collective-permute-start(bf16[384,768]{1,0:T(8,128)(2,1)S(1)} %get-tuple-element.43), channel_id=1, source_target_pairs={{0,4},{2,6},{4,0},{6,2},{1,5},{3,7},{5,1},{7,3},{8,12},{10,14},{12... | collective-permute-start | bytes 1769480 | tf_op jit(solution)/shard_map/ppermute | solution.py:421
  41.2 0.6 shard_map.87
  41.7 0.1 collective-permute-start.8
  41.8 2.5 %collective-permute-start.9 = (bf16[320,768]{1,0:T(8,128)(2,1)S(1)}, bf16[320,768]{1,0:T(8,128)(2,1)S(1)}, u32[]{:S(2)}, u32[]{:S(2)}) collective-permute-start(bf16[320,768]{1,0:T(8,128)(2,1)S(1)} %get-tuple-element.48), channel_id=1, source_target_pairs={{0,24},{2,10},{4,28},{6,14},{8,16},{10,2},{12,20},{14,6},{16,8},{1... | collective-permute-start | bytes 1474568 | tf_op jit(solution)/shard_map/ppermute | solution.py:406
  44.3 0.0 collective-permute-start.12
  44.3 0.0 copy-done.6
  44.3 0.5 shard_map.83
  44.8 0.6 collective-permute-done.12
  45.5 0.5 collective-permute-start.13
  46.0 0.3 shard_map.89
  46.2 8.9 %collective-permute-done.13 = f32[8,128]{1,0:T(8,128)S(1)} collective-permute-done((f32[8,128]{1,0:T(8,128)S(1)}, f32[8,128]{1,0:T(8,128)S(1)}, u32[]{:S(2)}, u32[]{:S(2)}) %collective-permute-start.13) | collective-permute-done | bytes 4128 | tf_op jit(solution)/shard_map/ppermute | solution.py:276
  55.1 0.0 collective-permute-start.10
  55.1 11.0 %collective-permute-done.8.refs_3_ = bf16[320,768]{1,0:T(8,128)(2,1)S(1)} collective-permute-done((bf16[320,768]{1,0:T(8,128)(2,1)S(1)}, bf16[320,768]{1,0:T(8,128)(2,1)S(1)}, u32[]{:S(2)}, u32[]{:S(2)}) %collective-permute-start.8) | collective-permute-done | bytes 491552 | tf_op jit(solution)/shard_map/ppermute | solution.py:406
  66.1 0.1 collective-permute-start.11
  66.2 0.5 collective-permute-done.9.refs_4_
  66.7 0.0 collective-permute-start.14
  66.7 0.0 collective-permute-done.7.refs_2_
  66.7 3.8 %collective-permute-start.15 = (f32[8,128]{1,0:T(8,128)S(1)}, f32[8,128]{1,0:T(8,128)S(1)}, u32[]{:S(2)}, u32[]{:S(2)}) collective-permute-start(f32[8,128]{1,0:T(8,128)S(1)} %add.7.refs_2_), channel_id=1, source_target_pairs={{0,16},{8,24},{16,0},{24,8},{1,17},{9,25},{17,1},{25,9},{2,18},{10... | collective-permute-start | bytes 12296 | tf_op jit(solution)/shard_map/ppermute | solution.py:292
  70.5 0.0 collective-permute-done.6.refs_1_
  70.5 0.6 collective-permute-start.16
  71.1 0.0 copy-done.2
  71.1 3.8 %shard_map.91 = f32[512,768]{1,0:T(8,128)} custom-call(bf16[384,512]{1,0:T(8,128)(2,1)S(1)} %get-tuple-element.55.refs_0_, bf16[384,512]{1,0:T(8,128)(2,1)S(1)} %get-tuple-element.56.refs_1_, bf16[384,512]{1,0:T(8,128)(2,1)S(1)} %get-tuple-element.57.refs_2_, bf16[384,512]{1,0:T(8,128)(2,1)S(1)} %get-tuple-element.58.refs_3_, ...), custom_call_target="tpu_custom_call" | custom-call | flops 1811939328 | bytes 7471104 | tf_op jit(solution)/shard_map/pallas_call | solution.py:25
  74.9 1.1 %shard_map.88 = (f32[384,768]{1,0:T(8,128)}, f32[64,768]{1,0:T(8,128)S(1)}) custom-call(f32[384,768]{1,0:T(8,128)S(1)} %get-tuple-element.39.refs_0_, bf16[384,768]{1,0:T(8,128)(2,1)S(1)} %collective-permute-done.6.refs_1_, bf16[384,768]{1,0:T(8,128)(2,1)S(1)} %collective-permute-done.7.refs_2_, bf16[320,768]{1,0:T(8,128)(2,1)S(1)} %collective-permute-done.8.refs_3_, ...), custom_call_target="tpu_custom_call" | custom-call | bytes 4718592 | tf_op jit(solution)/shard_map/pallas_call | solution.py:25
  75.9 0.0 collective-permute-done.14.refs_3_
  76.0 0.0 collective-permute-done.15.refs_4_
  76.0 0.0 collective-permute-done.16.refs_5_
  76.0 0.0 collective-permute-done.10.refs_0_
  76.0 0.0 collective-permute-done.11.refs_1_
  76.0 0.7 shard_map.90
  (4 shorter events, 0.0 us)
Async XLA Ops:
  0.6 16.6 %collective-permute-start.2 = (bf16[384,768]{1,0:T(8,128)(2,1)}, bf16[384,768]{1,0:T(8,128)(2,1)S(1)}, u32[]{:S(2)}, u32[]{:S(2)}) collective-permute-start(bf16[384,768]{1,0:T(8,128)(2,1)} %refs_6_.1), channel_id=1, source_target_pairs={{0,4},{2,6},{4,0},{6,2},{1,5},{3,7},{5,1},{7,3},{8,12},{10,14},{12... | collective-permute-start | bytes 1769480 | tf_op jit(solution)/shard_map/ppermute | solution.py:315
  3.7 23.9 %collective-permute-start.1 = (bf16[384,768]{1,0:T(8,128)(2,1)}, bf16[384,768]{1,0:T(8,128)(2,1)S(1)}, u32[]{:S(2)}, u32[]{:S(2)}) collective-permute-start(bf16[384,768]{1,0:T(8,128)(2,1)} %refs_6_.1), channel_id=1, source_target_pairs={{0,2},{2,0},{4,6},{6,4},{1,3},{3,1},{5,7},{7,5},{8,10},{10,8},{12,... | collective-permute-start | bytes 1769480 | tf_op jit(solution)/shard_map/ppermute | solution.py:312
  3.7 24.5 %collective-permute-start.4 = (bf16[384,768]{1,0:T(8,128)(2,1)}, bf16[384,768]{1,0:T(8,128)(2,1)S(1)}, u32[]{:S(2)}, u32[]{:S(2)}) collective-permute-start(bf16[384,768]{1,0:T(8,128)(2,1)} %refs_6_.1), channel_id=1, source_target_pairs={{0,8},{2,26},{4,12},{6,30},{8,0},{10,18},{12,4},{14,22},{16,24},{1... | collective-permute-start | bytes 1769480 | tf_op jit(solution)/shard_map/ppermute | solution.py:306
  17.2 11.6 %collective-permute-start.3 = (bf16[384,768]{1,0:T(8,128)(2,1)S(1)}, bf16[384,768]{1,0:T(8,128)(2,1)S(1)}, u32[]{:S(2)}, u32[]{:S(2)}) collective-permute-start(bf16[384,768]{1,0:T(8,128)(2,1)S(1)} %collective-permute-done.2.refs_1_.refs_8_), channel_id=1, source_target_pairs={{0,2},{2,0},{4,6},{6,4},{1,3},{3,1},{5,7},{7,5},{8,10},{10,8},{12,... | collective-permute-start | bytes 1769480 | tf_op jit(solution)/shard_map/ppermute | solution.py:316
  17.2 18.2 %collective-permute-start = (bf16[384,768]{1,0:T(8,128)(2,1)}, bf16[384,768]{1,0:T(8,128)(2,1)S(1)}, u32[]{:S(2)}, u32[]{:S(2)}) collective-permute-start(bf16[384,768]{1,0:T(8,128)(2,1)} %refs_6_.1), channel_id=1, source_target_pairs={{0,24},{2,10},{4,28},{6,14},{8,16},{10,2},{12,20},{14,6},{16,8},{1... | collective-permute-start | bytes 1769480 | tf_op jit(solution)/shard_map/ppermute | solution.py:306
  21.1 0.8 copy-start.3
  21.8 0.7 copy-start.4
  22.5 0.7 copy-start.7
  23.4 1.1 %copy-start = (bf16[512,768]{1,0:T(8,128)(2,1)S(1)}, bf16[512,768]{1,0:T(8,128)(2,1)}, u32[]{:S(2)}) copy-start(bf16[512,768]{1,0:T(8,128)(2,1)} %q_ref.3) | copy-start | bytes 2359300
  24.5 1.1 %copy-start.1 = (bf16[384,768]{1,0:T(8,128)(2,1)S(1)}, bf16[384,768]{1,0:T(8,128)(2,1)}, u32[]{:S(2)}) copy-start(bf16[384,768]{1,0:T(8,128)(2,1)} %refs_6_.1) | copy-start | bytes 1769476
  25.6 0.7 copy-start.5
  37.0 2.1 %collective-permute-start.5 = (bf16[384,768]{1,0:T(8,128)(2,1)S(1)}, bf16[384,768]{1,0:T(8,128)(2,1)S(1)}, u32[]{:S(2)}, u32[]{:S(2)}) collective-permute-start(bf16[384,768]{1,0:T(8,128)(2,1)S(1)} %get-tuple-element.42), channel_id=1, source_target_pairs={{0,2},{2,0},{4,6},{6,4},{1,3},{3,1},{5,7},{7,5},{8,10},{10,8},{12,... | collective-permute-start | bytes 1769480 | tf_op jit(solution)/shard_map/ppermute | solution.py:417
  37.6 29.1 %collective-permute-start.7 = (bf16[384,768]{1,0:T(8,128)(2,1)S(1)}, bf16[384,768]{1,0:T(8,128)(2,1)S(1)}, u32[]{:S(2)}, u32[]{:S(2)}) collective-permute-start(bf16[384,768]{1,0:T(8,128)(2,1)S(1)} %get-tuple-element.45), channel_id=1, source_target_pairs={{0,2},{2,0},{4,6},{6,4},{1,3},{3,1},{5,7},{7,5},{8,10},{10,8},{12,... | collective-permute-start | bytes 1769480 | tf_op jit(solution)/shard_map/ppermute | solution.py:422
  39.6 4.7 %copy-start.6 = (s32[512]{0:T(512)S(1)}, s32[512]{0:T(512)}, u32[]{:S(2)}) copy-start(s32[512]{0:T(512)} %param.7) | copy-start | bytes 6148
  39.6 30.9 %collective-permute-start.6 = (bf16[384,768]{1,0:T(8,128)(2,1)S(1)}, bf16[384,768]{1,0:T(8,128)(2,1)S(1)}, u32[]{:S(2)}, u32[]{:S(2)}) collective-permute-start(bf16[384,768]{1,0:T(8,128)(2,1)S(1)} %get-tuple-element.43), channel_id=1, source_target_pairs={{0,4},{2,6},{4,0},{6,2},{1,5},{3,7},{5,1},{7,3},{8,12},{10,14},{12... | collective-permute-start | bytes 1769480 | tf_op jit(solution)/shard_map/ppermute | solution.py:421
  41.7 24.3 %collective-permute-start.8 = (bf16[320,768]{1,0:T(8,128)(2,1)S(1)}, bf16[320,768]{1,0:T(8,128)(2,1)S(1)}, u32[]{:S(2)}, u32[]{:S(2)}) collective-permute-start(bf16[320,768]{1,0:T(8,128)(2,1)S(1)} %get-tuple-element.47), channel_id=1, source_target_pairs={{0,8},{2,26},{4,12},{6,30},{8,0},{10,18},{12,4},{14,22},{16,24},{1... | collective-permute-start | bytes 1474568 | tf_op jit(solution)/shard_map/ppermute | solution.py:406
  41.8 24.9 %collective-permute-start.9 = (bf16[320,768]{1,0:T(8,128)(2,1)S(1)}, bf16[320,768]{1,0:T(8,128)(2,1)S(1)}, u32[]{:S(2)}, u32[]{:S(2)}) collective-permute-start(bf16[320,768]{1,0:T(8,128)(2,1)S(1)} %get-tuple-element.48), channel_id=1, source_target_pairs={{0,24},{2,10},{4,28},{6,14},{8,16},{10,2},{12,20},{14,6},{16,8},{1... | collective-permute-start | bytes 1474568 | tf_op jit(solution)/shard_map/ppermute | solution.py:406
  44.3 1.2 %collective-permute-start.12 = (f32[8,128]{1,0:T(8,128)S(1)}, f32[8,128]{1,0:T(8,128)S(1)}, u32[]{:S(2)}, u32[]{:S(2)}) collective-permute-start(f32[8,128]{1,0:T(8,128)S(1)} %get-tuple-element.52), channel_id=1, source_target_pairs={{0,2},{2,0},{4,6},{6,4},{1,3},{3,1},{5,7},{7,5},{8,10},{10,8},{12,... | collective-permute-start | bytes 12296 | tf_op jit(solution)/shard_map/ppermute | solution.py:276
  44.3 26.8 %copy-start.2 = (bf16[384,768]{1,0:T(8,128)(2,1)S(1)}, bf16[384,768]{1,0:T(8,128)(2,1)}, u32[]{:S(2)}) copy-start(bf16[384,768]{1,0:T(8,128)(2,1)} %refs_6_.1) | copy-start | bytes 1769476
  45.5 9.7 %collective-permute-start.13 = (f32[8,128]{1,0:T(8,128)S(1)}, f32[8,128]{1,0:T(8,128)S(1)}, u32[]{:S(2)}, u32[]{:S(2)}) collective-permute-start(f32[8,128]{1,0:T(8,128)S(1)} %add.6), channel_id=1, source_target_pairs={{0,4},{2,6},{4,0},{6,2},{1,5},{3,7},{5,1},{7,3},{8,12},{10,14},{12... | collective-permute-start | bytes 12296 | tf_op jit(solution)/shard_map/ppermute | solution.py:276
  55.1 20.9 %collective-permute-start.10 = (bf16[64,768]{1,0:T(8,128)(2,1)S(1)}, bf16[64,768]{1,0:T(8,128)(2,1)S(1)}, u32[]{:S(2)}, u32[]{:S(2)}) collective-permute-start(bf16[64,768]{1,0:T(8,128)(2,1)S(1)} %get-tuple-element.50), channel_id=1, source_target_pairs={{0,8},{2,26},{4,12},{6,30},{8,0},{10,18},{12,4},{14,22},{16,24},{1... | collective-permute-start | bytes 294920 | tf_op jit(solution)/shard_map/ppermute | solution.py:407
  66.1 9.9 %collective-permute-start.11 = (bf16[64,768]{1,0:T(8,128)(2,1)S(1)}, bf16[64,768]{1,0:T(8,128)(2,1)S(1)}, u32[]{:S(2)}, u32[]{:S(2)}) collective-permute-start(bf16[64,768]{1,0:T(8,128)(2,1)S(1)} %shard_map.89), channel_id=1, source_target_pairs={{0,24},{2,10},{4,28},{6,14},{8,16},{10,2},{12,20},{14,6},{16,8},{1... | collective-permute-start | bytes 294920 | tf_op jit(solution)/shard_map/ppermute | solution.py:407
  66.7 9.3 %collective-permute-start.14 = (f32[8,128]{1,0:T(8,128)S(1)}, f32[8,128]{1,0:T(8,128)S(1)}, u32[]{:S(2)}, u32[]{:S(2)}) collective-permute-start(f32[8,128]{1,0:T(8,128)S(1)} %add.7.refs_2_), channel_id=1, source_target_pairs={{0,8},{8,0},{16,24},{24,16},{1,9},{9,1},{17,25},{25,17},{2,10},{10... | collective-permute-start | bytes 12296 | tf_op jit(solution)/shard_map/ppermute | solution.py:292
  66.7 9.3 %collective-permute-start.15 = (f32[8,128]{1,0:T(8,128)S(1)}, f32[8,128]{1,0:T(8,128)S(1)}, u32[]{:S(2)}, u32[]{:S(2)}) collective-permute-start(f32[8,128]{1,0:T(8,128)S(1)} %add.7.refs_2_), channel_id=1, source_target_pairs={{0,16},{8,24},{16,0},{24,8},{1,17},{9,25},{17,1},{25,9},{2,18},{10... | collective-permute-start | bytes 12296 | tf_op jit(solution)/shard_map/ppermute | solution.py:292
  70.5 5.5 %collective-permute-start.16 = (f32[8,128]{1,0:T(8,128)S(1)}, f32[8,128]{1,0:T(8,128)S(1)}, u32[]{:S(2)}, u32[]{:S(2)}) collective-permute-start(f32[8,128]{1,0:T(8,128)S(1)} %add.7.refs_2_), channel_id=1, source_target_pairs={{0,24},{8,16},{16,8},{24,0},{1,25},{9,17},{17,9},{25,1},{2,26},{10... | collective-permute-start | bytes 12296 | tf_op jit(solution)/shard_map/ppermute | solution.py:292

commit v6 on v5

--- a/solution.py
+++ b/solution.py
@@ -116,10 +116,29 @@
     return jnp.concatenate(parts, axis=0)
 
 
-def last_body(scale, blocks, cells, *refs):
-    f_ref, head_ref, w_ref, loss_ref, e_ref = refs[-5:]
-    q_ref, p_ref, vis_ref = refs[:3]
-    stats_refs = refs[3:-5]
+def known_body(blocks, vis_ref, *refs):
+    stats_refs, out_ref = refs[:-1], refs[-1]
+    seen = [vis_ref[at * 8 : at * 8 + blocks, :] > 0 for at in range(len(stats_refs))]
+    tops = [
+        jnp.where(flags, ref[0:blocks, :], LOWEST) for flags, ref in zip(seen, stats_refs)
+    ]
+    highest = None
+    for top in tops:
+        top = jnp.max(top, axis=0, keepdims=True)
+        highest = top if highest is None else jnp.maximum(highest, top)
+    total = None
+    for flags, top, ref in zip(seen, tops, stats_refs):
+        gap = jnp.where(flags, top - highest, LOWEST)
+        part = jnp.sum(ref[blocks : 2 * blocks, :] * jnp.exp(gap), axis=0, keepdims=True)
+        total = part if total is None else total + part
+    out_ref[...] = jnp.zeros_like(out_ref)
+    out_ref[0:1, :] = highest
+    out_ref[1:2, :] = total
+    out_ref[2:3, :] = stats_refs[0][2 * blocks : 2 * blocks + 1, :]
+
+
+def last_body(scale, blocks, cell, q_ref, p_ref, vis_ref, known_ref, *refs):
+    head_ref, w_ref, total_ref, loss_ref, e_ref = refs
     scores = scores_of(q_ref, p_ref)
     tops, sums = [], []
     for block_at in range(blocks):
@@ -127,29 +146,31 @@
         e_ref[block_at * BLK : (block_at + 1) * BLK, :] = raised
         tops.append(highest * scale)
         sums.append(summed)
-    all_tops = [s[0:blocks, :] for s in stats_refs] + [jnp.concatenate(tops, axis=0)]
-    all_sums = [s[blocks : 2 * blocks, :] for s in stats_refs] + [jnp.concatenate(sums, axis=0)]
-    seen = [vis_ref[cell * 8 : cell * 8 + blocks, :] > 0 for cell in range(cells)]
-    highest = None
-    for cell in range(cells):
-        top = jnp.max(jnp.where(seen[cell], all_tops[cell], LOWEST), axis=0, keepdims=True)
-        highest = top if highest is None else jnp.maximum(highest, top)
-    total = None
-    for cell in range(cells):
-        gap = jnp.where(seen[cell], all_tops[cell] - highest, LOWEST)
-        part = jnp.sum(all_sums[cell] * jnp.exp(gap), axis=0, keepdims=True)
-        total = part if total is None else total + part
+    tops, sums = jnp.concatenate(tops, axis=0), jnp.concatenate(sums, axis=0)
+    seen = vis_ref[cell * 8 : cell * 8 + blocks, :] > 0
+    tops = jnp.where(seen, tops, LOWEST)
+    known = known_ref[0:1, :]
+    highest = jnp.maximum(known, jnp.max(tops, axis=0, keepdims=True))
+    here = sums * jnp.exp(jnp.where(seen, tops - highest, LOWEST))
+    total = known_ref[1:2, :] * jnp.exp(known - highest) + jnp.sum(here, axis=0, keepdims=True)
     log_total = highest + jnp.log(total)
-    f_ref[...] = jnp.zeros_like(f_ref)
-    for cell in range(cells):
-        factor = jnp.exp(jnp.where(seen[cell], all_tops[cell] - log_total, LOWEST))
-        f_ref[cell * 8 : cell * 8 + blocks, :] = factor
-    positive_score = stats_refs[0][2 * blocks : 2 * blocks + 1, :]
-    lost = jnp.sum(log_total - positive_score, axis=1, keepdims=True)
+    factor = jnp.exp(jnp.where(seen, tops - log_total, LOWEST))
+    total_ref[...] = jnp.broadcast_to(log_total, total_ref.shape)
+    lost = jnp.sum(log_total - known_ref[2:3, :], axis=1, keepdims=True)
     loss_ref[...] = jnp.broadcast_to(lost, loss_ref.shape)
     weights = weights_of(e_ref, factor, blocks, None)
     w_ref[...] = weights
     put_pieces((head_ref,), weights, q_ref, scale)
+
+
+def factors_body(blocks, vis_ref, total_ref, *refs):
+    stats_refs, f_ref = refs[:-1], refs[-1]
+    f_ref[...] = jnp.zeros_like(f_ref)
+    log_total = total_ref[0:1, :]
+    for cell, ref in enumerate(stats_refs):
+        seen = vis_ref[cell * 8 : cell * 8 + blocks, :] > 0
+        gap = jnp.where(seen, ref[0:blocks, :] - log_total, LOWEST)
+        f_ref[cell * 8 : cell * 8 + blocks, :] = jnp.exp(gap)
 
 
 def put_pieces(pieces, weights, q_ref, scale):
@@ -365,13 +386,17 @@
     tail = BLK // 2
     head_shape = jax.ShapeDtypeStruct((held - tail, width), bf16)
     tail_shape = jax.ShapeDtypeStruct((tail, width), bf16)
-    factors, g_head, w_last, lost = call(
-        functools.partial(last_body, scale, blocks, cells),
-        (f_shape, head_shape, w_shape, loss_shape),
-        (queries, cell_rows[last], vis, *stats),
+    (known,) = call(functools.partial(known_body, blocks), (s_shape,), (vis, *stats), 0)
+    g_head, w_last, log_total, lost = call(
+        functools.partial(last_body, scale, blocks, last),
+        (head_shape, w_shape, s_shape, loss_shape),
+        (queries, cell_rows[last], vis, known),
         2 * dot_flops,
         held * count,
         scratch=(pltpu.VMEM((held, count), f32),),
+    )
+    (factors,) = call(
+        functools.partial(factors_body, blocks), (f_shape,), (vis, log_total, *stats), 0
     )
     weights = {last: w_last}
 

time: 77.1 us -> 77.1 us (level)
    pallas_call x16 -> x18, Pallas kernels: 12.8 us -> 12.9 us  [call(): pl.pallas_call(kernel, out_shape=tuple(outs), in_specs=[pl.BlockSpec(memo...]
    unnamed x16 -> x18, local copies, waits for them, and re-layouts: 5.02 us -> 5.02 us
where the time goes in v6:
time: 77.1 us; the launch traced here: 76.7 us
  waiting for transfers between devices  39.7 us (51%)
  starting transfers between devices  18.3 us (24%)
  Pallas kernels  12.9 us (17%)
  local copies, waits for them, and re-layouts  5.02 us (7%)
  between operations  0.83 us (1%)
    pallas_call x18, Pallas kernels, call(): pl.pallas_call(kernel, out_shape=tuple(outs), in_specs=[pl.BlockSpec(memo...  12.9 us
    ppermute x1, waiting for transfers between devices, local_loss(): far = lax.ppermute(passages, 'col', there)  12 us
    ppermute x2, waiting for transfers between devices, local_loss(): heads.append(lax.ppermute(graded[at][0], ('row', 'col'), back))  11.4 us
    ppermute x2, waiting for transfers between devices, sum_steps(): array = array + lax.ppermute(array, axis, pairs)  9.54 us
    ppermute x2, waiting for transfers between devices, local_loss(): lax.ppermute(passages, ('row', 'col'), there)  5.88 us
    ppermute x2, starting transfers between devices, local_loss(): lax.ppermute(passages, ('row', 'col'), there)  5.4 us
    unnamed x18, local copies, waits for them, and re-layouts  5.02 us
    ppermute x3, starting transfers between devices, from_all(): lax.ppermute(array, axis, partners(size, s))  4.39 us
  transfers between devices with their start and end apart: 17, of which 7 were waited for; matrix products, arithmetic and copies ran while one was open for 0% of the time, Pallas kernels for 14%

profile of v6, /device:TPU:0, one launch (start us, length us, event | category | flops | bytes accessed | tf_op | source)
XLA Modules:
  0.0 76.7 jit_solution(9658244430354316349)
XLA Ops:
  0.6 3.1 %collective-permute-start.2 = (bf16[384,768]{1,0:T(8,128)(2,1)}, bf16[384,768]{1,0:T(8,128)(2,1)S(1)}, u32[]{:S(2)}, u32[]{:S(2)}) collective-permute-start(bf16[384,768]{1,0:T(8,128)(2,1)} %refs_6_.1), channel_id=1, source_target_pairs={{0,4},{2,6},{4,0},{6,2},{1,5},{3,7},{5,1},{7,3},{8,12},{10,14},{12... | collective-permute-start | bytes 1769480 | tf_op jit(solution)/shard_map/ppermute | solution.py:336
  3.7 0.0 collective-permute-start.1
  3.7 1.6 %collective-permute-start.4 = (bf16[384,768]{1,0:T(8,128)(2,1)}, bf16[384,768]{1,0:T(8,128)(2,1)S(1)}, u32[]{:S(2)}, u32[]{:S(2)}) collective-permute-start(bf16[384,768]{1,0:T(8,128)(2,1)} %refs_6_.1), channel_id=1, source_target_pairs={{0,8},{2,26},{4,12},{6,30},{8,0},{10,18},{12,4},{14,22},{16,24},{1... | collective-permute-start | bytes 1769480 | tf_op jit(solution)/shard_map/ppermute | solution.py:327
  5.3 12.0 %collective-permute-done.2.refs_1_.refs_8_ = bf16[384,768]{1,0:T(8,128)(2,1)S(1)} collective-permute-done((bf16[384,768]{1,0:T(8,128)(2,1)}, bf16[384,768]{1,0:T(8,128)(2,1)S(1)}, u32[]{:S(2)}, u32[]{:S(2)}) %collective-permute-start.2) | collective-permute-done | bytes 589856 | tf_op jit(solution)/shard_map/ppermute | solution.py:336
  17.2 0.0 collective-permute-start.3
  17.2 3.8 %collective-permute-start = (bf16[384,768]{1,0:T(8,128)(2,1)}, bf16[384,768]{1,0:T(8,128)(2,1)S(1)}, u32[]{:S(2)}, u32[]{:S(2)}) collective-permute-start(bf16[384,768]{1,0:T(8,128)(2,1)} %refs_6_.1), channel_id=1, source_target_pairs={{0,24},{2,10},{4,28},{6,14},{8,16},{10,2},{12,20},{14,6},{16,8},{1... | collective-permute-start | bytes 1769480 | tf_op jit(solution)/shard_map/ppermute | solution.py:327
  21.1 0.0 copy-start.4
  21.1 0.8 copy-done.4
  21.8 0.7 copy-done.5
  22.5 0.7 copy-done.8
  23.2 0.2 shard_map.77.vis_ref
  23.4 0.0 copy-start
  23.4 1.1 %copy-done = bf16[512,768]{1,0:T(8,128)(2,1)S(1)} copy-done((bf16[512,768]{1,0:T(8,128)(2,1)S(1)}, bf16[512,768]{1,0:T(8,128)(2,1)}, u32[]{:S(2)}) %copy-start) | copy-done | bytes 786456
  24.5 1.1 %copy-done.2 = bf16[384,768]{1,0:T(8,128)(2,1)S(1)} copy-done((bf16[384,768]{1,0:T(8,128)(2,1)S(1)}, bf16[384,768]{1,0:T(8,128)(2,1)}, u32[]{:S(2)}) %copy-start.2) | copy-done | bytes 589848
  25.6 0.7 copy-done.6
  26.3 0.7 shard_map.76
  26.9 0.6 shard_map.79
  27.6 0.0 collective-permute-done.1.refs_1_.refs_7_
  27.6 0.6 shard_map.78
  28.2 0.0 copy-start.1
  28.2 0.0 collective-permute-done.4.refs_1_.refs_10_
  28.2 0.6 shard_map.81
  28.8 0.0 collective-permute-done.3.refs_1_.refs_9_
  28.8 0.6 shard_map.80
  29.5 0.1 shard_map.82.known_ref
  29.6 5.9 %collective-permute-done.p_ref.refs_11_ = bf16[384,768]{1,0:T(8,128)(2,1)S(1)} collective-permute-done((bf16[384,768]{1,0:T(8,128)(2,1)}, bf16[384,768]{1,0:T(8,128)(2,1)S(1)}, u32[]{:S(2)}, u32[]{:S(2)}) %collective-permute-start) | collective-permute-done | bytes 589856 | tf_op jit(solution)/shard_map/ppermute | solution.py:327
  35.4 0.0 copy-done.1
  35.4 1.1 %shard_map.83 = (bf16[320,768]{1,0:T(8,128)(2,1)S(1)}, bf16[384,512]{1,0:T(8,128)(2,1)S(1)}, f32[8,512]{1,0:T(8,128)S(1)}, f32[8,128]{1,0:T(8,128)S(1)}) custom-call(bf16[512,768]{1,0:T(8,128)(2,1)S(1)} %copy-done.1, bf16[384,768]{1,0:T(8,128)(2,1)S(1)} %collective-permute-done.p_ref.refs_11_, f32[48,512]{1,0:T(8,128)S(1)} %shard_map.77.vis_ref, ...), custom_call_target="tpu_custom_call" | custom-call | flops 603979776 | bytes 2396160 | tf_op jit(solution)/shard_map/pallas_call | solution.py:25
  36.5 0.5 shard_map.86
  37.0 0.1 collective-permute-start.5
  37.1 0.5 shard_map.88
  37.6 0.6 collective-permute-start.7
  38.2 0.9 %collective-permute-done.5.refs_3_ = bf16[384,768]{1,0:T(8,128)(2,1)S(1)} collective-permute-done((bf16[384,768]{1,0:T(8,128)(2,1)S(1)}, bf16[384,768]{1,0:T(8,128)(2,1)S(1)}, u32[]{:S(2)}, u32[]{:S(2)}) %collective-permute-start.5) | collective-permute-done | bytes 589856 | tf_op jit(solution)/shard_map/ppermute | solution.py:442
  39.1 0.5 shard_map.87
  39.6 0.0 copy-start.7
  39.6 1.6 %collective-permute-start.6 = (bf16[384,768]{1,0:T(8,128)(2,1)S(1)}, bf16[384,768]{1,0:T(8,128)(2,1)S(1)}, u32[]{:S(2)}, u32[]{:S(2)}) collective-permute-start(bf16[384,768]{1,0:T(8,128)(2,1)S(1)} %get-tuple-element.43), channel_id=1, source_target_pairs={{0,4},{2,6},{4,0},{6,2},{1,5},{3,7},{5,1},{7,3},{8,12},{10,14},{12... | collective-permute-start | bytes 1769480 | tf_op jit(solution)/shard_map/ppermute | solution.py:446
  41.2 0.5 shard_map.89
  41.7 0.1 collective-permute-start.8
  41.8 2.5 %collective-permute-start.9 = (bf16[320,768]{1,0:T(8,128)(2,1)S(1)}, bf16[320,768]{1,0:T(8,128)(2,1)S(1)}, u32[]{:S(2)}, u32[]{:S(2)}) collective-permute-start(bf16[320,768]{1,0:T(8,128)(2,1)S(1)} %get-tuple-element.48), channel_id=1, source_target_pairs={{0,24},{2,10},{4,28},{6,14},{8,16},{10,2},{12,20},{14,6},{16,8},{1... | collective-permute-start | bytes 1474568 | tf_op jit(solution)/shard_map/ppermute | solution.py:431
  44.3 0.0 collective-permute-start.12
  44.3 0.0 copy-done.7
  44.3 0.5 shard_map.85
  44.8 0.7 collective-permute-done.12
  45.5 0.5 collective-permute-start.13
  46.0 0.3 shard_map.91
  46.2 8.9 %collective-permute-done.13 = f32[8,128]{1,0:T(8,128)S(1)} collective-permute-done((f32[8,128]{1,0:T(8,128)S(1)}, f32[8,128]{1,0:T(8,128)S(1)}, u32[]{:S(2)}, u32[]{:S(2)}) %collective-permute-start.13) | collective-permute-done | bytes 4128 | tf_op jit(solution)/shard_map/ppermute | solution.py:297
  55.1 0.0 collective-permute-start.10
  55.1 10.9 %collective-permute-done.8.refs_3_ = bf16[320,768]{1,0:T(8,128)(2,1)S(1)} collective-permute-done((bf16[320,768]{1,0:T(8,128)(2,1)S(1)}, bf16[320,768]{1,0:T(8,128)(2,1)S(1)}, u32[]{:S(2)}, u32[]{:S(2)}) %collective-permute-start.8) | collective-permute-done | bytes 491552 | tf_op jit(solution)/shard_map/ppermute | solution.py:431
  66.0 0.2 collective-permute-start.11
  66.2 0.5 collective-permute-done.9.refs_4_
  66.7 0.0 collective-permute-start.14
  66.7 0.0 collective-permute-done.7.refs_2_
  66.7 3.7 %collective-permute-start.15 = (f32[8,128]{1,0:T(8,128)S(1)}, f32[8,128]{1,0:T(8,128)S(1)}, u32[]{:S(2)}, u32[]{:S(2)}) collective-permute-start(f32[8,128]{1,0:T(8,128)S(1)} %add.7.refs_2_), channel_id=1, source_target_pairs={{0,16},{8,24},{16,0},{24,8},{1,17},{9,25},{17,1},{25,9},{2,18},{10... | collective-permute-start | bytes 12296 | tf_op jit(solution)/shard_map/ppermute | solution.py:313
  70.4 0.0 collective-permute-done.6.refs_1_
  70.4 0.6 collective-permute-start.16
  71.1 0.0 copy-done.3
  71.1 3.8 %shard_map.93 = f32[512,768]{1,0:T(8,128)} custom-call(bf16[384,512]{1,0:T(8,128)(2,1)S(1)} %get-tuple-element.55.refs_0_, bf16[384,512]{1,0:T(8,128)(2,1)S(1)} %get-tuple-element.56.refs_1_, bf16[384,512]{1,0:T(8,128)(2,1)S(1)} %get-tuple-element.57.refs_2_, bf16[384,512]{1,0:T(8,128)(2,1)S(1)} %get-tuple-element.58.refs_3_, ...), custom_call_target="tpu_custom_call" | custom-call | flops 1811939328 | bytes 7471104 | tf_op jit(solution)/shard_map/pallas_call | solution.py:25
  74.9 1.1 %shard_map.90 = (f32[384,768]{1,0:T(8,128)}, f32[64,768]{1,0:T(8,128)S(1)}) custom-call(f32[384,768]{1,0:T(8,128)S(1)} %get-tuple-element.39.refs_0_, bf16[384,768]{1,0:T(8,128)(2,1)S(1)} %collective-permute-done.6.refs_1_, bf16[384,768]{1,0:T(8,128)(2,1)S(1)} %collective-permute-done.7.refs_2_, bf16[320,768]{1,0:T(8,128)(2,1)S(1)} %collective-permute-done.8.refs_3_, ...), custom_call_target="tpu_custom_call" | custom-call | bytes 4718592 | tf_op jit(solution)/shard_map/pallas_call | solution.py:25
  76.0 0.0 collective-permute-done.14.refs_3_
  76.0 0.0 collective-permute-done.15.refs_4_
  76.0 0.0 collective-permute-done.16.refs_5_
  76.0 0.0 collective-permute-done.10.refs_0_
  76.0 0.0 collective-permute-done.11.refs_1_
  76.0 0.7 shard_map.92
  (8 shorter events, 0.0 us)
Async XLA Ops:
  0.6 16.6 %collective-permute-start.2 = (bf16[384,768]{1,0:T(8,128)(2,1)}, bf16[384,768]{1,0:T(8,128)(2,1)S(1)}, u32[]{:S(2)}, u32[]{:S(2)}) collective-permute-start(bf16[384,768]{1,0:T(8,128)(2,1)} %refs_6_.1), channel_id=1, source_target_pairs={{0,4},{2,6},{4,0},{6,2},{1,5},{3,7},{5,1},{7,3},{8,12},{10,14},{12... | collective-permute-start | bytes 1769480 | tf_op jit(solution)/shard_map/ppermute | solution.py:336
  3.7 23.9 %collective-permute-start.1 = (bf16[384,768]{1,0:T(8,128)(2,1)}, bf16[384,768]{1,0:T(8,128)(2,1)S(1)}, u32[]{:S(2)}, u32[]{:S(2)}) collective-permute-start(bf16[384,768]{1,0:T(8,128)(2,1)} %refs_6_.1), channel_id=1, source_target_pairs={{0,2},{2,0},{4,6},{6,4},{1,3},{3,1},{5,7},{7,5},{8,10},{10,8},{12,... | collective-permute-start | bytes 1769480 | tf_op jit(solution)/shard_map/ppermute | solution.py:333
  3.7 24.5 %collective-permute-start.4 = (bf16[384,768]{1,0:T(8,128)(2,1)}, bf16[384,768]{1,0:T(8,128)(2,1)S(1)}, u32[]{:S(2)}, u32[]{:S(2)}) collective-permute-start(bf16[384,768]{1,0:T(8,128)(2,1)} %refs_6_.1), channel_id=1, source_target_pairs={{0,8},{2,26},{4,12},{6,30},{8,0},{10,18},{12,4},{14,22},{16,24},{1... | collective-permute-start | bytes 1769480 | tf_op jit(solution)/shard_map/ppermute | solution.py:327
  17.2 11.6 %collective-permute-start.3 = (bf16[384,768]{1,0:T(8,128)(2,1)S(1)}, bf16[384,768]{1,0:T(8,128)(2,1)S(1)}, u32[]{:S(2)}, u32[]{:S(2)}) collective-permute-start(bf16[384,768]{1,0:T(8,128)(2,1)S(1)} %collective-permute-done.2.refs_1_.refs_8_), channel_id=1, source_target_pairs={{0,2},{2,0},{4,6},{6,4},{1,3},{3,1},{5,7},{7,5},{8,10},{10,8},{12,... | collective-permute-start | bytes 1769480 | tf_op jit(solution)/shard_map/ppermute | solution.py:337
  17.2 18.2 %collective-permute-start = (bf16[384,768]{1,0:T(8,128)(2,1)}, bf16[384,768]{1,0:T(8,128)(2,1)S(1)}, u32[]{:S(2)}, u32[]{:S(2)}) collective-permute-start(bf16[384,768]{1,0:T(8,128)(2,1)} %refs_6_.1), channel_id=1, source_target_pairs={{0,24},{2,10},{4,28},{6,14},{8,16},{10,2},{12,20},{14,6},{16,8},{1... | collective-permute-start | bytes 1769480 | tf_op jit(solution)/shard_map/ppermute | solution.py:327
  21.1 0.8 copy-start.4
  21.8 0.7 copy-start.5
  22.5 0.7 copy-start.8
  23.4 1.1 %copy-start = (bf16[512,768]{1,0:T(8,128)(2,1)S(1)}, bf16[512,768]{1,0:T(8,128)(2,1)}, u32[]{:S(2)}) copy-start(bf16[512,768]{1,0:T(8,128)(2,1)} %q_ref.5) | copy-start | bytes 2359300
  24.5 1.1 %copy-start.2 = (bf16[384,768]{1,0:T(8,128)(2,1)S(1)}, bf16[384,768]{1,0:T(8,128)(2,1)}, u32[]{:S(2)}) copy-start(bf16[384,768]{1,0:T(8,128)(2,1)} %refs_6_.1) | copy-start | bytes 1769476
  25.6 0.7 copy-start.6
  28.2 7.2 %copy-start.1 = (bf16[512,768]{1,0:T(8,128)(2,1)S(1)}, bf16[512,768]{1,0:T(8,128)(2,1)}, u32[]{:S(2)}) copy-start(bf16[512,768]{1,0:T(8,128)(2,1)} %q_ref.5) | copy-start | bytes 2359300
  37.0 2.1 %collective-permute-start.5 = (bf16[384,768]{1,0:T(8,128)(2,1)S(1)}, bf16[384,768]{1,0:T(8,128)(2,1)S(1)}, u32[]{:S(2)}, u32[]{:S(2)}) collective-permute-start(bf16[384,768]{1,0:T(8,128)(2,1)S(1)} %get-tuple-element.42), channel_id=1, source_target_pairs={{0,2},{2,0},{4,6},{6,4},{1,3},{3,1},{5,7},{7,5},{8,10},{10,8},{12,... | collective-permute-start | bytes 1769480 | tf_op jit(solution)/shard_map/ppermute | solution.py:442
  37.6 29.1 %collective-permute-start.7 = (bf16[384,768]{1,0:T(8,128)(2,1)S(1)}, bf16[384,768]{1,0:T(8,128)(2,1)S(1)}, u32[]{:S(2)}, u32[]{:S(2)}) collective-permute-start(bf16[384,768]{1,0:T(8,128)(2,1)S(1)} %get-tuple-element.45), channel_id=1, source_target_pairs={{0,2},{2,0},{4,6},{6,4},{1,3},{3,1},{5,7},{7,5},{8,10},{10,8},{12,... | collective-permute-start | bytes 1769480 | tf_op jit(solution)/shard_map/ppermute | solution.py:447
  39.6 4.7 %copy-start.7 = (s32[512]{0:T(512)S(1)}, s32[512]{0:T(512)}, u32[]{:S(2)}) copy-start(s32[512]{0:T(512)} %param.7) | copy-start | bytes 6148
  39.6 30.8 %collective-permute-start.6 = (bf16[384,768]{1,0:T(8,128)(2,1)S(1)}, bf16[384,768]{1,0:T(8,128)(2,1)S(1)}, u32[]{:S(2)}, u32[]{:S(2)}) collective-permute-start(bf16[384,768]{1,0:T(8,128)(2,1)S(1)} %get-tuple-element.43), channel_id=1, source_target_pairs={{0,4},{2,6},{4,0},{6,2},{1,5},{3,7},{5,1},{7,3},{8,12},{10,14},{12... | collective-permute-start | bytes 1769480 | tf_op jit(solution)/shard_map/ppermute | solution.py:446
  41.7 24.3 %collective-permute-start.8 = (bf16[320,768]{1,0:T(8,128)(2,1)S(1)}, bf16[320,768]{1,0:T(8,128)(2,1)S(1)}, u32[]{:S(2)}, u32[]{:S(2)}) collective-permute-start(bf16[320,768]{1,0:T(8,128)(2,1)S(1)} %get-tuple-element.47), channel_id=1, source_target_pairs={{0,8},{2,26},{4,12},{6,30},{8,0},{10,18},{12,4},{14,22},{16,24},{1... | collective-permute-start | bytes 1474568 | tf_op jit(solution)/shard_map/ppermute | solution.py:431
  41.8 24.9 %collective-permute-start.9 = (bf16[320,768]{1,0:T(8,128)(2,1)S(1)}, bf16[320,768]{1,0:T(8,128)(2,1)S(1)}, u32[]{:S(2)}, u32[]{:S(2)}) collective-permute-start(bf16[320,768]{1,0:T(8,128)(2,1)S(1)} %get-tuple-element.48), channel_id=1, source_target_pairs={{0,24},{2,10},{4,28},{6,14},{8,16},{10,2},{12,20},{14,6},{16,8},{1... | collective-permute-start | bytes 1474568 | tf_op jit(solution)/shard_map/ppermute | solution.py:431
  44.3 1.2 %collective-permute-start.12 = (f32[8,128]{1,0:T(8,128)S(1)}, f32[8,128]{1,0:T(8,128)S(1)}, u32[]{:S(2)}, u32[]{:S(2)}) collective-permute-start(f32[8,128]{1,0:T(8,128)S(1)} %get-tuple-element.52), channel_id=1, source_target_pairs={{0,2},{2,0},{4,6},{6,4},{1,3},{3,1},{5,7},{7,5},{8,10},{10,8},{12,... | collective-permute-start | bytes 12296 | tf_op jit(solution)/shard_map/ppermute | solution.py:297
  44.3 26.8 %copy-start.3 = (bf16[384,768]{1,0:T(8,128)(2,1)S(1)}, bf16[384,768]{1,0:T(8,128)(2,1)}, u32[]{:S(2)}) copy-start(bf16[384,768]{1,0:T(8,128)(2,1)} %refs_6_.1) | copy-start | bytes 1769476
  45.5 9.7 %collective-permute-start.13 = (f32[8,128]{1,0:T(8,128)S(1)}, f32[8,128]{1,0:T(8,128)S(1)}, u32[]{:S(2)}, u32[]{:S(2)}) collective-permute-start(f32[8,128]{1,0:T(8,128)S(1)} %add.6), channel_id=1, source_target_pairs={{0,4},{2,6},{4,0},{6,2},{1,5},{3,7},{5,1},{7,3},{8,12},{10,14},{12... | collective-permute-start | bytes 12296 | tf_op jit(solution)/shard_map/ppermute | solution.py:297
  55.1 20.9 %collective-permute-start.10 = (bf16[64,768]{1,0:T(8,128)(2,1)S(1)}, bf16[64,768]{1,0:T(8,128)(2,1)S(1)}, u32[]{:S(2)}, u32[]{:S(2)}) collective-permute-start(bf16[64,768]{1,0:T(8,128)(2,1)S(1)} %get-tuple-element.50), channel_id=1, source_target_pairs={{0,8},{2,26},{4,12},{6,30},{8,0},{10,18},{12,4},{14,22},{16,24},{1... | collective-permute-start | bytes 294920 | tf_op jit(solution)/shard_map/ppermute | solution.py:432
  66.0 10.0 %collective-permute-start.11 = (bf16[64,768]{1,0:T(8,128)(2,1)S(1)}, bf16[64,768]{1,0:T(8,128)(2,1)S(1)}, u32[]{:S(2)}, u32[]{:S(2)}) collective-permute-start(bf16[64,768]{1,0:T(8,128)(2,1)S(1)} %shard_map.91), channel_id=1, source_target_pairs={{0,24},{2,10},{4,28},{6,14},{8,16},{10,2},{12,20},{14,6},{16,8},{1... | collective-permute-start | bytes 294920 | tf_op jit(solution)/shard_map/ppermute | solution.py:432
  66.7 9.3 %collective-permute-start.14 = (f32[8,128]{1,0:T(8,128)S(1)}, f32[8,128]{1,0:T(8,128)S(1)}, u32[]{:S(2)}, u32[]{:S(2)}) collective-permute-start(f32[8,128]{1,0:T(8,128)S(1)} %add.7.refs_2_), channel_id=1, source_target_pairs={{0,8},{8,0},{16,24},{24,16},{1,9},{9,1},{17,25},{25,17},{2,10},{10... | collective-permute-start | bytes 12296 | tf_op jit(solution)/shard_map/ppermute | solution.py:313
  66.7 9.3 %collective-permute-start.15 = (f32[8,128]{1,0:T(8,128)S(1)}, f32[8,128]{1,0:T(8,128)S(1)}, u32[]{:S(2)}, u32[]{:S(2)}) collective-permute-start(f32[8,128]{1,0:T(8,128)S(1)} %add.7.refs_2_), channel_id=1, source_target_pairs={{0,16},{8,24},{16,0},{24,8},{1,17},{9,25},{17,1},{25,9},{2,18},{10... | collective-permute-start | bytes 12296 | tf_op jit(solution)/shard_map/ppermute | solution.py:313
  70.4 5.5 %collective-permute-start.16 = (f32[8,128]{1,0:T(8,128)S(1)}, f32[8,128]{1,0:T(8,128)S(1)}, u32[]{:S(2)}, u32[]{:S(2)}) collective-permute-start(f32[8,128]{1,0:T(8,128)S(1)} %add.7.refs_2_), channel_id=1, source_target_pairs={{0,24},{8,16},{16,8},{24,0},{1,25},{9,17},{17,9},{25,1},{2,26},{10... | collective-permute-start | bytes 12296 | tf_op jit(solution)/shard_map/ppermute | solution.py:313

commit v7 on v6

--- a/solution.py
+++ b/solution.py
@@ -138,7 +138,7 @@
 
 
 def last_body(scale, blocks, cell, q_ref, p_ref, vis_ref, known_ref, *refs):
-    head_ref, w_ref, total_ref, loss_ref, e_ref = refs
+    head_ref, w_ref, total_ref, e_ref = refs
     scores = scores_of(q_ref, p_ref)
     tops, sums = [], []
     for block_at in range(blocks):
@@ -156,17 +156,17 @@
     log_total = highest + jnp.log(total)
     factor = jnp.exp(jnp.where(seen, tops - log_total, LOWEST))
     total_ref[...] = jnp.broadcast_to(log_total, total_ref.shape)
-    lost = jnp.sum(log_total - known_ref[2:3, :], axis=1, keepdims=True)
-    loss_ref[...] = jnp.broadcast_to(lost, loss_ref.shape)
     weights = weights_of(e_ref, factor, blocks, None)
     w_ref[...] = weights
     put_pieces((head_ref,), weights, q_ref, scale)
 
 
-def factors_body(blocks, vis_ref, total_ref, *refs):
-    stats_refs, f_ref = refs[:-1], refs[-1]
+def factors_body(blocks, vis_ref, total_ref, known_ref, *refs):
+    stats_refs, f_ref, loss_ref = refs[:-2], refs[-2], refs[-1]
     f_ref[...] = jnp.zeros_like(f_ref)
     log_total = total_ref[0:1, :]
+    lost = jnp.sum(log_total - known_ref[2:3, :], axis=1, keepdims=True)
+    loss_ref[...] = jnp.broadcast_to(lost, loss_ref.shape)
     for cell, ref in enumerate(stats_refs):
         seen = vis_ref[cell * 8 : cell * 8 + blocks, :] > 0
         gap = jnp.where(seen, ref[0:blocks, :] - log_total, LOWEST)
@@ -387,16 +387,19 @@
     head_shape = jax.ShapeDtypeStruct((held - tail, width), bf16)
     tail_shape = jax.ShapeDtypeStruct((tail, width), bf16)
     (known,) = call(functools.partial(known_body, blocks), (s_shape,), (vis, *stats), 0)
-    g_head, w_last, log_total, lost = call(
+    g_head, w_last, log_total = call(
         functools.partial(last_body, scale, blocks, last),
-        (head_shape, w_shape, s_shape, loss_shape),
+        (head_shape, w_shape, s_shape),
         (queries, cell_rows[last], vis, known),
         2 * dot_flops,
         held * count,
         scratch=(pltpu.VMEM((held, count), f32),),
     )
-    (factors,) = call(
-        functools.partial(factors_body, blocks), (f_shape,), (vis, log_total, *stats), 0
+    factors, lost = call(
+        functools.partial(factors_body, blocks),
+        (f_shape, loss_shape),
+        (vis, log_total, known, *stats),
+        0,
     )
     weights = {last: w_last}
 

time: 77.1 us -> 77.2 us (level)
  no operation moved by 1% of the time
where the time goes in v7:
time: 77.2 us; the launch traced here: 76.8 us
  waiting for transfers between devices  39.8 us (52%)
  starting transfers between devices  18.2 us (24%)
  Pallas kernels  12.9 us (17%)
  local copies, waits for them, and re-layouts  5.02 us (7%)
  between operations  0.82 us (1%)
    pallas_call x18, Pallas kernels, call(): pl.pallas_call(kernel, out_shape=tuple(outs), in_specs=[pl.BlockSpec(memo...  12.9 us
    ppermute x1, waiting for transfers between devices, local_loss(): far = lax.ppermute(passages, 'col', there)  12 us
    ppermute x2, waiting for transfers between devices, local_loss(): heads.append(lax.ppermute(graded[at][0], ('row', 'col'), back))  11.4 us
    ppermute x2, waiting for transfers between devices, sum_steps(): array = array + lax.ppermute(array, axis, pairs)  9.54 us
    ppermute x2, waiting for transfers between devices, local_loss(): lax.ppermute(passages, ('row', 'col'), there)  5.88 us
    ppermute x2, starting transfers between devices, local_loss(): lax.ppermute(passages, ('row', 'col'), there)  5.4 us
    unnamed x18, local copies, waits for them, and re-layouts  5.02 us
    ppermute x3, starting transfers between devices, from_all(): lax.ppermute(array, axis, partners(size, s))  4.39 us
  transfers between devices with their start and end apart: 17, of which 7 were waited for; matrix products, arithmetic and copies ran while one was open for 0% of the time, Pallas kernels for 14%

profile of v7, /device:TPU:0, one launch (start us, length us, event | category | flops | bytes accessed | tf_op | source)
XLA Modules:
  0.0 76.8 jit_solution(180080459988568808)
XLA Ops:
  0.6 3.1 %collective-permute-start.2 = (bf16[384,768]{1,0:T(8,128)(2,1)}, bf16[384,768]{1,0:T(8,128)(2,1)S(1)}, u32[]{:S(2)}, u32[]{:S(2)}) collective-permute-start(bf16[384,768]{1,0:T(8,128)(2,1)} %refs_6_.1), channel_id=1, source_target_pairs={{0,4},{2,6},{4,0},{6,2},{1,5},{3,7},{5,1},{7,3},{8,12},{10,14},{12... | collective-permute-start | bytes 1769480 | tf_op jit(solution)/shard_map/ppermute | solution.py:336
  3.7 0.0 collective-permute-start.1
  3.7 1.6 %collective-permute-start.4 = (bf16[384,768]{1,0:T(8,128)(2,1)}, bf16[384,768]{1,0:T(8,128)(2,1)S(1)}, u32[]{:S(2)}, u32[]{:S(2)}) collective-permute-start(bf16[384,768]{1,0:T(8,128)(2,1)} %refs_6_.1), channel_id=1, source_target_pairs={{0,8},{2,26},{4,12},{6,30},{8,0},{10,18},{12,4},{14,22},{16,24},{1... | collective-permute-start | bytes 1769480 | tf_op jit(solution)/shard_map/ppermute | solution.py:327
  5.3 12.0 %collective-permute-done.2.refs_1_.refs_8_ = bf16[384,768]{1,0:T(8,128)(2,1)S(1)} collective-permute-done((bf16[384,768]{1,0:T(8,128)(2,1)}, bf16[384,768]{1,0:T(8,128)(2,1)S(1)}, u32[]{:S(2)}, u32[]{:S(2)}) %collective-permute-start.2) | collective-permute-done | bytes 589856 | tf_op jit(solution)/shard_map/ppermute | solution.py:336
  17.2 0.0 collective-permute-start.3
  17.2 3.8 %collective-permute-start = (bf16[384,768]{1,0:T(8,128)(2,1)}, bf16[384,768]{1,0:T(8,128)(2,1)S(1)}, u32[]{:S(2)}, u32[]{:S(2)}) collective-permute-start(bf16[384,768]{1,0:T(8,128)(2,1)} %refs_6_.1), channel_id=1, source_target_pairs={{0,24},{2,10},{4,28},{6,14},{8,16},{10,2},{12,20},{14,6},{16,8},{1... | collective-permute-start | bytes 1769480 | tf_op jit(solution)/shard_map/ppermute | solution.py:327
  21.1 0.8 copy-done.4
  21.8 0.7 copy-done.5
  22.5 0.7 copy-done.8
  23.2 0.2 shard_map.77.vis_ref
  23.4 0.0 copy-start
  23.4 1.1 %copy-done = bf16[512,768]{1,0:T(8,128)(2,1)S(1)} copy-done((bf16[512,768]{1,0:T(8,128)(2,1)S(1)}, bf16[512,768]{1,0:T(8,128)(2,1)}, u32[]{:S(2)}) %copy-start) | copy-done | bytes 786456
  24.5 1.1 %copy-done.2 = bf16[384,768]{1,0:T(8,128)(2,1)S(1)} copy-done((bf16[384,768]{1,0:T(8,128)(2,1)S(1)}, bf16[384,768]{1,0:T(8,128)(2,1)}, u32[]{:S(2)}) %copy-start.2) | copy-done | bytes 589848
  25.6 0.7 copy-done.6
  26.3 0.7 shard_map.76
  26.9 0.6 shard_map.79
  27.6 0.0 collective-permute-done.1.refs_1_.refs_7_
  27.6 0.6 shard_map.78
  28.2 0.0 copy-start.1
  28.2 0.0 collective-permute-done.4.refs_1_.refs_10_
  28.2 0.6 shard_map.81
  28.8 0.0 collective-permute-done.3.refs_1_.refs_9_
  28.8 0.6 shard_map.80
  29.5 0.1 shard_map.82.known_ref
  29.6 5.9 %collective-permute-done.p_ref.refs_11_ = bf16[384,768]{1,0:T(8,128)(2,1)S(1)} collective-permute-done((bf16[384,768]{1,0:T(8,128)(2,1)}, bf16[384,768]{1,0:T(8,128)(2,1)S(1)}, u32[]{:S(2)}, u32[]{:S(2)}) %collective-permute-start) | collective-permute-done | bytes 589856 | tf_op jit(solution)/shard_map/ppermute | solution.py:327
  35.4 0.0 copy-done.1
  35.4 1.1 %shard_map.83 = (bf16[320,768]{1,0:T(8,128)(2,1)S(1)}, bf16[384,512]{1,0:T(8,128)(2,1)S(1)}, f32[8,512]{1,0:T(8,128)S(1)}) custom-call(bf16[512,768]{1,0:T(8,128)(2,1)S(1)} %copy-done.1, bf16[384,768]{1,0:T(8,128)(2,1)S(1)} %collective-permute-done.p_ref.refs_11_, f32[48,512]{1,0:T(8,128)S(1)} %shard_map.77.vis_ref, f32[8,512]{1,0:T(8,128)S(1)} %shard_map.82.known_ref), custom_call_target="tpu_custom_call" | custom-call | flops 603979776 | bytes 2392064 | tf_op jit(solution)/shard_map/pallas_call | solution.py:25
  36.5 0.1 shard_map.84
  36.6 0.5 shard_map.86
  37.1 0.1 collective-permute-start.5
  37.2 0.5 shard_map.88
  37.6 0.6 collective-permute-start.7
  38.2 0.9 %collective-permute-done.5.refs_3_ = bf16[384,768]{1,0:T(8,128)(2,1)S(1)} collective-permute-done((bf16[384,768]{1,0:T(8,128)(2,1)S(1)}, bf16[384,768]{1,0:T(8,128)(2,1)S(1)}, u32[]{:S(2)}, u32[]{:S(2)}) %collective-permute-start.5) | collective-permute-done | bytes 589856 | tf_op jit(solution)/shard_map/ppermute | solution.py:445
  39.1 0.5 shard_map.87
  39.6 0.0 copy-start.7
  39.6 1.6 %collective-permute-start.6 = (bf16[384,768]{1,0:T(8,128)(2,1)S(1)}, bf16[384,768]{1,0:T(8,128)(2,1)S(1)}, u32[]{:S(2)}, u32[]{:S(2)}) collective-permute-start(bf16[384,768]{1,0:T(8,128)(2,1)S(1)} %get-tuple-element.45), channel_id=1, source_target_pairs={{0,4},{2,6},{4,0},{6,2},{1,5},{3,7},{5,1},{7,3},{8,12},{10,14},{12... | collective-permute-start | bytes 1769480 | tf_op jit(solution)/shard_map/ppermute | solution.py:449
  41.2 0.5 shard_map.89
  41.8 0.1 collective-permute-start.8
  41.9 2.5 %collective-permute-start.9 = (bf16[320,768]{1,0:T(8,128)(2,1)S(1)}, bf16[320,768]{1,0:T(8,128)(2,1)S(1)}, u32[]{:S(2)}, u32[]{:S(2)}) collective-permute-start(bf16[320,768]{1,0:T(8,128)(2,1)S(1)} %get-tuple-element.50), channel_id=1, source_target_pairs={{0,24},{2,10},{4,28},{6,14},{8,16},{10,2},{12,20},{14,6},{16,8},{1... | collective-permute-start | bytes 1474568 | tf_op jit(solution)/shard_map/ppermute | solution.py:434
  44.4 0.0 collective-permute-start.12
  44.4 0.0 copy-done.7
  44.4 0.5 shard_map.85
  44.9 0.7 collective-permute-done.12
  45.5 0.5 collective-permute-start.13
  46.0 0.3 shard_map.91
  46.3 8.9 %collective-permute-done.13 = f32[8,128]{1,0:T(8,128)S(1)} collective-permute-done((f32[8,128]{1,0:T(8,128)S(1)}, f32[8,128]{1,0:T(8,128)S(1)}, u32[]{:S(2)}, u32[]{:S(2)}) %collective-permute-start.13) | collective-permute-done | bytes 4128 | tf_op jit(solution)/shard_map/ppermute | solution.py:297
  55.2 0.0 collective-permute-start.10
  55.2 10.9 %collective-permute-done.8.refs_3_ = bf16[320,768]{1,0:T(8,128)(2,1)S(1)} collective-permute-done((bf16[320,768]{1,0:T(8,128)(2,1)S(1)}, bf16[320,768]{1,0:T(8,128)(2,1)S(1)}, u32[]{:S(2)}, u32[]{:S(2)}) %collective-permute-start.8) | collective-permute-done | bytes 491552 | tf_op jit(solution)/shard_map/ppermute | solution.py:434
  66.1 0.1 collective-permute-start.11
  66.2 0.5 collective-permute-done.9.refs_4_
  66.7 0.0 collective-permute-start.14
  66.7 0.0 collective-permute-done.7.refs_2_
  66.8 3.7 %collective-permute-start.15 = (f32[8,128]{1,0:T(8,128)S(1)}, f32[8,128]{1,0:T(8,128)S(1)}, u32[]{:S(2)}, u32[]{:S(2)}) collective-permute-start(f32[8,128]{1,0:T(8,128)S(1)} %add.7.refs_2_), channel_id=1, source_target_pairs={{0,16},{8,24},{16,0},{24,8},{1,17},{9,25},{17,1},{25,9},{2,18},{10... | collective-permute-start | bytes 12296 | tf_op jit(solution)/shard_map/ppermute | solution.py:313
  70.5 0.0 collective-permute-done.6.refs_1_
  70.5 0.6 collective-permute-start.16
  71.1 0.0 copy-done.3
  71.1 3.8 %shard_map.93 = f32[512,768]{1,0:T(8,128)} custom-call(bf16[384,512]{1,0:T(8,128)(2,1)S(1)} %get-tuple-element.57.refs_0_, bf16[384,512]{1,0:T(8,128)(2,1)S(1)} %get-tuple-element.58.refs_1_, bf16[384,512]{1,0:T(8,128)(2,1)S(1)} %get-tuple-element.59.refs_2_, bf16[384,512]{1,0:T(8,128)(2,1)S(1)} %get-tuple-element.60.refs_3_, ...), custom_call_target="tpu_custom_call" | custom-call | flops 1811939328 | bytes 7471104 | tf_op jit(solution)/shard_map/pallas_call | solution.py:25
  74.9 1.1 %shard_map.90 = (f32[384,768]{1,0:T(8,128)}, f32[64,768]{1,0:T(8,128)S(1)}) custom-call(f32[384,768]{1,0:T(8,128)S(1)} %get-tuple-element.41.refs_0_, bf16[384,768]{1,0:T(8,128)(2,1)S(1)} %collective-permute-done.6.refs_1_, bf16[384,768]{1,0:T(8,128)(2,1)S(1)} %collective-permute-done.7.refs_2_, bf16[320,768]{1,0:T(8,128)(2,1)S(1)} %collective-permute-done.8.refs_3_, ...), custom_call_target="tpu_custom_call" | custom-call | bytes 4718592 | tf_op jit(solution)/shard_map/pallas_call | solution.py:25
  76.0 0.0 collective-permute-done.14.refs_3_
  76.0 0.0 collective-permute-done.15.refs_4_
  76.0 0.0 collective-permute-done.16.refs_5_
  76.0 0.0 collective-permute-done.10.refs_0_
  76.1 0.0 collective-permute-done.11.refs_1_
  76.1 0.7 shard_map.92
  (8 shorter events, 0.0 us)
Async XLA Ops:
  0.6 16.6 %collective-permute-start.2 = (bf16[384,768]{1,0:T(8,128)(2,1)}, bf16[384,768]{1,0:T(8,128)(2,1)S(1)}, u32[]{:S(2)}, u32[]{:S(2)}) collective-permute-start(bf16[384,768]{1,0:T(8,128)(2,1)} %refs_6_.1), channel_id=1, source_target_pairs={{0,4},{2,6},{4,0},{6,2},{1,5},{3,7},{5,1},{7,3},{8,12},{10,14},{12... | collective-permute-start | bytes 1769480 | tf_op jit(solution)/shard_map/ppermute | solution.py:336
  3.7 23.9 %collective-permute-start.1 = (bf16[384,768]{1,0:T(8,128)(2,1)}, bf16[384,768]{1,0:T(8,128)(2,1)S(1)}, u32[]{:S(2)}, u32[]{:S(2)}) collective-permute-start(bf16[384,768]{1,0:T(8,128)(2,1)} %refs_6_.1), channel_id=1, source_target_pairs={{0,2},{2,0},{4,6},{6,4},{1,3},{3,1},{5,7},{7,5},{8,10},{10,8},{12,... | collective-permute-start | bytes 1769480 | tf_op jit(solution)/shard_map/ppermute | solution.py:333
  3.7 24.5 %collective-permute-start.4 = (bf16[384,768]{1,0:T(8,128)(2,1)}, bf16[384,768]{1,0:T(8,128)(2,1)S(1)}, u32[]{:S(2)}, u32[]{:S(2)}) collective-permute-start(bf16[384,768]{1,0:T(8,128)(2,1)} %refs_6_.1), channel_id=1, source_target_pairs={{0,8},{2,26},{4,12},{6,30},{8,0},{10,18},{12,4},{14,22},{16,24},{1... | collective-permute-start | bytes 1769480 | tf_op jit(solution)/shard_map/ppermute | solution.py:327
  17.2 11.6 %collective-permute-start.3 = (bf16[384,768]{1,0:T(8,128)(2,1)S(1)}, bf16[384,768]{1,0:T(8,128)(2,1)S(1)}, u32[]{:S(2)}, u32[]{:S(2)}) collective-permute-start(bf16[384,768]{1,0:T(8,128)(2,1)S(1)} %collective-permute-done.2.refs_1_.refs_8_), channel_id=1, source_target_pairs={{0,2},{2,0},{4,6},{6,4},{1,3},{3,1},{5,7},{7,5},{8,10},{10,8},{12,... | collective-permute-start | bytes 1769480 | tf_op jit(solution)/shard_map/ppermute | solution.py:337
  17.2 18.2 %collective-permute-start = (bf16[384,768]{1,0:T(8,128)(2,1)}, bf16[384,768]{1,0:T(8,128)(2,1)S(1)}, u32[]{:S(2)}, u32[]{:S(2)}) collective-permute-start(bf16[384,768]{1,0:T(8,128)(2,1)} %refs_6_.1), channel_id=1, source_target_pairs={{0,24},{2,10},{4,28},{6,14},{8,16},{10,2},{12,20},{14,6},{16,8},{1... | collective-permute-start | bytes 1769480 | tf_op jit(solution)/shard_map/ppermute | solution.py:327
  21.1 0.8 copy-start.4
  21.8 0.7 copy-start.5
  22.5 0.7 copy-start.8
  23.4 1.1 %copy-start = (bf16[512,768]{1,0:T(8,128)(2,1)S(1)}, bf16[512,768]{1,0:T(8,128)(2,1)}, u32[]{:S(2)}) copy-start(bf16[512,768]{1,0:T(8,128)(2,1)} %q_ref.5) | copy-start | bytes 2359300
  24.5 1.1 %copy-start.2 = (bf16[384,768]{1,0:T(8,128)(2,1)S(1)}, bf16[384,768]{1,0:T(8,128)(2,1)}, u32[]{:S(2)}) copy-start(bf16[384,768]{1,0:T(8,128)(2,1)} %refs_6_.1) | copy-start | bytes 1769476
  25.6 0.7 copy-start.6
  28.2 7.2 %copy-start.1 = (bf16[512,768]{1,0:T(8,128)(2,1)S(1)}, bf16[512,768]{1,0:T(8,128)(2,1)}, u32[]{:S(2)}) copy-start(bf16[512,768]{1,0:T(8,128)(2,1)} %q_ref.5) | copy-start | bytes 2359300
  37.1 2.1 %collective-permute-start.5 = (bf16[384,768]{1,0:T(8,128)(2,1)S(1)}, bf16[384,768]{1,0:T(8,128)(2,1)S(1)}, u32[]{:S(2)}, u32[]{:S(2)}) collective-permute-start(bf16[384,768]{1,0:T(8,128)(2,1)S(1)} %get-tuple-element.44), channel_id=1, source_target_pairs={{0,2},{2,0},{4,6},{6,4},{1,3},{3,1},{5,7},{7,5},{8,10},{10,8},{12,... | collective-permute-start | bytes 1769480 | tf_op jit(solution)/shard_map/ppermute | solution.py:445
  37.6 29.1 %collective-permute-start.7 = (bf16[384,768]{1,0:T(8,128)(2,1)S(1)}, bf16[384,768]{1,0:T(8,128)(2,1)S(1)}, u32[]{:S(2)}, u32[]{:S(2)}) collective-permute-start(bf16[384,768]{1,0:T(8,128)(2,1)S(1)} %get-tuple-element.47), channel_id=1, source_target_pairs={{0,2},{2,0},{4,6},{6,4},{1,3},{3,1},{5,7},{7,5},{8,10},{10,8},{12,... | collective-permute-start | bytes 1769480 | tf_op jit(solution)/shard_map/ppermute | solution.py:450
  39.6 4.7 %copy-start.7 = (s32[512]{0:T(512)S(1)}, s32[512]{0:T(512)}, u32[]{:S(2)}) copy-start(s32[512]{0:T(512)} %param.7) | copy-start | bytes 6148
  39.6 30.9 %collective-permute-start.6 = (bf16[384,768]{1,0:T(8,128)(2,1)S(1)}, bf16[384,768]{1,0:T(8,128)(2,1)S(1)}, u32[]{:S(2)}, u32[]{:S(2)}) collective-permute-start(bf16[384,768]{1,0:T(8,128)(2,1)S(1)} %get-tuple-element.45), channel_id=1, source_target_pairs={{0,4},{2,6},{4,0},{6,2},{1,5},{3,7},{5,1},{7,3},{8,12},{10,14},{12... | collective-permute-start | bytes 1769480 | tf_op jit(solution)/shard_map/ppermute | solution.py:449
  41.8 24.3 %collective-permute-start.8 = (bf16[320,768]{1,0:T(8,128)(2,1)S(1)}, bf16[320,768]{1,0:T(8,128)(2,1)S(1)}, u32[]{:S(2)}, u32[]{:S(2)}) collective-permute-start(bf16[320,768]{1,0:T(8,128)(2,1)S(1)} %get-tuple-element.49), channel_id=1, source_target_pairs={{0,8},{2,26},{4,12},{6,30},{8,0},{10,18},{12,4},{14,22},{16,24},{1... | collective-permute-start | bytes 1474568 | tf_op jit(solution)/shard_map/ppermute | solution.py:434
  41.9 24.9 %collective-permute-start.9 = (bf16[320,768]{1,0:T(8,128)(2,1)S(1)}, bf16[320,768]{1,0:T(8,128)(2,1)S(1)}, u32[]{:S(2)}, u32[]{:S(2)}) collective-permute-start(bf16[320,768]{1,0:T(8,128)(2,1)S(1)} %get-tuple-element.50), channel_id=1, source_target_pairs={{0,24},{2,10},{4,28},{6,14},{8,16},{10,2},{12,20},{14,6},{16,8},{1... | collective-permute-start | bytes 1474568 | tf_op jit(solution)/shard_map/ppermute | solution.py:434
  44.4 1.2 %collective-permute-start.12 = (f32[8,128]{1,0:T(8,128)S(1)}, f32[8,128]{1,0:T(8,128)S(1)}, u32[]{:S(2)}, u32[]{:S(2)}) collective-permute-start(f32[8,128]{1,0:T(8,128)S(1)} %get-tuple-element.54), channel_id=1, source_target_pairs={{0,2},{2,0},{4,6},{6,4},{1,3},{3,1},{5,7},{7,5},{8,10},{10,8},{12,... | collective-permute-start | bytes 12296 | tf_op jit(solution)/shard_map/ppermute | solution.py:297
  44.4 26.8 %copy-start.3 = (bf16[384,768]{1,0:T(8,128)(2,1)S(1)}, bf16[384,768]{1,0:T(8,128)(2,1)}, u32[]{:S(2)}) copy-start(bf16[384,768]{1,0:T(8,128)(2,1)} %refs_6_.1) | copy-start | bytes 1769476
  45.5 9.6 %collective-permute-start.13 = (f32[8,128]{1,0:T(8,128)S(1)}, f32[8,128]{1,0:T(8,128)S(1)}, u32[]{:S(2)}, u32[]{:S(2)}) collective-permute-start(f32[8,128]{1,0:T(8,128)S(1)} %add.6), channel_id=1, source_target_pairs={{0,4},{2,6},{4,0},{6,2},{1,5},{3,7},{5,1},{7,3},{8,12},{10,14},{12... | collective-permute-start | bytes 12296 | tf_op jit(solution)/shard_map/ppermute | solution.py:297
  55.2 20.9 %collective-permute-start.10 = (bf16[64,768]{1,0:T(8,128)(2,1)S(1)}, bf16[64,768]{1,0:T(8,128)(2,1)S(1)}, u32[]{:S(2)}, u32[]{:S(2)}) collective-permute-start(bf16[64,768]{1,0:T(8,128)(2,1)S(1)} %get-tuple-element.52), channel_id=1, source_target_pairs={{0,8},{2,26},{4,12},{6,30},{8,0},{10,18},{12,4},{14,22},{16,24},{1... | collective-permute-start | bytes 294920 | tf_op jit(solution)/shard_map/ppermute | solution.py:435
  66.1 10.0 %collective-permute-start.11 = (bf16[64,768]{1,0:T(8,128)(2,1)S(1)}, bf16[64,768]{1,0:T(8,128)(2,1)S(1)}, u32[]{:S(2)}, u32[]{:S(2)}) collective-permute-start(bf16[64,768]{1,0:T(8,128)(2,1)S(1)} %shard_map.91), channel_id=1, source_target_pairs={{0,24},{2,10},{4,28},{6,14},{8,16},{10,2},{12,20},{14,6},{16,8},{1... | collective-permute-start | bytes 294920 | tf_op jit(solution)/shard_map/ppermute | solution.py:435
  66.7 9.3 %collective-permute-start.14 = (f32[8,128]{1,0:T(8,128)S(1)}, f32[8,128]{1,0:T(8,128)S(1)}, u32[]{:S(2)}, u32[]{:S(2)}) collective-permute-start(f32[8,128]{1,0:T(8,128)S(1)} %add.7.refs_2_), channel_id=1, source_target_pairs={{0,8},{8,0},{16,24},{24,16},{1,9},{9,1},{17,25},{25,17},{2,10},{10... | collective-permute-start | bytes 12296 | tf_op jit(solution)/shard_map/ppermute | solution.py:313
  66.8 9.3 %collective-permute-start.15 = (f32[8,128]{1,0:T(8,128)S(1)}, f32[8,128]{1,0:T(8,128)S(1)}, u32[]{:S(2)}, u32[]{:S(2)}) collective-permute-start(f32[8,128]{1,0:T(8,128)S(1)} %add.7.refs_2_), channel_id=1, source_target_pairs={{0,16},{8,24},{16,0},{24,8},{1,17},{9,25},{17,1},{25,9},{2,18},{10... | collective-permute-start | bytes 12296 | tf_op jit(solution)/shard_map/ppermute | solution.py:313
  70.5 5.5 %collective-permute-start.16 = (f32[8,128]{1,0:T(8,128)S(1)}, f32[8,128]{1,0:T(8,128)S(1)}, u32[]{:S(2)}, u32[]{:S(2)}) collective-permute-start(f32[8,128]{1,0:T(8,128)S(1)} %add.7.refs_2_), channel_id=1, source_target_pairs={{0,24},{8,16},{16,8},{24,0},{1,25},{9,17},{17,9},{25,1},{2,26},{10... | collective-permute-start | bytes 12296 | tf_op jit(solution)/shard_map/ppermute | solution.py:313
